TPU v7x, 32 devices: a whole 2x2x4 slice. The times are simulated.
32 devices in a mesh: blk: 8 (over y, x, core), pitch: 4 (over z).
Axes of the slice: x: 2, y: 2, z: 4, core: 2. Of those that a mesh axis runs over, the one named last changes fastest.
Arguments:
- flow_state: float32 [5, 32, 128, 128], P(None, 'pitch', 'blk'), may hold values from -0.6 to 3.2, as said below
- prior_state: float32 [5, 32, 128, 128], P(None, 'pitch', 'blk'), may hold values from -0.75 to 3.35, as said below
- fourier_store: float32 [2, 49, 10, 128, 128], P(None, None, None, ('blk', 'pitch')), may hold values from -0.15 to 2.6, as said below
- sample_times: int32 [2, 128, 128], P(None, ('blk', 'pitch')), may hold values from 0 to 95
- harmonics: int32 [128, 128], P(('blk', 'pitch')), may hold values from 12 to 24
Outputs:
- new_state: float32 [5, 32, 128, 128], P(None, 'pitch', 'blk')
- new_store: float32 [2, 49, 10, 128, 128], P(None, None, None, ('blk', 'pitch'))
- new_ghosts: float32 [2, 10, 128, 128], P(None, None, ('blk', 'pitch'))
Inputs may be any that keep to these rules, and one draw needn't show every extreme that they name: `flow_state`: density between 0.7 and 1.3, momenta between -0.6 and 0.6, total energy between 2.2 and 3.2. `prior_state`: each entry within 0.15 of flow_state's. `fourier_store`: the k-th cosine and sine coefficients are at most 0.08 / k in magnitude.
All inputs are finite; a program needn't handle non-finite values.
Results may differ from a plain program's by a relative error of at most 0.000068.
Values sent between devices are 32-bit elements; how exact they have to be, the bound alone decides.
No kernel may reach another device: no remote copies, remote signals or barrier semaphores. Data moves between devices by JAX's collectives and lax.ppermute only.
A program may use at most 64 MiB of HBM per device.

v0:
```python
import math

import jax
import jax.numpy as jnp
from jax import lax
from jax.sharding import PartitionSpec as P

NT = 96


gamma_less = 0.4
diss_coeff = 0.03125
section_coefs = (1.0 / 3.0, 0.5, 1.0)
pseudo_step = 0.1
physical_step = 0.25
relax_rate = 0.125
lag_turns = 0.3


def padded_2(block, sides, width):
    for axis, dim in sides:
        count = lax.axis_size(axis)
        forward = [(i, i + 1) for i in range(count - 1)]
        backward = [(target, source) for source, target in forward]
        low = lax.ppermute(
            lax.slice_in_dim(block, block.shape[dim] - width, None, axis=dim), axis, forward
        )
        high = lax.ppermute(lax.slice_in_dim(block, 0, width, axis=dim), axis, backward)
        block = jnp.concatenate([low, block, high], axis=dim)
    return block


def fluxes(current, direction):
    density = current[0]
    velocity = current[direction] / density
    pressure = gamma_less * (
        current[4]
        - 0.5
        * (current[1] * current[1] + current[2] * current[2] + current[3] * current[3])
        / density
    )
    flux_parts = [
        current[direction],
        current[1] * velocity,
        current[2] * velocity,
        current[3] * velocity,
        (current[4] + pressure) * velocity,
    ]
    flux_parts[direction] = flux_parts[direction] + pressure
    return jnp.stack(flux_parts)


def face_sum(padded, direction):
    cells_n = padded.shape[direction] - 4
    faces_n = cells_n + 1
    cell_flux = fluxes(padded, direction)

    def window(values, offset, length):
        return lax.slice_in_dim(values, offset, offset + length, axis=direction)

    face_flux = 0.5 * (
        window(cell_flux, 1, faces_n) + window(cell_flux, 2, faces_n)
    ) - diss_coeff * (
        window(padded, 3, faces_n)
        - 3.0 * window(padded, 2, faces_n)
        + 3.0 * window(padded, 1, faces_n)
        - window(padded, 0, faces_n)
    )
    return window(face_flux, 1, cells_n) - window(face_flux, 0, cells_n)


def harmonic_tables(phases_at, harm_count):
    orders = jnp.arange(1, harm_count + 1).astype(jnp.float32).reshape((harm_count, 1, 1))
    angles = orders * phases_at[None]
    return (jnp.cos(angles), jnp.sin(angles))


def rebuild(coeffs, phases_at, active):
    harm_count = (coeffs.shape[0] - 1) // 2
    cosines, sines = harmonic_tables(phases_at, harm_count)
    orders = jnp.arange(1, harm_count + 1).reshape((harm_count, 1, 1))
    active_mask = (orders <= active[None]).astype(jnp.float32)
    harm_terms = (
        coeffs[1 : harm_count + 1] * (active_mask * cosines)[:, None]
        + coeffs[harm_count + 1 :] * (active_mask * sines)[:, None]
    )
    return coeffs[0] + jnp.sum(harm_terms, axis=0)


def refresh(coeffs, samples, phases_at):
    harm_count = (coeffs.shape[0] - 1) // 2
    cosines, sines = harmonic_tables(phases_at, harm_count)
    mean_part = (1.0 - relax_rate) * coeffs[0] + relax_rate * samples
    cos_part = (1.0 - relax_rate) * coeffs[1 : harm_count + 1] + 2.0 * relax_rate * samples[
        None
    ] * cosines[:, None]
    sin_part = (1.0 - relax_rate) * coeffs[harm_count + 1 :] + 2.0 * relax_rate * samples[
        None
    ] * sines[:, None]
    return jnp.concatenate([mean_part[None], cos_part, sin_part], axis=0)


def shards(flow_state, prior_state, fourier_store, sample_times, harmonics):
    pitch_at = lax.axis_index("pitch")
    pitch_end = lax.axis_size("pitch") - 1
    blk_at = lax.axis_index("blk")
    blk_end = lax.axis_size("blk") - 1
    block_rows = flow_state.shape[2]
    radial_cells = flow_state.shape[3]
    period = 2.0 * math.pi / NT
    phase_lag = 2.0 * math.pi * lag_turns
    phases = sample_times.astype(jnp.float32) * period
    low_share = rebuild(fourier_store[0], phases[0] - phase_lag, harmonics)
    high_share = rebuild(fourier_store[1], phases[1] + phase_lag, harmonics)
    low_whole, high_whole = (
        lax.all_gather(low_share, "pitch", axis=1, tiled=True),
        lax.all_gather(high_share, "pitch", axis=1, tiled=True),
    )
    ghost_shape = (5, 2, block_rows, radial_cells)
    low_ghost = low_whole.reshape(ghost_shape)
    high_ghost = high_whole.reshape(ghost_shape)
    current = flow_state
    for section_coef in section_coefs:
        pitch_pad = padded_2(current, (("pitch", 1),), 2)
        axial_pad = padded_2(current, (("blk", 2),), 2)
        pitch_pad = jnp.concatenate(
            [
                jnp.where(pitch_at == 0, low_ghost, pitch_pad[:, :2]),
                current,
                jnp.where(pitch_at == pitch_end, high_ghost, pitch_pad[:, -2:]),
            ],
            axis=1,
        )
        lower_edge = jnp.broadcast_to(current[:, :, :1], axial_pad[:, :, :2].shape)
        upper_edge = jnp.broadcast_to(current[:, :, -1:], axial_pad[:, :, :2].shape)
        axial_pad = jnp.concatenate(
            [
                jnp.where(blk_at == 0, lower_edge, axial_pad[:, :, :2]),
                current,
                jnp.where(blk_at == blk_end, upper_edge, axial_pad[:, :, -2:]),
            ],
            axis=2,
        )
        radial_pad = jnp.pad(current, ((0, 0), (0, 0), (0, 0), (2, 2)), mode="edge")
        summed = face_sum(pitch_pad, 1) + face_sum(axial_pad, 2) + face_sum(radial_pad, 3)
        summed = summed + (3.0 * current - 4.0 * flow_state + prior_state) * (0.5 / physical_step)
        current = flow_state - section_coef * pseudo_step * summed
    face_shape = (10, block_rows, radial_cells)
    upper_face = current[:, -2:].reshape(face_shape)
    lower_face = current[:, :2].reshape(face_shape)
    nothing = jnp.zeros_like(lower_face)
    upper_mine, lower_mine = (
        lax.psum_scatter(
            jnp.where(pitch_at == pitch_end, upper_face, nothing),
            "pitch",
            scatter_dimension=1,
            tiled=True,
        ),
        lax.psum_scatter(
            jnp.where(pitch_at == 0, lower_face, nothing), "pitch", scatter_dimension=1, tiled=True
        ),
    )
    next_phases = phases + period
    low_store = refresh(fourier_store[0], upper_mine, next_phases[0])
    high_store = refresh(fourier_store[1], lower_mine, next_phases[1])
    ghosts = jnp.stack(
        [
            rebuild(low_store, next_phases[0] - phase_lag, harmonics),
            rebuild(high_store, next_phases[1] + phase_lag, harmonics),
        ]
    )
    return (current, jnp.stack([low_store, high_store]), ghosts)


def solution(mesh):
    placed = (
        P(None, "pitch", "blk", None),
        P(None, "pitch", "blk", None),
        P(None, None, None, ("blk", "pitch"), None),
        P(None, ("blk", "pitch"), None),
        P(("blk", "pitch"), None),
    )
    return jax.shard_map(
        shards,
        mesh=mesh,
        in_specs=placed,
        out_specs=(
            P(None, "pitch", "blk", None),
            P(None, None, None, ("blk", "pitch"), None),
            P(None, None, ("blk", "pitch"), None),
        ),
        check_vma=False,
    )
```

profile of v0, /device:TPU:4, one launch (start us, length us, event | category | flops | bytes accessed | tf_op | source)
XLA Modules:
  0.0 150.9 jit_solution(4150837358878901428)
XLA Ops:
  7.2 1.7 %fusion.114 = (f32[5,8,2,128]{3,2,1,0:T(2,128)}, f32[5,8,2,128]{3,2,1,0:T(2,128)}) fusion(f32[5,8,16,128]{3,2,1,0:T(8,128)} %param.5), kind=kLoop, calls=%fused_computation.305 | loop fusion | bytes 163840 | tf_op jit(solution)/shard_map/slice | solution.py:28
  8.9 1.9 %collective-permute-start.2 = (f32[5,8,2,128]{3,2,1,0:T(2,128)}, f32[5,8,2,128]{3,2,1,0:T(2,128)}, u32[]{:S(2)}, u32[]{:S(2)}) collective-permute-start(f32[5,8,2,128]{3,2,1,0:T(2,128)} %get-tuple-element.86), channel_id=1, source_target_pairs={{0,4},{4,8},{8,12},{12,16},{16,20},{20,24},{24,28},{1,5},{5,9},{9,... | collective-permute-start | bytes 122888 | tf_op jit(solution)/shard_map/ppermute | solution.py:25
  10.8 4.5 %collective-permute-start.3 = (f32[5,8,2,128]{3,2,1,0:T(2,128)}, f32[5,8,2,128]{3,2,1,0:T(2,128)}, u32[]{:S(2)}, u32[]{:S(2)}) collective-permute-start(f32[5,8,2,128]{3,2,1,0:T(2,128)} %get-tuple-element.85), channel_id=1, source_target_pairs={{4,0},{8,4},{12,8},{16,12},{20,16},{24,20},{28,24},{5,1},{9,5},{13... | collective-permute-start | bytes 122888 | tf_op jit(solution)/shard_map/ppermute | solution.py:28
  15.4 1.6 %fusion.112 = (f32[5,2,16,128]{3,2,1,0:T(8,128)}, f32[5,2,16,128]{3,2,1,0:T(8,128)}) fusion(f32[5,8,16,128]{3,2,1,0:T(8,128)} %param.5), kind=kLoop, calls=%fused_computation.303 | loop fusion | bytes 327680 | tf_op jit(solution)/shard_map/slice | solution.py:28
  17.0 4.1 %collective-permute-start = (f32[5,2,16,128]{3,2,1,0:T(8,128)}, f32[5,2,16,128]{3,2,1,0:T(8,128)}, u32[]{:S(2)}, u32[]{:S(2)}) collective-permute-start(f32[5,2,16,128]{3,2,1,0:T(8,128)} %get-tuple-element.82), channel_id=1, source_target_pairs={{0,1},{1,2},{2,3},{4,5},{5,6},{6,7},{8,9},{9,10},{10,11},{12,13},{... | collective-permute-start | bytes 245768 | tf_op jit(solution)/shard_map/ppermute | solution.py:25
  21.1 1.3 collective-permute-start.1
  22.4 1.2 fusion.115
  23.6 1.6 %fusion.113 = (f32[5,8,1,128]{3,2,1,0:T(1,128)}, f32[5,8,1,128]{3,2,1,0:T(1,128)}) fusion(f32[5,8,16,128]{3,2,1,0:T(8,128)} %param.5), kind=kLoop, calls=%fused_computation.304 | loop fusion | bytes 81920 | tf_op jit(solution)/shard_map/slice | solution.py:135
  26.2 0.3 pad_maximum_fusion.7
  26.7 1.1 fusion.16
  27.9 2.9 %multiply_sine_fusion.3 = (f32[24,4,128]{2,1,0:T(4,128)S(1)}, f32[24,4,128]{2,1,0:T(4,128)S(1)}, f32[24,4,128]{2,1,0:T(4,128)S(1)}, f32[24,4,128]{2,1,0:T(4,128)...) fusion(f32[4,128]{1,0:T(4,128)S(1)} %get-tuple-element.128, ...), kind=kLoop, calls=%fused_computation.246 | loop fusion | flops 184320 | bytes 604352 | tf_op jit(solution)/shard_map/sin | solution.py:75
  30.8 0.4 fusion.43
  31.2 0.6 bitcast_add_fusion
  31.8 14.2 %all_gather.6 = f32[10,16,128]{2,0,1:T(8,128)S(1)} all-gather(f32[10,4,128]{2,0,1:T(8,128)S(1)} %copy.52), channel_id=1, replica_groups=mesh['blk'=8,'pitch'=4] {'pitch'}, dimensions={1}, use_global_device_ids=true | all-gather | bytes 102400 | tf_op jit(solution)/shard_map/all_gather | solution.py:116
  46.1 0.7 copy.54
  46.8 13.4 %all_gather.7 = f32[10,16,128]{2,0,1:T(8,128)S(1)} all-gather(f32[10,4,128]{2,0,1:T(8,128)S(1)} %copy.54), channel_id=1, replica_groups=mesh['blk'=8,'pitch'=4] {'pitch'}, dimensions={1}, use_global_device_ids=true | all-gather | bytes 102400 | tf_op jit(solution)/shard_map/all_gather | solution.py:117
  60.3 0.8 broadcast_select_fusion.5
  61.1 0.8 broadcast_select_fusion.2
  62.2 0.4 fusion.37
  62.6 0.9 broadcast_select_fusion.8
  63.9 0.7 copy-done.2
  64.8 0.4 slice_reduce_fusion.2
  65.5 0.3 pad_maximum_fusion.8
  66.1 1.1 fusion.9
  67.2 1.9 %collective-permute-start.6 = (f32[5,8,2,128]{3,2,1,0:T(2,128)S(1)}, f32[5,8,2,128]{3,2,1,0:T(2,128)S(1)}, u32[]{:S(2)}, u32[]{:S(2)}) collective-permute-start(f32[5,8,2,128]{3,2,1,0:T(2,128)S(1)} %get-tuple-element.80), channel_id=1, source_target_pairs={{0,4},{4,8},{8,12},{12,16},{16,20},{20,24},{24,28},{1,5},{5,9},{9,... | collective-permute-start | bytes 122888 | tf_op jit(solution)/shard_map/ppermute | solution.py:25
  69.1 4.5 %collective-permute-start.7 = (f32[5,8,2,128]{3,2,1,0:T(2,128)S(1)}, f32[5,8,2,128]{3,2,1,0:T(2,128)S(1)}, u32[]{:S(2)}, u32[]{:S(2)}) collective-permute-start(f32[5,8,2,128]{3,2,1,0:T(2,128)S(1)} %get-tuple-element.79), channel_id=1, source_target_pairs={{4,0},{8,4},{12,8},{16,12},{20,16},{24,20},{28,24},{5,1},{9,5},{13... | collective-permute-start | bytes 122888 | tf_op jit(solution)/shard_map/ppermute | solution.py:28
  73.7 5.0 %collective-permute-start.4 = (f32[5,2,16,128]{3,2,1,0:T(8,128)S(1)}, f32[5,2,16,128]{3,2,1,0:T(8,128)S(1)}, u32[]{:S(2)}, u32[]{:S(2)}) collective-permute-start(f32[5,2,16,128]{3,2,1,0:T(8,128)S(1)} %get-tuple-element.76), channel_id=1, source_target_pairs={{0,1},{1,2},{2,3},{4,5},{5,6},{6,7},{8,9},{9,10},{10,11},{12,13},{... | collective-permute-start | bytes 245768 | tf_op jit(solution)/shard_map/ppermute | solution.py:25
  78.7 1.3 collective-permute-start.5
  80.3 0.4 fusion.30
  80.8 4.3 %collective-permute-done.5 = f32[5,2,16,128]{3,2,1,0:T(8,128)S(1)} collective-permute-done((f32[5,2,16,128]{3,2,1,0:T(8,128)S(1)}, f32[5,2,16,128]{3,2,1,0:T(8,128)S(1)}, u32[]{:S(2)}, u32[]{:S(2)}) %collective-permute-start.5) | collective-permute-done | bytes 81952 | tf_op jit(solution)/shard_map/ppermute | solution.py:28
  85.6 0.4 slice_reduce_fusion
  86.4 0.3 pad_maximum_fusion.9
  86.9 1.1 fusion.2
  88.0 1.9 %collective-permute-start.10 = (f32[5,8,2,128]{3,2,1,0:T(2,128)S(1)}, f32[5,8,2,128]{3,2,1,0:T(2,128)S(1)}, u32[]{:S(2)}, u32[]{:S(2)}) collective-permute-start(f32[5,8,2,128]{3,2,1,0:T(2,128)S(1)} %get-tuple-element.74), channel_id=1, source_target_pairs={{0,4},{4,8},{8,12},{12,16},{16,20},{20,24},{24,28},{1,5},{5,9},{9,... | collective-permute-start | bytes 122888 | tf_op jit(solution)/shard_map/ppermute | solution.py:25
  90.0 4.5 %collective-permute-start.11 = (f32[5,8,2,128]{3,2,1,0:T(2,128)S(1)}, f32[5,8,2,128]{3,2,1,0:T(2,128)S(1)}, u32[]{:S(2)}, u32[]{:S(2)}) collective-permute-start(f32[5,8,2,128]{3,2,1,0:T(2,128)S(1)} %get-tuple-element.73), channel_id=1, source_target_pairs={{4,0},{8,4},{12,8},{16,12},{20,16},{24,20},{28,24},{5,1},{9,5},{13... | collective-permute-start | bytes 122888 | tf_op jit(solution)/shard_map/ppermute | solution.py:28
  94.5 2.0 %collective-permute-start.8 = (f32[5,2,16,128]{3,2,1,0:T(8,128)S(1)}, f32[5,2,16,128]{3,2,1,0:T(8,128)S(1)}, u32[]{:S(2)}, u32[]{:S(2)}) collective-permute-start(f32[5,2,16,128]{3,2,1,0:T(8,128)S(1)} %get-tuple-element.70), channel_id=1, source_target_pairs={{0,1},{1,2},{2,3},{4,5},{5,6},{6,7},{8,9},{9,10},{10,11},{12,13},{... | collective-permute-start | bytes 245768 | tf_op jit(solution)/shard_map/ppermute | solution.py:25
  96.5 1.5 collective-permute-start.9
  98.3 0.4 fusion.23
  98.7 4.1 %collective-permute-done.9 = f32[5,2,16,128]{3,2,1,0:T(8,128)S(1)} collective-permute-done((f32[5,2,16,128]{3,2,1,0:T(8,128)S(1)}, f32[5,2,16,128]{3,2,1,0:T(8,128)S(1)}, u32[]{:S(2)}, u32[]{:S(2)}) %collective-permute-start.9) | collective-permute-done | bytes 81952 | tf_op jit(solution)/shard_map/ppermute | solution.py:28
  103.5 0.7 slice_select_fusion.1
  104.2 0.6 dynamic-slice
  105.5 32.4 %all-reduce.5.cloned.1.call-done = (f32[10,16,128]{2,1,0:T(8,128)}, f32[10,16,128]{2,1,0:T(8,128)}) async-done(((f32[10,16,128]{2,1,0:T(8,128)}, f32[10,16,128]{2,1,0:T(8,128)}), (f32[10,16,128]{2,1,0:T(8,128)}, f32[10,16,128]{2,1,0:T(8,128)})) %all-reduce.5.cloned.1.call-update) | async-done | bytes 163856
  137.9 0.8 dynamic-slice_multiply_fusion.1
  138.7 0.8 dynamic-slice_multiply_fusion
  139.5 0.9 add_reduce_fusion.1
  140.4 0.8 add_bitcast_fusion.1
  141.7 1.8 %pad_maximum_fusion = f32[2,49,10,4,128]{4,3,2,1,0:T(4,128)} fusion(f32[1,49,10,4,128]{4,3,2,1,0:T(4,128)S(1)} %maximum_bitcast_fusion.1, f32[1,49,10,4,128]{4,3,2,1,0:T(4,128)S(1)} %maximum_bitcast_fusion), kind=kLoop, calls=%fused_computation | loop fusion | flops 501760 | bytes 4014080 | tf_op jit(solution)/shard_map/stack | solution.py:172
  143.5 0.6 pad_maximum_fusion.28
  (115 shorter events, 5.1 us)
Async XLA Ops:
  7.2 19.0 %copy-start = (f32[5,8,16,128]{3,2,1,0:T(8,128)S(1)}, f32[5,8,16,128]{3,2,1,0:T(8,128)}, u32[]{:S(2)}) copy-start(f32[5,8,16,128]{3,2,1,0:T(8,128)} %param.5) | copy-start | bytes 983044
  7.2 130.7 %all-reduce.5.cloned.1.call-start = ((), (), s32[]{:S(2)}) async-start(), calls=%async_computation | async-start | bytes 327680
  8.9 51.4 %collective-permute-start.2 = (f32[5,8,2,128]{3,2,1,0:T(2,128)}, f32[5,8,2,128]{3,2,1,0:T(2,128)}, u32[]{:S(2)}, u32[]{:S(2)}) collective-permute-start(f32[5,8,2,128]{3,2,1,0:T(2,128)} %get-tuple-element.86), channel_id=1, source_target_pairs={{0,4},{4,8},{8,12},{12,16},{16,20},{20,24},{24,28},{1,5},{5,9},{9,... | collective-permute-start | bytes 122888 | tf_op jit(solution)/shard_map/ppermute | solution.py:25
  10.8 50.3 %collective-permute-start.3 = (f32[5,8,2,128]{3,2,1,0:T(2,128)}, f32[5,8,2,128]{3,2,1,0:T(2,128)}, u32[]{:S(2)}, u32[]{:S(2)}) collective-permute-start(f32[5,8,2,128]{3,2,1,0:T(2,128)} %get-tuple-element.85), channel_id=1, source_target_pairs={{4,0},{8,4},{12,8},{16,12},{20,16},{24,20},{28,24},{5,1},{9,5},{13... | collective-permute-start | bytes 122888 | tf_op jit(solution)/shard_map/ppermute | solution.py:28
  17.0 45.6 %collective-permute-start = (f32[5,2,16,128]{3,2,1,0:T(8,128)}, f32[5,2,16,128]{3,2,1,0:T(8,128)}, u32[]{:S(2)}, u32[]{:S(2)}) collective-permute-start(f32[5,2,16,128]{3,2,1,0:T(8,128)} %get-tuple-element.82), channel_id=1, source_target_pairs={{0,1},{1,2},{2,3},{4,5},{5,6},{6,7},{8,9},{9,10},{10,11},{12,13},{... | collective-permute-start | bytes 245768 | tf_op jit(solution)/shard_map/ppermute | solution.py:25
  21.1 41.5 %collective-permute-start.1 = (f32[5,2,16,128]{3,2,1,0:T(8,128)}, f32[5,2,16,128]{3,2,1,0:T(8,128)}, u32[]{:S(2)}, u32[]{:S(2)}) collective-permute-start(f32[5,2,16,128]{3,2,1,0:T(8,128)} %get-tuple-element.81), channel_id=1, source_target_pairs={{1,0},{2,1},{3,2},{5,4},{6,5},{7,6},{9,8},{10,9},{11,10},{13,12},{... | collective-permute-start | bytes 245768 | tf_op jit(solution)/shard_map/ppermute | solution.py:28
  26.6 1.2 copy-start.5
  26.7 1.2 copy-start.6
  26.7 4.1 %copy-start.1 = (f32[2,49,10,4,128]{4,3,2,1,0:T(4,128)S(1)}, f32[2,49,10,4,128]{4,3,2,1,0:T(4,128)}, u32[]{:S(2)}) copy-start(f32[2,49,10,4,128]{4,3,2,1,0:T(4,128)} %param.7) | copy-start | bytes 6021124
  63.6 1.0 copy-start.2
  67.2 12.9 %collective-permute-start.6 = (f32[5,8,2,128]{3,2,1,0:T(2,128)S(1)}, f32[5,8,2,128]{3,2,1,0:T(2,128)S(1)}, u32[]{:S(2)}, u32[]{:S(2)}) collective-permute-start(f32[5,8,2,128]{3,2,1,0:T(2,128)S(1)} %get-tuple-element.80), channel_id=1, source_target_pairs={{0,4},{4,8},{8,12},{12,16},{16,20},{20,24},{24,28},{1,5},{5,9},{9,... | collective-permute-start | bytes 122888 | tf_op jit(solution)/shard_map/ppermute | solution.py:25
  69.1 10.9 %collective-permute-start.7 = (f32[5,8,2,128]{3,2,1,0:T(2,128)S(1)}, f32[5,8,2,128]{3,2,1,0:T(2,128)S(1)}, u32[]{:S(2)}, u32[]{:S(2)}) collective-permute-start(f32[5,8,2,128]{3,2,1,0:T(2,128)S(1)} %get-tuple-element.79), channel_id=1, source_target_pairs={{4,0},{8,4},{12,8},{16,12},{20,16},{24,20},{28,24},{5,1},{9,5},{13... | collective-permute-start | bytes 122888 | tf_op jit(solution)/shard_map/ppermute | solution.py:28
  73.7 7.1 %collective-permute-start.4 = (f32[5,2,16,128]{3,2,1,0:T(8,128)S(1)}, f32[5,2,16,128]{3,2,1,0:T(8,128)S(1)}, u32[]{:S(2)}, u32[]{:S(2)}) collective-permute-start(f32[5,2,16,128]{3,2,1,0:T(8,128)S(1)} %get-tuple-element.76), channel_id=1, source_target_pairs={{0,1},{1,2},{2,3},{4,5},{5,6},{6,7},{8,9},{9,10},{10,11},{12,13},{... | collective-permute-start | bytes 245768 | tf_op jit(solution)/shard_map/ppermute | solution.py:25
  78.7 6.3 %collective-permute-start.5 = (f32[5,2,16,128]{3,2,1,0:T(8,128)S(1)}, f32[5,2,16,128]{3,2,1,0:T(8,128)S(1)}, u32[]{:S(2)}, u32[]{:S(2)}) collective-permute-start(f32[5,2,16,128]{3,2,1,0:T(8,128)S(1)} %get-tuple-element.75), channel_id=1, source_target_pairs={{1,0},{2,1},{3,2},{5,4},{6,5},{7,6},{9,8},{10,9},{11,10},{13,12},{... | collective-permute-start | bytes 245768 | tf_op jit(solution)/shard_map/ppermute | solution.py:28
  88.0 10.0 %collective-permute-start.10 = (f32[5,8,2,128]{3,2,1,0:T(2,128)S(1)}, f32[5,8,2,128]{3,2,1,0:T(2,128)S(1)}, u32[]{:S(2)}, u32[]{:S(2)}) collective-permute-start(f32[5,8,2,128]{3,2,1,0:T(2,128)S(1)} %get-tuple-element.74), channel_id=1, source_target_pairs={{0,4},{4,8},{8,12},{12,16},{16,20},{20,24},{24,28},{1,5},{5,9},{9,... | collective-permute-start | bytes 122888 | tf_op jit(solution)/shard_map/ppermute | solution.py:25
  90.0 8.1 %collective-permute-start.11 = (f32[5,8,2,128]{3,2,1,0:T(2,128)S(1)}, f32[5,8,2,128]{3,2,1,0:T(2,128)S(1)}, u32[]{:S(2)}, u32[]{:S(2)}) collective-permute-start(f32[5,8,2,128]{3,2,1,0:T(2,128)S(1)} %get-tuple-element.73), channel_id=1, source_target_pairs={{4,0},{8,4},{12,8},{16,12},{20,16},{24,20},{28,24},{5,1},{9,5},{13... | collective-permute-start | bytes 122888 | tf_op jit(solution)/shard_map/ppermute | solution.py:28
  94.5 4.2 %collective-permute-start.8 = (f32[5,2,16,128]{3,2,1,0:T(8,128)S(1)}, f32[5,2,16,128]{3,2,1,0:T(8,128)S(1)}, u32[]{:S(2)}, u32[]{:S(2)}) collective-permute-start(f32[5,2,16,128]{3,2,1,0:T(8,128)S(1)} %get-tuple-element.70), channel_id=1, source_target_pairs={{0,1},{1,2},{2,3},{4,5},{5,6},{6,7},{8,9},{9,10},{10,11},{12,13},{... | collective-permute-start | bytes 245768 | tf_op jit(solution)/shard_map/ppermute | solution.py:25
  96.5 6.3 %collective-permute-start.9 = (f32[5,2,16,128]{3,2,1,0:T(8,128)S(1)}, f32[5,2,16,128]{3,2,1,0:T(8,128)S(1)}, u32[]{:S(2)}, u32[]{:S(2)}) collective-permute-start(f32[5,2,16,128]{3,2,1,0:T(8,128)S(1)} %get-tuple-element.69), channel_id=1, source_target_pairs={{1,0},{2,1},{3,2},{5,4},{6,5},{7,6},{9,8},{10,9},{11,10},{13,12},{... | collective-permute-start | bytes 245768 | tf_op jit(solution)/shard_map/ppermute | solution.py:28
  103.1 1.1 copy-start.7
  103.2 36.3 %copy-start.4 = (f32[24,4,128]{2,1,0:T(4,128)S(1)}, f32[24,4,128]{2,1,0:T(4,128)}, u32[]{:S(2)}) copy-start(f32[24,4,128]{2,1,0:T(4,128)} %get-tuple-element.124) | copy-start | bytes 147460
  103.4 37.0 %copy-start.3 = (f32[5,8,16,128]{3,2,1,0:T(8,128)}, f32[5,8,16,128]{3,2,1,0:T(8,128)S(1)}, u32[]{:S(2)}) copy-start(f32[5,8,16,128]{3,2,1,0:T(8,128)S(1)} %fusion.83) | copy-start | bytes 983044
Sparse Core Ops, SparseCore 0:
  104.3 33.5 all-reduce.4
where the time goes:
time: 153 us; the launch traced here: 151 us
  waiting for transfers between devices  41 us (27%)
  starting transfers between devices  34.6 us (23%)
  blocking collectives  27.7 us (18%)
  other arithmetic  21.4 us (14%)
  between operations  15.6 us (10%)
  local copies, waits for them, and re-layouts  10.7 us (7%)
    unnamed x2, waiting for transfers between devices  32.5 us
    ppermute x6, starting transfers between devices, padded_2(): lax.ppermute(lax.slice_in_dim(block, 0, width, axis=dim), axis, backward)  17.7 us
    ppermute x6, starting transfers between devices, padded_2(): lax.ppermute(lax.slice_in_dim(block, block.shape[dim] - width, None, axis...  16.9 us
    all_gather x1, blocking collectives, shards(): lax.all_gather(low_share, 'pitch', axis=1, tiled=True)  14.2 us
    all_gather x1, blocking collectives, shards(): lax.all_gather(high_share, 'pitch', axis=1, tiled=True)  13.4 us
    ppermute x6, waiting for transfers between devices, padded_2(): lax.ppermute(lax.slice_in_dim(block, 0, width, axis=dim), axis, backward)  8.43 us
    sub x9, other arithmetic, face_sum(): 0.5 * (window(cell_flux, 1, faces_n) + window(cell_flux, 2, faces_n))  4.7 us
    slice x6, local copies, waits for them, and re-layouts, padded_2(): lax.slice_in_dim(block, 0, width, axis=dim)  3.38 us
  transfers between devices with their start and end apart: 13, of which 4 were waited for; matrix products, arithmetic and copies ran while one was open for 10% of the time, Pallas kernels for 0%

commit v1 on v0

v1 whole, which is shorter than its diff:
```python
import functools
import math

import jax
import jax.numpy as jnp
from jax import lax
from jax.experimental import pallas as pl
from jax.experimental.pallas import tpu as pltpu
from jax.sharding import PartitionSpec as P

NT = 96

gamma_less = 0.4
diss_coeff = 0.03125
section_coefs = (1.0 / 3.0, 0.5, 1.0)
pseudo_step = 0.1
physical_step = 0.25
relax_rate = 0.125
lag_turns = 0.3
period = 2.0 * math.pi / NT
phase_lag = 2.0 * math.pi * lag_turns

HF = 2 * len(section_coefs)
HP = HF - 2
PAD = 8

F32 = jnp.float32
VMEM = pl.BlockSpec(memory_space=pltpu.VMEM)


def call(body, outs, *args, scratch=(), aliases=None, out_specs=None, cost=0, limit=8):
    outs = [jax.ShapeDtypeStruct(shape, F32) for shape in outs]
    moved = 4 * sum(math.prod(a.shape) for a in list(args) + outs)
    return pl.pallas_call(
        body,
        out_shape=outs,
        in_specs=[VMEM] * len(args),
        out_specs=out_specs or [VMEM] * len(outs),
        scratch_shapes=list(scratch),
        input_output_aliases=aliases or {},
        compiler_params=pltpu.CompilerParams(vmem_limit_bytes=limit << 20),
        cost_estimate=pl.CostEstimate(flops=cost, bytes_accessed=moved, transcendentals=0),
    )(*args)


def is_even(axis):
    return lax.axis_index(axis) % 2 == 0


def source_of(flow, prior):
    return (2.0 / physical_step) * flow - (0.5 / physical_step) * prior


def pack_pitch(flow_ref, prior_ref, first_ref, second_ref):
    cells = flow_ref.shape[1]
    even = is_even("pitch")
    for out_ref, top in ((first_ref, even), (second_ref, jnp.logical_not(even))):
        at = jnp.where(top, cells - HF, 0)
        out_ref[:, :HF] = flow_ref[:, pl.ds(at, HF)]
        at = jnp.where(top, cells - HP, 0)
        out_ref[:, HF:] = source_of(flow_ref[:, pl.ds(at, HP)], prior_ref[:, pl.ds(at, HP)])


def doubled(values):
    return jnp.concatenate([values, values], axis=0)


def rebuild_shares(store_ref, times_ref, active_ref, *out_refs):
    share_ref, send_refs = out_refs[0], out_refs[1:]
    harm_count = (store_ref.shape[1] - 1) // 2
    signals = store_ref.shape[2]
    active = doubled(active_ref[...])
    for which in range(2):
        angle = doubled(times_ref[which]).astype(F32) * period
        angle = angle - phase_lag if which == 0 else angle + phase_lag
        cos_1, sin_1 = jnp.cos(angle), jnp.sin(angle)
        cos_k, sin_k = cos_1, sin_1
        totals = [store_ref[which, 0, v] for v in range(signals)]
        for k in range(1, harm_count + 1):
            used = active >= k
            a, b = jnp.where(used, cos_k, 0.0), jnp.where(used, sin_k, 0.0)
            for v in range(signals):
                totals[v] = totals[v] + (
                    store_ref[which, k, v] * a + store_ref[which, harm_count + k, v] * b
                )
            cos_k, sin_k = cos_k * cos_1 - sin_k * sin_1, sin_k * cos_1 + cos_k * sin_1
        for v in range(signals):
            share_ref[which, v] = totals[v]
    at = lax.axis_index("pitch")
    for step, send_ref in enumerate(send_refs, start=1):
        send_ref[...] = share_ref[jnp.where(at == step, 0, 1)]


def prepare_close(store_ref, times_ref, active_ref, table_ref, base_ref, gain_ref):
    harm_count = (store_ref.shape[1] - 1) // 2
    signals = store_ref.shape[2]
    active = doubled(active_ref[...])
    gain = jnp.full(active.shape, relax_rate, F32)
    for k in range(1, harm_count + 1):
        gain = gain + jnp.where(active >= k, 2.0 * relax_rate * math.cos(k * phase_lag), 0.0)
    gain_ref[...] = gain
    keep = 1.0 - relax_rate
    for which in range(2):
        angle = doubled(times_ref[which]).astype(F32) * period + period
        cos_1, sin_1 = jnp.cos(angle), jnp.sin(angle)
        cos_k, sin_k = cos_1, sin_1
        totals = [store_ref[which, 0, v] for v in range(signals)]
        turn = -phase_lag if which == 0 else phase_lag
        for k in range(1, harm_count + 1):
            table_ref[which, k - 1] = (2.0 * relax_rate) * cos_k
            table_ref[which, harm_count + k - 1] = (2.0 * relax_rate) * sin_k
            used = active >= k
            c, s = math.cos(k * turn), math.sin(k * turn)
            a = jnp.where(used, cos_k * c - sin_k * s, 0.0)
            b = jnp.where(used, sin_k * c + cos_k * s, 0.0)
            for v in range(signals):
                totals[v] = totals[v] + (
                    store_ref[which, k, v] * a + store_ref[which, harm_count + k, v] * b
                )
            cos_k, sin_k = cos_k * cos_1 - sin_k * sin_1, sin_k * cos_1 + cos_k * sin_1
        for v in range(signals):
            base_ref[which, v] = keep * totals[v]


def place_own(flow_ref, prior_ref, state_ref, source_ref):
    cells, rows = flow_ref.shape[1:3]
    state_ref[:, HF : HF + cells, PAD : PAD + rows] = flow_ref[...]
    source_ref[:, HP : HP + cells, PAD : PAD + rows] = source_of(flow_ref[...], prior_ref[...])


def message_layout(variables, cells):
    parts, place = [], 0
    for v in range(variables):
        for which, width in ((0, HF), (1, HP)):
            for plane in range(1 - width, cells + width - 1):
                outside = max(0, -plane, plane - cells + 1)
                count = width - outside
                parts.append((v, which, plane + width, count, place))
                place += count
    return parts, -(-place // 8) * 8


def place_pitch(own_count, rows, *refs):
    state_in, source_in, first_ref, second_ref, share_ref = refs[:5]
    state_ref, source_ref, out_1, out_2 = refs[-4:]
    ghost_refs = refs[5:-4]
    del state_in, source_in
    cells = own_count
    even = is_even("pitch")
    own_rows = slice(PAD, PAD + rows)
    for halo_ref, upper in ((first_ref, even), (second_ref, jnp.logical_not(even))):
        at = jnp.where(upper, HF + cells, 0)
        state_ref[:, pl.ds(at, HF), own_rows] = halo_ref[:, :HF]
        at = jnp.where(upper, HP + cells, 0)
        source_ref[:, pl.ds(at, HP), own_rows] = halo_ref[:, HF:]
    slabs = len(ghost_refs) + 1
    part = rows // slabs
    pitch_at = lax.axis_index("pitch")

    def place_ghosts(plane, pieces):
        for piece, piece_rows in pieces:
            for layer in range(2):
                at = PAD + piece_rows * part
                state_ref[:, plane + layer, at : at + part] = piece[:, layer * part : (layer + 1) * part]

    @pl.when(pitch_at == 0)
    def _():
        place_ghosts(
            HF - 2,
            [(share_ref[0], 0)] + [(ghost_refs[j - 1][...], j) for j in range(1, slabs)],
        )

    @pl.when(pitch_at == slabs - 1)
    def _():
        place_ghosts(
            HF + cells,
            [(share_ref[1], slabs - 1)]
            + [(ghost_refs[j - 1][...], slabs - 1 - j) for j in range(1, slabs)],
        )

    parts, _ = message_layout(state_ref.shape[0], cells)
    blk_even = is_even("blk")

    def write(up_ref, down_ref):
        for v, which, plane, count, place in parts:
            from_ref = (state_ref, source_ref)[which]
            up_ref[place : place + count] = from_ref[v, plane, PAD + rows - count : PAD + rows]
            down_ref[place : place + count] = from_ref[v, plane, PAD : PAD + count]

    @pl.when(blk_even)
    def _():
        write(out_1, out_2)

    @pl.when(jnp.logical_not(blk_even))
    def _():
        write(out_2, out_1)


def sections(cells, rows, slabs, blocks, *refs):
    state_in, source_in, first_ref, second_ref = refs[:4]
    new_ref, own_ref = refs[4:6]
    send_refs = refs[6 : 6 + slabs - 1]
    state_ref, source_ref = refs[5 + slabs : 7 + slabs]
    mid_refs = refs[7 + slabs : 9 + slabs]
    pitch_ref, axial_ref, radial_ref = refs[9 + slabs :]
    del state_in, source_in
    variables = new_ref.shape[0]
    pitch_at = lax.axis_index("pitch")
    blk_at = lax.axis_index("blk")
    parts, _ = message_layout(variables, cells)

    def unpack(low_ref, high_ref):
        for v, which, plane, count, place in parts:
            to_ref = (state_ref, source_ref)[which]
            to_ref[v, plane, PAD - count : PAD] = low_ref[place : place + count]
            to_ref[v, plane, PAD + rows : PAD + rows + count] = high_ref[place : place + count]

    @pl.when(is_even("blk"))
    def _():
        unpack(second_ref, first_ref)

    @pl.when(jnp.logical_not(is_even("blk")))
    def _():
        unpack(first_ref, second_ref)

    def clamp_ends(ref):
        planes = ref.shape[1]

        @pl.when(blk_at == 0)
        def _():
            ref[:, :, PAD - 2 : PAD] = jnp.broadcast_to(
                ref[:, :, PAD : PAD + 1], (variables, planes, 2, ref.shape[3])
            )

        @pl.when(blk_at == blocks - 1)
        def _():
            ref[:, :, PAD + rows : PAD + rows + 2] = jnp.broadcast_to(
                ref[:, :, PAD + rows - 1 : PAD + rows], (variables, planes, 2, ref.shape[3])
            )

    def keep_ghosts(ref, width):
        @pl.when(pitch_at == 0)
        def _():
            ref[:, width - 2 : width] = state_ref[:, HF - 2 : HF]

        @pl.when(pitch_at == slabs - 1)
        def _():
            ref[:, width + cells : width + cells + 2] = state_ref[:, HF + cells : HF + cells + 2]

    clamp_ends(state_ref)
    lanes = state_ref.shape[3]

    def shift_down(values, lane):
        return jnp.where(lane == lanes - 1, values, pltpu.roll(values, lanes - 1, 1))

    def shift_up(values, lane):
        return jnp.where(lane == 0, values, pltpu.roll(values, 1, 1))

    def section(coef, from_ref, width, to_ref, out_width, row_at, count):
        def fluxes(index, carry):
            plane = index + width - out_width - 1
            u = [from_ref[v, plane] for v in range(variables)]
            inverse = 1.0 / u[0]
            speed = [u[d] * inverse for d in (1, 2, 3)]
            pressure = gamma_less * (
                u[4] - 0.5 * (u[1] * speed[0] + u[2] * speed[1] + u[3] * speed[2])
            )
            half = 0.5 * pressure
            total = u[4] + pressure
            for d, flux_ref in enumerate((pitch_ref, axial_ref, radial_ref)):
                w = 0.5 * speed[d]
                for v in (1, 2, 3):
                    flux = u[v] * w
                    flux_ref[v - 1, index] = flux + half if v == d + 1 else flux
                flux_ref[3, index] = total * w
            return carry

        planes = cells + 2 * out_width
        lax.fori_loop(0, planes + 2, fluxes, 0)
        rows_at = slice(row_at, row_at + count)

        def update(index, carry):
            plane = index + width - out_width
            lane = lax.broadcasted_iota(jnp.int32, (count, lanes), 1)
            for v in range(variables):

                def state(ahead, over):
                    return from_ref[v, plane + ahead, row_at + over : row_at + over + count]

                def flux(ref, d, ahead, over):
                    at = slice(row_at + over, row_at + over + count)
                    if v == 0:
                        return 0.5 * from_ref[d, plane + ahead, at]
                    return ref[v - 1, index + 1 + ahead, at]

                here = state(0, 0)
                change = flux(pitch_ref, 1, 1, 0) - flux(pitch_ref, 1, -1, 0)
                change = change + (flux(axial_ref, 2, 0, 1) - flux(axial_ref, 2, 0, -1))
                near = (state(1, 0) + state(-1, 0)) + (state(0, 1) + state(0, -1))
                far = (state(2, 0) + state(-2, 0)) + (state(0, 2) + state(0, -2))
                scaled = diss_coeff * here
                along = flux(radial_ref, 3, 0, 0)
                near_here = 4.0 * scaled
                ahead = shift_down(near_here + along - shift_down(scaled, lane), lane)
                behind = shift_up(near_here - along - shift_up(scaled, lane), lane)
                change = change + (ahead + behind) + diss_coeff * (4.0 * near - far)
                change = change + (1.5 / physical_step - 18.0 * diss_coeff) * here
                source = source_ref[v, index + HP - out_width, rows_at]
                flow = state_ref[v, index + HF - out_width, rows_at]
                if to_ref is new_ref:
                    to_at = slice(row_at - PAD, row_at - PAD + count)
                else:
                    to_at = rows_at
                to_ref[v, index, to_at] = flow + (coef * pseudo_step) * (source - change)
            return carry

        lax.fori_loop(0, planes, update, 0)

    last = len(section_coefs) - 1
    from_ref, width = state_ref, HF
    for step, coef in enumerate(section_coefs):
        out_width = width - 2
        if step == last:
            section(coef, from_ref, width, new_ref, 0, PAD, rows)
            break
        to_ref = mid_refs[step]
        count = -(-(rows + 2 * out_width) // 8) * 8
        section(coef, from_ref, width, to_ref, out_width, PAD - out_width, count)
        clamp_ends(to_ref)
        keep_ghosts(to_ref, out_width)
        from_ref, width = to_ref, out_width

    part = rows // slabs

    def write_face(plane, piece, out_ref):
        for layer in range(2):
            out_ref[:, layer * part : (layer + 1) * part] = new_ref[
                :, plane + layer, piece * part : (piece + 1) * part
            ]

    @pl.when(pitch_at == 0)
    def _():
        write_face(0, 0, own_ref)
        for j in range(1, slabs):
            write_face(0, j, send_refs[j - 1])

    @pl.when(pitch_at == slabs - 1)
    def _():
        write_face(cells - 2, slabs - 1, own_ref)
        for j in range(1, slabs):
            write_face(cells - 2, slabs - 1 - j, send_refs[j - 1])


def close(chunks, *refs):
    store_ref, table_ref, base_ref, gain_ref, own_ref = refs[:5]
    got_refs = refs[5:-4]
    out_ref, ghost_ref, fresh_ref, sems = refs[-4:]
    slabs = len(got_refs) + 1
    at = lax.axis_index("pitch")
    top, bottom = own_ref[...], own_ref[...]
    for j in range(1, slabs):
        got = got_refs[j - 1][...]
        top = jnp.where(at == slabs - 1 - j, got, top)
        bottom = jnp.where(at == j, got, bottom)
    keep = 1.0 - relax_rate
    count = store_ref.shape[1]
    signals = store_ref.shape[2]
    copies = []
    for which, sample in enumerate((top, bottom)):
        ghost_ref[which] = base_ref[which] + sample * gain_ref[...][None]
        for lo, hi in zip(chunks[:-1], chunks[1:]):
            for k in range(lo, hi):
                weight = relax_rate if k == 0 else table_ref[which, k - 1]
                for v in range(signals):
                    fresh_ref[which, k, v] = keep * store_ref[which, k, v] + weight * sample[v]
            copy = pltpu.make_async_copy(
                fresh_ref.at[which, pl.ds(lo, hi - lo)],
                out_ref.at[which, pl.ds(lo, hi - lo)],
                sems.at[len(copies)],
            )
            copy.start()
            copies.append(copy)
    for copy in copies:
        copy.wait()


def swap_pairs(count, start):
    pairs = [(i, i + 1) for i in range(start, count - 1, 2)]
    return pairs + [(b, a) for a, b in pairs]


def shards(flow_state, prior_state, fourier_store, sample_times, harmonics):
    slabs = lax.axis_size("pitch")
    blocks = lax.axis_size("blk")
    variables, cells, rows, lanes = flow_state.shape
    orders, signals, part = fourier_store.shape[1:4]
    store = fourier_store.reshape(2, orders, variables, 2 * part, lanes)
    halo = (variables, HF + HP, rows, lanes)
    face = (variables, 2 * part, lanes)

    first, second = call(pack_pitch, [halo, halo], flow_state, prior_state)
    first = lax.ppermute(first, "pitch", swap_pairs(slabs, 0))
    second = lax.ppermute(second, "pitch", swap_pairs(slabs, 1))

    share, *sends = call(
        rebuild_shares,
        [(2,) + face] + [face] * (slabs - 1),
        store,
        sample_times,
        harmonics,
    )
    ghosts = [
        lax.ppermute(send, "pitch", [(j, 0), (slabs - 1 - j, slabs - 1)])
        for j, send in enumerate(sends, start=1)
    ]

    long_rows = rows + 2 * PAD
    state_shape = (variables, cells + 2 * HF, long_rows, lanes)
    source_shape = (variables, cells + 2 * HP, long_rows, lanes)
    state, source = call(place_own, [state_shape, source_shape], flow_state, prior_state)
    _, length = message_layout(variables, cells)
    state, source, out_1, out_2 = call(
        functools.partial(place_pitch, cells, rows),
        [state_shape, source_shape, (length, lanes), (length, lanes)],
        state,
        source,
        first,
        second,
        share,
        *ghosts,
        aliases={0: 0, 1: 1},
    )
    got_1 = lax.ppermute(out_1, "blk", swap_pairs(blocks, 0))
    got_2 = lax.ppermute(out_2, "blk", swap_pairs(blocks, 1))
    table, base, gain = call(
        prepare_close,
        [(2, orders - 1, 2 * part, lanes), (2,) + face, (2 * part, lanes)],
        store,
        sample_times,
        harmonics,
    )
    flux_shape = (variables - 1, cells + 2 * HP + 2, long_rows, lanes)
    outs = call(
        functools.partial(sections, cells, rows, slabs, blocks),
        [flow_state.shape] + [face] * slabs + [state_shape, source_shape],
        state,
        source,
        got_1,
        got_2,
        scratch=[
            pltpu.VMEM((variables, cells + 2 * HP, long_rows, lanes), F32),
            pltpu.VMEM((variables, cells + 2 * HP - 4, long_rows, lanes), F32),
        ]
        + [pltpu.VMEM(flux_shape, F32)] * 3,
        aliases={0: 1 + slabs, 1: 2 + slabs},
        limit=16,
    )
    new_state, own, sends = outs[0], outs[1], outs[2 : 1 + slabs]
    got = [
        lax.ppermute(send, "pitch", [(0, j), (slabs - 1, slabs - 1 - j)])
        for j, send in enumerate(sends, start=1)
    ]
    pieces = 7
    chunks = [orders * i // pieces for i in range(pieces + 1)]
    new_store, new_ghosts = call(
        functools.partial(close, chunks),
        [store.shape, (2,) + face],
        store,
        table,
        base,
        gain,
        own,
        *got,
        scratch=[pltpu.VMEM(store.shape, F32), pltpu.SemaphoreType.DMA((2 * pieces,))],
        out_specs=[pl.BlockSpec(memory_space=pl.ANY), VMEM],
    )
    return (
        new_state,
        new_store.reshape(fourier_store.shape),
        new_ghosts.reshape(2, signals, part, lanes),
    )


def solution(mesh):
    placed = (
        P(None, "pitch", "blk", None),
        P(None, "pitch", "blk", None),
        P(None, None, None, ("blk", "pitch"), None),
        P(None, ("blk", "pitch"), None),
        P(("blk", "pitch"), None),
    )
    return jax.shard_map(
        shards,
        mesh=mesh,
        in_specs=placed,
        out_specs=(
            P(None, "pitch", "blk", None),
            P(None, None, None, ("blk", "pitch"), None),
            P(None, None, ("blk", "pitch"), None),
        ),
        check_vma=False,
    )
```

time: 153 us -> 54.5 us (0.36); the launches traced: 151 us -> 54 us
  blocking collectives: 27.7 us -> 0 us
  waiting for transfers between devices: 41 us -> 16.1 us
  other arithmetic: 21.4 us -> 0 us
  between operations: 15.6 us -> 0.82 us
  starting transfers between devices: 34.6 us -> 20.8 us
  Pallas kernels: 0 us -> 11.4 us
  local copies, waits for them, and re-layouts: 10.7 us -> 4.88 us
    unnamed x2 -> x0, waiting for transfers between devices: 32.5 us -> none
    all_gather x2 -> x0, blocking collectives: 27.7 us -> none  [the longest x1 14.2 us: shards(): lax.all_gather(low_share, 'pitch', axis=1, tiled=True)]
    ppermute x12 -> x10, starting transfers between devices: 34.5 us -> 20.8 us  [the longest x3 8.01 us: shards(): lax.ppermute(send, 'pitch', [(0, j), (slabs - 1, slabs - 1 - j)])]
    pallas_call x0 -> x7, Pallas kernels: none -> 11.4 us  [call(): pl.pallas_call(body, out_shape=outs, in_specs=[VMEM] * len(args), out_spe...]
    ppermute x12 -> x10, waiting for transfers between devices: 8.49 us -> 16.1 us  [the longest x1 8.8 us: shards(): got_2 = lax.ppermute(out_2, 'blk', swap_pairs(blocks, 1))]
    slice x12 -> x0, local copies, waits for them, and re-layouts: 7.07 us -> none  [the longest x6 3.38 us: padded_2(): lax.slice_in_dim(block, 0, width, axis=dim)]
    sub x12 -> x0, other arithmetic: 5.45 us -> none  [the longest x9 4.7 us: face_sum(): 0.5 * (window(cell_flux, 1, faces_n) + window(cell_flux, 2, faces_n))]
    another operation x14 -> x0, other arithmetic: 3.89 us -> none  [the longest x3 2.19 us: shards(): return (current, jnp.stack([low_store, high_store]), ghosts)]
  transfers between devices with their start and end apart: 13 -> 10, of which waited for: 4 -> 4; matrix products, arithmetic and copies ran while one was open for 10% -> 0% of each run, Pallas kernels for 0% -> 1%
where the time goes in v1:
time: 54.5 us; the launch traced here: 54 us
  starting transfers between devices  20.8 us (38%)
  waiting for transfers between devices  16.1 us (30%)
  Pallas kernels  11.4 us (21%)
  local copies, waits for them, and re-layouts  4.88 us (9%)
  between operations  0.82 us (2%)
    pallas_call x7, Pallas kernels, call(): pl.pallas_call(body, out_shape=outs, in_specs=[VMEM] * len(args), out_spe...  11.4 us
    ppermute x1, waiting for transfers between devices, shards(): got_2 = lax.ppermute(out_2, 'blk', swap_pairs(blocks, 1))  8.8 us
    ppermute x3, starting transfers between devices, shards(): lax.ppermute(send, 'pitch', [(0, j), (slabs - 1, slabs - 1 - j)])  8.01 us
    ppermute x3, starting transfers between devices, shards(): lax.ppermute(send, 'pitch', [(j, 0), (slabs - 1 - j, slabs - 1)])  6.97 us
    unnamed x20, local copies, waits for them, and re-layouts  4.88 us
    ppermute x3, waiting for transfers between devices, shards(): lax.ppermute(send, 'pitch', [(0, j), (slabs - 1, slabs - 1 - j)])  3.75 us
    ppermute x3, waiting for transfers between devices, shards(): lax.ppermute(send, 'pitch', [(j, 0), (slabs - 1 - j, slabs - 1)])  3.59 us
    ppermute x1, starting transfers between devices, shards(): got_2 = lax.ppermute(out_2, 'blk', swap_pairs(blocks, 1))  3.43 us
  transfers between devices with their start and end apart: 10, of which 4 were waited for; matrix products, arithmetic and copies ran while one was open for 0% of the time, Pallas kernels for 1%

profile of v1, /device:TPU:4, one launch (start us, length us, event | category | flops | bytes accessed | tf_op | source)
XLA Modules:
  0.0 54.0 jit_solution(3586294732691617739)
XLA Ops:
  0.6 0.0 copy-start.2
  0.6 1.0 %copy-done.2 = f32[5,8,16,128]{3,2,1,0:T(8,128)S(1)} copy-done((f32[5,8,16,128]{3,2,1,0:T(8,128)S(1)}, f32[5,8,16,128]{3,2,1,0:T(8,128)}, u32[]{:S(2)}) %copy-start.2) | copy-done | bytes 327704
  1.6 0.0 copy-start.4
  1.6 1.0 %copy-done.4 = f32[5,8,16,128]{3,2,1,0:T(8,128)S(1)} copy-done((f32[5,8,16,128]{3,2,1,0:T(8,128)S(1)}, f32[5,8,16,128]{3,2,1,0:T(8,128)}, u32[]{:S(2)}) %copy-start.4) | copy-done | bytes 327704
  2.6 0.0 copy-start.3
  2.6 0.0 copy-start.5
  2.6 0.1 shard_map.77
  2.7 1.6 %collective-permute-start = (f32[5,10,16,128]{3,2,1,0:T(8,128)S(1)}, f32[5,10,16,128]{3,2,1,0:T(8,128)S(1)}, u32[]{:S(2)}, u32[]{:S(2)}) collective-permute-start(f32[5,10,16,128]{3,2,1,0:T(8,128)S(1)} %get-tuple-element.27), channel_id=1, source_target_pairs={{0,1},{2,3},{1,0},{3,2},{4,5},{6,7},{5,4},{7,6},{8,9},{10,11},{9,8... | collective-permute-start | bytes 1228808 | tf_op jit(solution)/shard_map/ppermute | solution.py:402
  4.3 0.7 %collective-permute-start.1 = (f32[5,10,16,128]{3,2,1,0:T(8,128)S(1)}, f32[5,10,16,128]{3,2,1,0:T(8,128)S(1)}, u32[]{:S(2)}, u32[]{:S(2)}) collective-permute-start(f32[5,10,16,128]{3,2,1,0:T(8,128)S(1)} %get-tuple-element.28), channel_id=1, source_target_pairs={{1,2},{2,1},{5,6},{6,5},{9,10},{10,9},{13,14},{14,13},{17,18},{18,... | collective-permute-start | bytes 1228808 | tf_op jit(solution)/shard_map/ppermute | solution.py:403
  5.0 0.0 copy-start
  5.0 1.6 %copy-done = f32[2,49,10,4,128]{4,3,2,1,0:T(4,128)S(1)} copy-done((f32[2,49,10,4,128]{4,3,2,1,0:T(4,128)S(1)}, f32[2,49,10,4,128]{4,3,2,1,0:T(4,128)}, u32[]{:S(2)}) %copy-start) | copy-done | bytes 2007064
  6.5 0.0 copy-start.6
  6.5 0.7 %copy-done.6 = s32[2,4,128]{2,1,0:T(4,128)S(1)} copy-done((s32[2,4,128]{2,1,0:T(4,128)S(1)}, s32[2,4,128]{2,1,0:T(4,128)}, u32[]{:S(2)}) %copy-start.6) | copy-done | bytes 4120
  7.2 0.0 copy-start.8
  7.2 0.7 %copy-done.8 = s32[4,128]{1,0:T(4,128)S(1)} copy-done((s32[4,128]{1,0:T(4,128)S(1)}, s32[4,128]{1,0:T(4,128)}, u32[]{:S(2)}) %copy-start.8) | copy-done | bytes 2072
  7.9 0.2 shard_map.78
  8.2 1.3 %collective-permute-start.2 = (f32[5,8,128]{2,1,0:T(8,128)S(1)}, f32[5,8,128]{2,1,0:T(8,128)S(1)}, u32[]{:S(2)}, u32[]{:S(2)}) collective-permute-start(f32[5,8,128]{2,1,0:T(8,128)S(1)} %get-tuple-element.30), channel_id=1, source_target_pairs={{1,0},{2,3},{5,4},{6,7},{9,8},{10,11},{13,12},{14,15},{17,16},{18,... | collective-permute-start | bytes 61448 | tf_op jit(solution)/shard_map/ppermute | solution.py:413
  9.5 1.3 %collective-permute-start.3 = (f32[5,8,128]{2,1,0:T(8,128)S(1)}, f32[5,8,128]{2,1,0:T(8,128)S(1)}, u32[]{:S(2)}, u32[]{:S(2)}) collective-permute-start(f32[5,8,128]{2,1,0:T(8,128)S(1)} %get-tuple-element.31), channel_id=1, source_target_pairs={{2,0},{1,3},{6,4},{5,7},{10,8},{9,11},{14,12},{13,15},{18,16},{17,... | collective-permute-start | bytes 61448 | tf_op jit(solution)/shard_map/ppermute | solution.py:413
  10.8 4.4 %collective-permute-start.4 = (f32[5,8,128]{2,1,0:T(8,128)S(1)}, f32[5,8,128]{2,1,0:T(8,128)S(1)}, u32[]{:S(2)}, u32[]{:S(2)}) collective-permute-start(f32[5,8,128]{2,1,0:T(8,128)S(1)} %get-tuple-element.32), channel_id=1, source_target_pairs={{3,0},{0,3},{7,4},{4,7},{11,8},{8,11},{15,12},{12,15},{19,16},{16,... | collective-permute-start | bytes 61448 | tf_op jit(solution)/shard_map/ppermute | solution.py:413
  15.2 0.0 copy-done.3
  15.2 0.0 copy-done.5
  15.2 0.1 shard_map.76
  15.2 0.3 collective-permute-done.2.refs_5_
  15.6 3.3 %collective-permute-done.3.refs_6_ = f32[5,8,128]{2,1,0:T(8,128)S(1)} collective-permute-done((f32[5,8,128]{2,1,0:T(8,128)S(1)}, f32[5,8,128]{2,1,0:T(8,128)S(1)}, u32[]{:S(2)}, u32[]{:S(2)}) %collective-permute-start.3) | collective-permute-done | bytes 20512 | tf_op jit(solution)/shard_map/ppermute | solution.py:413
  18.8 0.0 collective-permute-done.4.refs_7_
  18.8 0.0 collective-permute-done.refs_2_
  18.8 0.0 collective-permute-done.1.refs_3_
  18.8 0.2 shard_map.79
  19.1 0.1 collective-permute-start.5
  19.2 3.4 %collective-permute-start.6 = (f32[616,128]{1,0:T(8,128)S(1)}, f32[616,128]{1,0:T(8,128)S(1)}, u32[]{:S(2)}, u32[]{:S(2)}) collective-permute-start(f32[616,128]{1,0:T(8,128)S(1)} %get-tuple-element.36), channel_id=1, source_target_pairs={{4,8},{12,16},{20,24},{8,4},{16,12},{24,20},{5,9},{13,17},{21,25},... | collective-permute-start | bytes 946184 | tf_op jit(solution)/shard_map/ppermute | solution.py:434
  22.6 0.0 collective-permute-done.5.refs_2_
  22.6 8.8 %collective-permute-done.6.refs_3_ = f32[616,128]{1,0:T(8,128)S(1)} collective-permute-done((f32[616,128]{1,0:T(8,128)S(1)}, f32[616,128]{1,0:T(8,128)S(1)}, u32[]{:S(2)}, u32[]{:S(2)}) %collective-permute-start.6) | collective-permute-done | bytes 315424 | tf_op jit(solution)/shard_map/ppermute | solution.py:434
  31.4 0.0 copy-start.1
  31.4 0.0 copy-start.7
  31.4 0.0 copy-start.9
  31.4 8.5 %shard_map.80 = (f32[5,8,16,128]{3,2,1,0:T(8,128)}, f32[5,8,128]{2,1,0:T(8,128)S(1)}, f32[5,8,128]{2,1,0:T(8,128)S(1)}, f32[5,8,128]{2,1,0:T(8,128)S(1)}, f32[5,...) custom-call(f32[5,20,32,128]{3,2,1,0:T(8,128)S(1)} %get-tuple-elemen, ...), custom_call_target="tpu_custom_call", output_to_operand_aliasing={{5}: (0, {}), {6}: (1, {})} | custom-call | bytes 6938624 | tf_op jit(solution)/shard_map/pallas_call | solution.py:34
  39.9 2.2 %collective-permute-start.7 = (f32[5,8,128]{2,1,0:T(8,128)S(1)}, f32[5,8,128]{2,1,0:T(8,128)S(1)}, u32[]{:S(2)}, u32[]{:S(2)}) collective-permute-start(f32[5,8,128]{2,1,0:T(8,128)S(1)} %get-tuple-element.42), channel_id=1, source_target_pairs={{0,1},{3,2},{4,5},{7,6},{8,9},{11,10},{12,13},{15,14},{16,17},{19,... | collective-permute-start | bytes 61448 | tf_op jit(solution)/shard_map/ppermute | solution.py:460
  42.1 2.5 %collective-permute-start.8 = (f32[5,8,128]{2,1,0:T(8,128)S(1)}, f32[5,8,128]{2,1,0:T(8,128)S(1)}, u32[]{:S(2)}, u32[]{:S(2)}) collective-permute-start(f32[5,8,128]{2,1,0:T(8,128)S(1)} %get-tuple-element.43), channel_id=1, source_target_pairs={{0,2},{3,1},{4,6},{7,5},{8,10},{11,9},{12,14},{15,13},{16,18},{19,... | collective-permute-start | bytes 61448 | tf_op jit(solution)/shard_map/ppermute | solution.py:460
  44.5 3.4 %collective-permute-start.9 = (f32[5,8,128]{2,1,0:T(8,128)S(1)}, f32[5,8,128]{2,1,0:T(8,128)S(1)}, u32[]{:S(2)}, u32[]{:S(2)}) collective-permute-start(f32[5,8,128]{2,1,0:T(8,128)S(1)} %get-tuple-element.44), channel_id=1, source_target_pairs={{0,3},{3,0},{4,7},{7,4},{8,11},{11,8},{12,15},{15,12},{16,19},{19,... | collective-permute-start | bytes 61448 | tf_op jit(solution)/shard_map/ppermute | solution.py:460
  47.9 0.0 copy-done.1
  47.9 0.0 copy-done.7
  47.9 0.0 copy-done.9
  47.9 0.3 shard_map.81
  48.2 0.0 collective-permute-done.7.refs_5_
  48.3 0.0 collective-permute-done.8.refs_6_
  48.3 3.7 %collective-permute-done.9.refs_7_ = f32[5,8,128]{2,1,0:T(8,128)S(1)} collective-permute-done((f32[5,8,128]{2,1,0:T(8,128)S(1)}, f32[5,8,128]{2,1,0:T(8,128)S(1)}, u32[]{:S(2)}, u32[]{:S(2)}) %collective-permute-start.9) | collective-permute-done | bytes 20512 | tf_op jit(solution)/shard_map/ppermute | solution.py:460
  52.0 2.0 %shard_map.82 = (f32[2,49,5,8,128]{4,3,2,1,0:T(8,128)}, f32[2,5,8,128]{3,2,1,0:T(8,128)}) custom-call(f32[2,49,5,8,128]{4,3,2,1,0:T(8,128)S(1)} %bitcast.5, f32[2,48,8,128]{3,2,1,0:T(8,128)S(1)} %get-tuple-element.38.refs_1_, f32[2,5,8,128]{3,2,1,0:T(8,128)S(1)} %get-tuple-element.39.refs_2_, f32[8,128]{1,0:T(8,128)S(1)} %get-tuple-element.40.refs_3_, ...), custom_call_target="tpu_custom_call" | custom-call | bytes 4575232 | tf_op jit(solution)/shard_map/pallas_call | solution.py:34
Async XLA Ops:
  0.6 1.0 %copy-start.2 = (f32[5,8,16,128]{3,2,1,0:T(8,128)S(1)}, f32[5,8,16,128]{3,2,1,0:T(8,128)}, u32[]{:S(2)}) copy-start(f32[5,8,16,128]{3,2,1,0:T(8,128)} %flow_ref.3) | copy-start | bytes 983044
  1.6 1.0 %copy-start.4 = (f32[5,8,16,128]{3,2,1,0:T(8,128)S(1)}, f32[5,8,16,128]{3,2,1,0:T(8,128)}, u32[]{:S(2)}) copy-start(f32[5,8,16,128]{3,2,1,0:T(8,128)} %prior_ref.3) | copy-start | bytes 983044
  2.6 12.6 %copy-start.3 = (f32[5,8,16,128]{3,2,1,0:T(8,128)S(1)}, f32[5,8,16,128]{3,2,1,0:T(8,128)}, u32[]{:S(2)}) copy-start(f32[5,8,16,128]{3,2,1,0:T(8,128)} %flow_ref.3) | copy-start | bytes 983044
  2.6 12.6 %copy-start.5 = (f32[5,8,16,128]{3,2,1,0:T(8,128)S(1)}, f32[5,8,16,128]{3,2,1,0:T(8,128)}, u32[]{:S(2)}) copy-start(f32[5,8,16,128]{3,2,1,0:T(8,128)} %prior_ref.3) | copy-start | bytes 983044
  2.7 16.2 %collective-permute-start = (f32[5,10,16,128]{3,2,1,0:T(8,128)S(1)}, f32[5,10,16,128]{3,2,1,0:T(8,128)S(1)}, u32[]{:S(2)}, u32[]{:S(2)}) collective-permute-start(f32[5,10,16,128]{3,2,1,0:T(8,128)S(1)} %get-tuple-element.27), channel_id=1, source_target_pairs={{0,1},{2,3},{1,0},{3,2},{4,5},{6,7},{5,4},{7,6},{8,9},{10,11},{9,8... | collective-permute-start | bytes 1228808 | tf_op jit(solution)/shard_map/ppermute | solution.py:402
  4.3 14.6 %collective-permute-start.1 = (f32[5,10,16,128]{3,2,1,0:T(8,128)S(1)}, f32[5,10,16,128]{3,2,1,0:T(8,128)S(1)}, u32[]{:S(2)}, u32[]{:S(2)}) collective-permute-start(f32[5,10,16,128]{3,2,1,0:T(8,128)S(1)} %get-tuple-element.28), channel_id=1, source_target_pairs={{1,2},{2,1},{5,6},{6,5},{9,10},{10,9},{13,14},{14,13},{17,18},{18,... | collective-permute-start | bytes 1228808 | tf_op jit(solution)/shard_map/ppermute | solution.py:403
  5.0 1.6 %copy-start = (f32[2,49,10,4,128]{4,3,2,1,0:T(4,128)S(1)}, f32[2,49,10,4,128]{4,3,2,1,0:T(4,128)}, u32[]{:S(2)}) copy-start(f32[2,49,10,4,128]{4,3,2,1,0:T(4,128)} %param.7) | copy-start | bytes 6021124
  6.5 0.7 %copy-start.6 = (s32[2,4,128]{2,1,0:T(4,128)S(1)}, s32[2,4,128]{2,1,0:T(4,128)}, u32[]{:S(2)}) copy-start(s32[2,4,128]{2,1,0:T(4,128)} %times_ref.3) | copy-start | bytes 12292
  7.2 0.7 %copy-start.8 = (s32[4,128]{1,0:T(4,128)S(1)}, s32[4,128]{1,0:T(4,128)}, u32[]{:S(2)}) copy-start(s32[4,128]{1,0:T(4,128)} %active_ref.3) | copy-start | bytes 6148
  8.2 7.4 %collective-permute-start.2 = (f32[5,8,128]{2,1,0:T(8,128)S(1)}, f32[5,8,128]{2,1,0:T(8,128)S(1)}, u32[]{:S(2)}, u32[]{:S(2)}) collective-permute-start(f32[5,8,128]{2,1,0:T(8,128)S(1)} %get-tuple-element.30), channel_id=1, source_target_pairs={{1,0},{2,3},{5,4},{6,7},{9,8},{10,11},{13,12},{14,15},{17,16},{18,... | collective-permute-start | bytes 61448 | tf_op jit(solution)/shard_map/ppermute | solution.py:413
  9.5 9.4 %collective-permute-start.3 = (f32[5,8,128]{2,1,0:T(8,128)S(1)}, f32[5,8,128]{2,1,0:T(8,128)S(1)}, u32[]{:S(2)}, u32[]{:S(2)}) collective-permute-start(f32[5,8,128]{2,1,0:T(8,128)S(1)} %get-tuple-element.31), channel_id=1, source_target_pairs={{2,0},{1,3},{6,4},{5,7},{10,8},{9,11},{14,12},{13,15},{18,16},{17,... | collective-permute-start | bytes 61448 | tf_op jit(solution)/shard_map/ppermute | solution.py:413
  10.8 8.1 %collective-permute-start.4 = (f32[5,8,128]{2,1,0:T(8,128)S(1)}, f32[5,8,128]{2,1,0:T(8,128)S(1)}, u32[]{:S(2)}, u32[]{:S(2)}) collective-permute-start(f32[5,8,128]{2,1,0:T(8,128)S(1)} %get-tuple-element.32), channel_id=1, source_target_pairs={{3,0},{0,3},{7,4},{4,7},{11,8},{8,11},{15,12},{12,15},{19,16},{16,... | collective-permute-start | bytes 61448 | tf_op jit(solution)/shard_map/ppermute | solution.py:413
  19.1 3.5 %collective-permute-start.5 = (f32[616,128]{1,0:T(8,128)S(1)}, f32[616,128]{1,0:T(8,128)S(1)}, u32[]{:S(2)}, u32[]{:S(2)}) collective-permute-start(f32[616,128]{1,0:T(8,128)S(1)} %get-tuple-element.35), channel_id=1, source_target_pairs={{0,4},{8,12},{16,20},{24,28},{4,0},{12,8},{20,16},{28,24},{1,5},{9... | collective-permute-start | bytes 946184 | tf_op jit(solution)/shard_map/ppermute | solution.py:433
  19.2 12.2 %collective-permute-start.6 = (f32[616,128]{1,0:T(8,128)S(1)}, f32[616,128]{1,0:T(8,128)S(1)}, u32[]{:S(2)}, u32[]{:S(2)}) collective-permute-start(f32[616,128]{1,0:T(8,128)S(1)} %get-tuple-element.36), channel_id=1, source_target_pairs={{4,8},{12,16},{20,24},{8,4},{16,12},{24,20},{5,9},{13,17},{21,25},... | collective-permute-start | bytes 946184 | tf_op jit(solution)/shard_map/ppermute | solution.py:434
  31.4 16.5 %copy-start.1 = (f32[2,49,10,4,128]{4,3,2,1,0:T(4,128)S(1)}, f32[2,49,10,4,128]{4,3,2,1,0:T(4,128)}, u32[]{:S(2)}) copy-start(f32[2,49,10,4,128]{4,3,2,1,0:T(4,128)} %param.7) | copy-start | bytes 6021124
  31.4 16.5 %copy-start.7 = (s32[2,4,128]{2,1,0:T(4,128)S(1)}, s32[2,4,128]{2,1,0:T(4,128)}, u32[]{:S(2)}) copy-start(s32[2,4,128]{2,1,0:T(4,128)} %times_ref.3) | copy-start | bytes 12292
  31.4 16.5 %copy-start.9 = (s32[4,128]{1,0:T(4,128)S(1)}, s32[4,128]{1,0:T(4,128)}, u32[]{:S(2)}) copy-start(s32[4,128]{1,0:T(4,128)} %active_ref.3) | copy-start | bytes 6148
  39.9 8.4 %collective-permute-start.7 = (f32[5,8,128]{2,1,0:T(8,128)S(1)}, f32[5,8,128]{2,1,0:T(8,128)S(1)}, u32[]{:S(2)}, u32[]{:S(2)}) collective-permute-start(f32[5,8,128]{2,1,0:T(8,128)S(1)} %get-tuple-element.42), channel_id=1, source_target_pairs={{0,1},{3,2},{4,5},{7,6},{8,9},{11,10},{12,13},{15,14},{16,17},{19,... | collective-permute-start | bytes 61448 | tf_op jit(solution)/shard_map/ppermute | solution.py:460
  42.1 6.2 %collective-permute-start.8 = (f32[5,8,128]{2,1,0:T(8,128)S(1)}, f32[5,8,128]{2,1,0:T(8,128)S(1)}, u32[]{:S(2)}, u32[]{:S(2)}) collective-permute-start(f32[5,8,128]{2,1,0:T(8,128)S(1)} %get-tuple-element.43), channel_id=1, source_target_pairs={{0,2},{3,1},{4,6},{7,5},{8,10},{11,9},{12,14},{15,13},{16,18},{19,... | collective-permute-start | bytes 61448 | tf_op jit(solution)/shard_map/ppermute | solution.py:460
  44.5 7.5 %collective-permute-start.9 = (f32[5,8,128]{2,1,0:T(8,128)S(1)}, f32[5,8,128]{2,1,0:T(8,128)S(1)}, u32[]{:S(2)}, u32[]{:S(2)}) collective-permute-start(f32[5,8,128]{2,1,0:T(8,128)S(1)} %get-tuple-element.44), channel_id=1, source_target_pairs={{0,3},{3,0},{4,7},{7,4},{8,11},{11,8},{12,15},{15,12},{16,19},{19,... | collective-permute-start | bytes 61448 | tf_op jit(solution)/shard_map/ppermute | solution.py:460

commit v2 on v1

v2 whole, which is shorter than its diff:
```python
import functools
import math

import jax
import jax.numpy as jnp
from jax import lax
from jax.experimental import pallas as pl
from jax.experimental.pallas import tpu as pltpu
from jax.sharding import PartitionSpec as P

NT = 96

gamma_less = 0.4
diss_coeff = 0.03125
section_coefs = (1.0 / 3.0, 0.5, 1.0)
pseudo_step = 0.1
physical_step = 0.25
relax_rate = 0.125
lag_turns = 0.3
period = 2.0 * math.pi / NT
phase_lag = 2.0 * math.pi * lag_turns

HF = 2 * len(section_coefs)
HP = HF - 2
PAD = 8

F32 = jnp.float32
VMEM = pl.BlockSpec(memory_space=pltpu.VMEM)


HBM = pl.BlockSpec(memory_space=pltpu.MemorySpace.HBM)


def call(body, outs, *args, scratch=(), aliases=None, in_specs=None, out_specs=None, cost=0, limit=8):
    outs = [jax.ShapeDtypeStruct(shape, F32) for shape in outs]
    moved = 4 * sum(math.prod(a.shape) for a in list(args) + outs)
    return pl.pallas_call(
        body,
        out_shape=outs,
        in_specs=in_specs or [VMEM] * len(args),
        out_specs=out_specs or [VMEM] * len(outs),
        scratch_shapes=list(scratch),
        input_output_aliases=aliases or {},
        compiler_params=pltpu.CompilerParams(vmem_limit_bytes=limit << 20),
        cost_estimate=pl.CostEstimate(flops=cost, bytes_accessed=moved, transcendentals=0),
    )(*args)


def is_even(axis):
    return lax.axis_index(axis) % 2 == 0


def source_of(flow, prior):
    return (2.0 / physical_step) * flow - (0.5 / physical_step) * prior


def start_block(flow_hbm, prior_hbm, state_ref, source_ref, first_ref, second_ref, prior_ref, sems):
    cells, rows = flow_hbm.shape[1:3]
    own_rows = slice(PAD, PAD + rows)
    flow_ref = state_ref.at[:, pl.ds(HF, cells), pl.ds(PAD, rows)]
    copies = [
        pltpu.make_async_copy(flow_hbm, flow_ref, sems.at[0]),
        pltpu.make_async_copy(prior_hbm, prior_ref, sems.at[1]),
    ]
    for copy in copies:
        copy.start()
    for copy in copies:
        copy.wait()
    even = is_even("pitch")
    source_ref[:, HP : HP + cells, own_rows] = source_of(
        state_ref[:, HF : HF + cells, own_rows], prior_ref[...]
    )
    for out_ref, top in ((first_ref, even), (second_ref, jnp.logical_not(even))):
        at = jnp.where(top, cells, HF)
        out_ref[:, :HF] = state_ref[:, pl.ds(at, HF), own_rows]
        at = jnp.where(top, cells, HP)
        out_ref[:, HF:] = source_ref[:, pl.ds(at, HP), own_rows]


def pack_axial(cells, rows, state_ref, source_ref, edge_ref, corner_ref):
    refs = (state_ref, source_ref)
    edges, _ = edge_layout(state_ref.shape[0], cells, 0)
    corners, _ = corner_layout(state_ref.shape[0])
    top = is_even("pitch")

    def write(up):
        for v, which, plane, count, place in edges:
            edge_ref[place : place + count] = refs[which][v, plane, edge_rows(rows, count, up)]
        for v, which, depth, count, place in corners:
            width = (HF, HP)[which]
            plane = jnp.where(top, width + cells - depth, width + depth - 1)
            corner_ref[place : place + count] = refs[which][v, plane, edge_rows(rows, count, up)]

    @pl.when(is_even("blk"))
    def _():
        write(False)

    @pl.when(jnp.logical_not(is_even("blk")))
    def _():
        write(True)


def edge_rows(rows, count, up):
    return slice(PAD + rows - count, PAD + rows) if up else slice(PAD, PAD + count)


def halo_rows(rows, count, up):
    return slice(PAD + rows, PAD + rows + count) if up else slice(PAD - count, PAD)


def doubled(values):
    return jnp.concatenate([values, values], axis=0)


def share_sent(step):
    return jnp.where(lax.axis_index("pitch") % (2 << step) == 1 << step, 0, 1)


def rebuild_shares(store_ref, times_ref, active_ref, share_ref, send_ref):
    harm_count = (store_ref.shape[1] - 1) // 2
    signals = store_ref.shape[2]
    active = doubled(active_ref[...])
    for which in range(2):
        angle = doubled(times_ref[which]).astype(F32) * period
        angle = angle - phase_lag if which == 0 else angle + phase_lag
        cos_1, sin_1 = jnp.cos(angle), jnp.sin(angle)
        cos_k, sin_k = cos_1, sin_1
        totals = [store_ref[which, 0, v] for v in range(signals)]
        for k in range(1, harm_count + 1):
            used = active >= k
            a, b = jnp.where(used, cos_k, 0.0), jnp.where(used, sin_k, 0.0)
            for v in range(signals):
                totals[v] = totals[v] + (
                    store_ref[which, k, v] * a + store_ref[which, harm_count + k, v] * b
                )
            cos_k, sin_k = cos_k * cos_1 - sin_k * sin_1, sin_k * cos_1 + cos_k * sin_1
        for v in range(signals):
            share_ref[which, v] = totals[v]
    send_ref[0] = share_ref[share_sent(0)]


def join_shares(step, share_ref, *refs):
    got_refs, out_ref = refs[:-1], refs[-1]
    out_ref[0] = share_ref[share_sent(step)]
    at = 1
    for got_ref in got_refs:
        out_ref[at : at + got_ref.shape[0]] = got_ref[...]
        at += got_ref.shape[0]


def join_ghosts(cells, rows, slabs, state_ref, source_ref, share_ref, *refs):
    got_refs, (ghost_ref, corner_ref) = refs[:-2], refs[-2:]
    refs = (state_ref, source_ref)
    part = rows // slabs
    pitch_at = lax.axis_index("pitch")
    blk_even = is_even("blk")
    corners, _ = corner_layout(state_ref.shape[0])

    for end in range(2):

        @pl.when(pitch_at == end * (slabs - 1))
        def _():
            pieces = [share_ref[end]]
            for got_ref in got_refs:
                pieces += [got_ref[i] for i in range(got_ref.shape[0])]
            for distance, piece in enumerate(pieces):
                at = part * (distance if end == 0 else slabs - 1 - distance)
                for layer in range(2):
                    ghost_ref[:, layer, at : at + part] = piece[:, layer * part : (layer + 1) * part]

            def write(up):
                for v, which, depth, count, place in corners:
                    if which == 0 and depth <= 2:
                        at = slice(rows - count, rows) if up else slice(0, count)
                        layer = depth - 1 if end else 2 - depth
                        corner_ref[place : place + count] = ghost_ref[v, layer, at]

            pl.when(blk_even)(lambda: write(False))
            pl.when(jnp.logical_not(blk_even))(lambda: write(True))

    @pl.when((pitch_at > 0) & (pitch_at < slabs - 1))
    def _():
        bottom = is_even("pitch")

        def write(up):
            for v, which, depth, count, place in corners:
                width = (HF, HP)[which]
                plane = jnp.where(bottom, width + depth - 1, width + cells - depth)
                corner_ref[place : place + count] = refs[which][v, plane, edge_rows(rows, count, up)]

        pl.when(blk_even)(lambda: write(False))
        pl.when(jnp.logical_not(blk_even))(lambda: write(True))


def prepare_close(store_ref, times_ref, active_ref, table_ref, base_ref, gain_ref):
    harm_count = (store_ref.shape[1] - 1) // 2
    signals = store_ref.shape[2]
    active = doubled(active_ref[...])
    gain = jnp.full(active.shape, relax_rate, F32)
    for k in range(1, harm_count + 1):
        gain = gain + jnp.where(active >= k, 2.0 * relax_rate * math.cos(k * phase_lag), 0.0)
    gain_ref[...] = gain
    keep = 1.0 - relax_rate
    for which in range(2):
        angle = doubled(times_ref[which]).astype(F32) * period + period
        cos_1, sin_1 = jnp.cos(angle), jnp.sin(angle)
        cos_k, sin_k = cos_1, sin_1
        totals = [store_ref[which, 0, v] for v in range(signals)]
        turn = -phase_lag if which == 0 else phase_lag
        for k in range(1, harm_count + 1):
            table_ref[which, k - 1] = (2.0 * relax_rate) * cos_k
            table_ref[which, harm_count + k - 1] = (2.0 * relax_rate) * sin_k
            used = active >= k
            c, s = math.cos(k * turn), math.sin(k * turn)
            a = jnp.where(used, cos_k * c - sin_k * s, 0.0)
            b = jnp.where(used, sin_k * c + cos_k * s, 0.0)
            for v in range(signals):
                totals[v] = totals[v] + (
                    store_ref[which, k, v] * a + store_ref[which, harm_count + k, v] * b
                )
            cos_k, sin_k = cos_k * cos_1 - sin_k * sin_1, sin_k * cos_1 + cos_k * sin_1
        for v in range(signals):
            base_ref[which, v] = keep * totals[v]


def edge_layout(variables, cells, reach):
    parts, place = [], 0
    for v in range(variables):
        for which, width in ((0, HF), (1, HP)):
            out = min(reach, width - 1)
            for plane in range(-out, cells + out):
                count = width - max(0, -plane, plane - cells + 1)
                parts.append((v, which, plane + width, count, place))
                place += count
    return parts, -(-place // 8) * 8


def corner_layout(variables):
    parts, place = [], 0
    for v in range(variables):
        for which, width in ((0, HF), (1, HP)):
            for depth in range(1, width):
                parts.append((v, which, depth, width - depth, place))
                place += width - depth
    return parts, -(-place // 8) * 8


def place_halos(cells, rows, slabs, *refs):
    first_ref, second_ref, edge_ref, corner_1, corner_2, ghost_ref = refs[2:8]
    state_ref, source_ref, out_ref = refs[-3:]
    refs = (state_ref, source_ref)
    pitch_at = lax.axis_index("pitch")
    even = is_even("pitch")
    blk_even = is_even("blk")
    variables = state_ref.shape[0]
    own_rows = slice(PAD, PAD + rows)
    for halo_ref, upper in ((first_ref, even), (second_ref, jnp.logical_not(even))):
        at = jnp.where(upper, HF + cells, 0)
        state_ref[:, pl.ds(at, HF), own_rows] = halo_ref[:, :HF]
        at = jnp.where(upper, HP + cells, 0)
        source_ref[:, pl.ds(at, HP), own_rows] = halo_ref[:, HF:]

    @pl.when(pitch_at == 0)
    def _():
        state_ref[:, HF - 2 : HF, own_rows] = ghost_ref[...]

    @pl.when(pitch_at == slabs - 1)
    def _():
        state_ref[:, HF + cells : HF + cells + 2, own_rows] = ghost_ref[...]

    edges, _ = edge_layout(variables, cells, 0)
    corners, _ = corner_layout(variables)
    parts, _ = edge_layout(variables, cells, HF)

    def move(up):
        for v, which, plane, count, place in parts:
            out_ref[place : place + count] = refs[which][v, plane, edge_rows(rows, count, not up)]
        for v, which, plane, count, place in edges:
            refs[which][v, plane, halo_rows(rows, count, up)] = edge_ref[place : place + count]
        for corner_ref, upper in ((corner_1, even), (corner_2, jnp.logical_not(even))):
            for v, which, depth, count, place in corners:
                width = (HF, HP)[which]
                plane = jnp.where(upper, width + cells + depth - 1, width - depth)
                refs[which][v, plane, halo_rows(rows, count, up)] = corner_ref[place : place + count]

    pl.when(blk_even)(lambda: move(False))
    pl.when(jnp.logical_not(blk_even))(lambda: move(True))


class Block:
    def __init__(self, cells, rows, slabs, blocks, state_ref, source_ref, flux_refs):
        self.cells, self.rows, self.slabs, self.blocks = cells, rows, slabs, blocks
        self.state_ref, self.source_ref, self.flux_refs = state_ref, source_ref, flux_refs
        self.variables, _, _, self.lanes = state_ref.shape
        self.pitch_at = lax.axis_index("pitch")
        self.blk_at = lax.axis_index("blk")

    def clamp_ends(self, ref):
        rows = self.rows
        shape = (self.variables, ref.shape[1], 2, self.lanes)

        @pl.when(self.blk_at == 0)
        def _():
            ref[:, :, PAD - 2 : PAD] = jnp.broadcast_to(ref[:, :, PAD : PAD + 1], shape)

        @pl.when(self.blk_at == self.blocks - 1)
        def _():
            ref[:, :, PAD + rows : PAD + rows + 2] = jnp.broadcast_to(
                ref[:, :, PAD + rows - 1 : PAD + rows], shape
            )

    def keep_ghosts(self, ref, width):
        for end, at in ((0, 0), (self.slabs - 1, 2 + self.cells)):

            @pl.when(self.pitch_at == end)
            def _():
                ref[:, width - 2 + at : width + at] = self.state_ref[:, HF - 2 + at : HF + at]

    def shift_down(self, values, lane):
        return jnp.where(lane == self.lanes - 1, values, pltpu.roll(values, self.lanes - 1, 1))

    def shift_up(self, values, lane):
        return jnp.where(lane == 0, values, pltpu.roll(values, 1, 1))

    def advance(self, step, from_ref, to_ref, lo, hi):
        width = HF - 2 * step
        out_width = width - 2
        last = step == len(section_coefs) - 1
        scale = section_coefs[step] * pseudo_step
        count = -(-(self.rows + 2 * out_width) // 8) * 8
        row_at = PAD - out_width
        variables, lanes = self.variables, self.lanes
        pitch_ref, axial_ref, radial_ref = self.flux_refs

        def fluxes(plane):
            u = [from_ref[v, plane + width] for v in range(variables)]
            inverse = 1.0 / u[0]
            speed = [u[d] * inverse for d in (1, 2, 3)]
            pressure = gamma_less * (
                u[4] - 0.5 * (u[1] * speed[0] + u[2] * speed[1] + u[3] * speed[2])
            )
            half = (0.5 * scale) * pressure
            total = u[4] + pressure
            for d, flux_ref in enumerate((pitch_ref, axial_ref, radial_ref)):
                w = (0.5 * scale) * speed[d]
                for v in (1, 2, 3):
                    flux = u[v] * w
                    flux_ref[v - 1, plane + HP + 1] = flux + half if v == d + 1 else flux
                flux_ref[3, plane + HP + 1] = total * w

        def update(plane):
            lane = lax.broadcasted_iota(jnp.int32, (count, lanes), 1)
            for v in range(variables):

                def state(ahead, over):
                    return from_ref[v, plane + width + ahead, row_at + over : row_at + over + count]

                def change_of(ref, d, ahead, over):
                    def flux(sign):
                        at = row_at + sign * over
                        at = slice(at, at + count)
                        if v == 0:
                            return from_ref[d, plane + width + sign * ahead, at]
                        return ref[v - 1, plane + HP + 1 + sign * ahead, at]

                    return flux(1) - flux(-1)

                here = state(0, 0)
                change = change_of(pitch_ref, 1, 1, 0) + change_of(axial_ref, 2, 0, 1)
                along = from_ref[3, plane + width, row_at : row_at + count] if v == 0 else (
                    radial_ref[v - 1, plane + HP + 1, row_at : row_at + count]
                )
                if v == 0:
                    change = (0.5 * scale) * change
                    along = (0.5 * scale) * along
                near = (state(1, 0) + state(-1, 0)) + (state(0, 1) + state(0, -1))
                far = (state(2, 0) + state(-2, 0)) + (state(0, 2) + state(0, -2))
                scaled = (scale * diss_coeff) * here
                near_here = 4.0 * scaled
                ahead = self.shift_down(near_here + along - self.shift_down(scaled, lane), lane)
                behind = self.shift_up(near_here - along - self.shift_up(scaled, lane), lane)
                change = change + (ahead + behind) + (scale * diss_coeff) * (4.0 * near - far)
                change = change + (scale * (1.5 / physical_step - 18.0 * diss_coeff)) * here
                source = self.source_ref[v, plane + HP, row_at : row_at + count]
                flow = self.state_ref[v, plane + HF, row_at : row_at + count]
                to_at = row_at - PAD if last else row_at
                to_ref[v, plane + out_width, to_at : to_at + count] = (flow + scale * source) - change

        def pairs(body, start, stop):
            def both(index, carry):
                plane = start + 2 * index
                body(plane)
                body(plane + 1)
                return carry

            lax.fori_loop(0, (stop - start) // 2, both, 0)

        pairs(fluxes, lo - 1, hi + 1)
        pairs(update, lo, hi)
        if not last:
            self.clamp_ends(to_ref)


def start_sections(cells, rows, slabs, blocks, *refs):
    got_ref = refs[2]
    state_ref, source_ref, mid_1, mid_2, new_ref, own_ref = refs[3:9]
    send_refs, flux_refs = refs[9 : 8 + slabs], refs[8 + slabs :]
    block = Block(cells, rows, slabs, blocks, state_ref, source_ref, flux_refs)
    variables = state_ref.shape[0]
    parts, _ = edge_layout(variables, cells, HF)
    into = (state_ref, source_ref)

    def unpack(up):
        for v, which, plane, count, place in parts:
            into[which][v, plane, halo_rows(rows, count, up)] = got_ref[place : place + count]

    pl.when(is_even("blk"))(lambda: unpack(True))
    pl.when(jnp.logical_not(is_even("blk")))(lambda: unpack(False))
    block.clamp_ends(state_ref)
    block.keep_ghosts(mid_1, HF - 2)
    block.keep_ghosts(mid_2, HF - 4)
    part = rows // slabs
    high = block.pitch_at == slabs - 1

    @pl.when((block.pitch_at == 0) | high)
    def _():
        for step, (from_ref, to_ref) in enumerate(
            ((state_ref, mid_1), (mid_1, mid_2), (mid_2, new_ref))
        ):
            planes = HF - 2 * step
            lo = jnp.where(high, cells - planes, 0)
            block.advance(step, from_ref, to_ref, lo, lo + planes)

    for end, plane in ((0, 0), (slabs - 1, cells - 2)):

        @pl.when(block.pitch_at == end)
        def _():
            for j, out_ref in enumerate((own_ref,) + tuple(send_refs)):
                at = (end ^ j) * part
                for layer in range(2):
                    out_ref[:, layer * part : (layer + 1) * part] = new_ref[
                        :, plane + layer, at : at + part
                    ]


def finish_sections(cells, rows, slabs, blocks, *refs):
    state_ref, source_ref = refs[:2]
    mid_1, mid_2, new_ref = refs[5:8]
    block = Block(cells, rows, slabs, blocks, state_ref, source_ref, refs[8:])
    low, high = block.pitch_at == 0, block.pitch_at == slabs - 1
    for step, (from_ref, to_ref) in enumerate(
        ((state_ref, mid_1), (mid_1, mid_2), (mid_2, new_ref))
    ):
        done = HF - 2 * step
        out_width = done - 2
        lo = jnp.where(low, done, -out_width)
        hi = jnp.where(high, cells - done, cells + out_width)
        block.advance(step, from_ref, to_ref, lo, hi)


def close(chunks, *refs):
    new_ref, store_ref, table_ref, base_ref, gain_ref, own_ref = refs[:6]
    got_refs = refs[6:-5]
    state_hbm, out_ref, ghost_ref, fresh_ref, sems = refs[-5:]
    slabs = len(got_refs) + 1
    at = lax.axis_index("pitch")
    copies = []

    def send(from_ref, to_ref):
        copy = pltpu.make_async_copy(from_ref, to_ref, sems.at[len(copies)])
        copy.start()
        copies.append(copy)

    send(new_ref, state_hbm)
    top, bottom = own_ref[...], own_ref[...]
    for j in range(1, slabs):
        got = got_refs[j - 1][...]
        top = jnp.where(at == slabs - 1 - j, got, top)
        bottom = jnp.where(at == j, got, bottom)
    keep = 1.0 - relax_rate
    signals = store_ref.shape[2]
    for which, sample in enumerate((top, bottom)):
        for lo, hi in zip(chunks[:-1], chunks[1:]):
            for k in range(lo, hi):
                weight = relax_rate if k == 0 else table_ref[which, k - 1]
                for v in range(signals):
                    fresh_ref[which, k, v] = keep * store_ref[which, k, v] + weight * sample[v]
            window = pl.ds(lo, hi - lo)
            send(fresh_ref.at[which, window], out_ref.at[which, window])
        ghost_ref[which] = base_ref[which] + sample * gain_ref[...][None]
    for copy in copies:
        copy.wait()


def swap_pairs(count, start):
    pairs = [(i, i + 1) for i in range(start, count - 1, 2)]
    return pairs + [(b, a) for a, b in pairs]


def flip_pairs(count, bits):
    return [(i, i ^ bits) for i in range(count)]


def diagonal_pairs(slabs, blocks, start):
    along = dict((i, i) for i in range(slabs))
    along.update(swap_pairs(slabs, start))
    return [
        (b * slabs + p, other * slabs + along[p])
        for b, other in swap_pairs(blocks, 1)
        for p in range(slabs)
    ]


def shards(flow_state, prior_state, fourier_store, sample_times, harmonics):
    slabs = lax.axis_size("pitch")
    blocks = lax.axis_size("blk")
    variables, cells, rows, lanes = flow_state.shape
    orders, signals, part = fourier_store.shape[1:4]
    store = fourier_store.reshape(2, orders, variables, 2 * part, lanes)
    halo = (variables, HF + HP, rows, lanes)
    face = (variables, 2 * part, lanes)
    long_rows = rows + 2 * PAD
    state_shape = (variables, cells + 2 * HF, long_rows, lanes)
    source_shape = (variables, cells + 2 * HP, long_rows, lanes)
    corner = (corner_layout(variables)[1], lanes)

    state, source, first, second = call(
        start_block,
        [state_shape, source_shape, halo, halo],
        pltpu.with_memory_space_constraint(flow_state, pltpu.MemorySpace.HBM),
        pltpu.with_memory_space_constraint(prior_state, pltpu.MemorySpace.HBM),
        scratch=[pltpu.VMEM(flow_state.shape, F32), pltpu.SemaphoreType.DMA((2,))],
        in_specs=[HBM, HBM],
        cost=1,
    )
    first = lax.ppermute(first, "pitch", swap_pairs(slabs, 0))
    second = lax.ppermute(second, "pitch", swap_pairs(slabs, 1))

    share, send = call(
        rebuild_shares, [(2,) + face, (1,) + face], store, sample_times, harmonics
    )
    gathered, step = [lax.ppermute(send, "pitch", flip_pairs(slabs, 1))], 1
    edge, corner_1 = call(
        functools.partial(pack_axial, cells, rows),
        [(edge_layout(variables, cells, 0)[1], lanes), corner],
        state,
        source,
    )
    edge = lax.ppermute(edge, "blk", swap_pairs(blocks, 1))
    corner_1 = lax.ppermute(corner_1, ("blk", "pitch"), diagonal_pairs(slabs, blocks, 0))
    while 1 << step < slabs:
        [send] = call(
            functools.partial(join_shares, step), [(1 << step,) + face], share, *gathered
        )
        gathered.append(lax.ppermute(send, "pitch", flip_pairs(slabs, 1 << step)))
        step += 1
    ghost, corner_2 = call(
        functools.partial(join_ghosts, cells, rows, slabs),
        [(variables, 2, rows, lanes), corner],
        state,
        source,
        share,
        *gathered,
    )
    corner_2 = lax.ppermute(corner_2, ("blk", "pitch"), diagonal_pairs(slabs, blocks, 1))
    table, base, gain = call(
        prepare_close,
        [(2, orders - 1, 2 * part, lanes), (2,) + face, (2 * part, lanes)],
        store,
        sample_times,
        harmonics,
    )

    state, source, out = call(
        functools.partial(place_halos, cells, rows, slabs),
        [state_shape, source_shape, (edge_layout(variables, cells, HF)[1], lanes)],
        state,
        source,
        first,
        second,
        edge,
        corner_1,
        corner_2,
        ghost,
        gain,
        aliases={0: 0, 1: 1},
    )
    got = lax.ppermute(out, "blk", swap_pairs(blocks, 0))
    mid_shapes = [
        (variables, cells + 2 * HP, long_rows, lanes),
        (variables, cells + 2 * HP - 4, long_rows, lanes),
    ]
    flux_shape = (variables - 1, cells + 2 * HP + 2, long_rows, lanes)
    flux_scratch = [pltpu.VMEM(flux_shape, F32)] * 3
    sizes = (cells, rows, slabs, blocks)
    state, source, mid_1, mid_2, new, own, *sends = call(
        functools.partial(start_sections, *sizes),
        [state_shape, source_shape] + mid_shapes + [flow_state.shape] + [face] * slabs,
        state,
        source,
        got,
        scratch=flux_scratch,
        aliases={0: 0, 1: 1},
        limit=12,
    )
    samples = [None] * (slabs - 1)
    for j in range(slabs - 1, 0, -1):
        samples[j - 1] = lax.ppermute(
            sends[j - 1], "pitch", [(0, j), (slabs - 1, slabs - 1 - j)]
        )
    _, _, new = call(
        functools.partial(finish_sections, *sizes),
        mid_shapes + [flow_state.shape],
        state,
        source,
        mid_1,
        mid_2,
        new,
        scratch=flux_scratch,
        aliases={2: 0, 3: 1, 4: 2},
        limit=12,
    )
    pieces = 7
    chunks = [orders * i // pieces for i in range(pieces + 1)]
    new_state, new_store, new_ghosts = call(
        functools.partial(close, chunks),
        [flow_state.shape, store.shape, (2,) + face],
        new,
        store,
        table,
        base,
        gain,
        own,
        *samples,
        scratch=[pltpu.VMEM(store.shape, F32), pltpu.SemaphoreType.DMA((2 * pieces + 1,))],
        out_specs=[HBM, HBM, VMEM],
    )
    return (
        new_state,
        new_store.reshape(fourier_store.shape),
        new_ghosts.reshape(2, signals, part, lanes),
    )


def solution(mesh):
    placed = (
        P(None, "pitch", "blk", None),
        P(None, "pitch", "blk", None),
        P(None, None, None, ("blk", "pitch"), None),
        P(None, ("blk", "pitch"), None),
        P(("blk", "pitch"), None),
    )
    return jax.shard_map(
        shards,
        mesh=mesh,
        in_specs=placed,
        out_specs=(
            P(None, "pitch", "blk", None),
            P(None, None, None, ("blk", "pitch"), None),
            P(None, None, ("blk", "pitch"), None),
        ),
        check_vma=False,
    )
```

time: 54.5 us -> 44.1 us (0.81)
  waiting for transfers between devices: 16.1 us -> 5.64 us
  starting transfers between devices: 20.8 us -> 27.5 us
  local copies, waits for them, and re-layouts: 4.88 us -> 0.02 us
  Pallas kernels: 11.4 us -> 9.38 us
    ppermute x8 -> x9, waiting for transfers between devices: 16.1 us -> 5.63 us  [the longest x1 2.12 us: shards(): gathered, step = ([lax.ppermute(send, 'pitch', flip_pairs(slabs, 1))], 1)]
    ppermute x8 -> x9, starting transfers between devices: 18.5 us -> 25.1 us  [the longest x3 7.45 us: shards(): lax.ppermute(sends[j - 1], 'pitch', [(0, j), (slabs - 1, slabs - 1 - j)])]
    unnamed x20 -> x6, local copies, waits for them, and re-layouts: 4.88 us -> 0.02 us
    pallas_call x7 -> x10, Pallas kernels: 11.4 us -> 9.38 us  [call(): pl.pallas_call(body, out_shape=outs, in_specs=in_specs or [VMEM] * len(ar...]
  transfers between devices with their start and end apart: 10 -> 11, of which waited for: 4 -> 4; matrix products, arithmetic and copies ran while one was open for 0% -> 0% of each run, Pallas kernels for 1% -> 8%
where the time goes in v2:
time: 44.1 us; the launch traced here: 43.3 us
  starting transfers between devices  27.5 us (62%)
  Pallas kernels  9.38 us (21%)
  waiting for transfers between devices  5.64 us (13%)
  between operations  0.82 us (2%)
    pallas_call x10, Pallas kernels, call(): pl.pallas_call(body, out_shape=outs, in_specs=in_specs or [VMEM] * len(ar...  9.38 us
    ppermute x3, starting transfers between devices, shards(): lax.ppermute(sends[j - 1], 'pitch', [(0, j), (slabs - 1, slabs - 1 - j)])  7.45 us
    ppermute x1, starting transfers between devices, shards(): lax.ppermute(corner_2, ('blk', 'pitch'), diagonal_pairs(slabs, blocks, 1))  4.81 us
    ppermute x1, starting transfers between devices, shards(): gathered, step = ([lax.ppermute(send, 'pitch', flip_pairs(slabs, 1))], 1)  4.16 us
    ppermute x1, starting transfers between devices, shards(): gathered.append(lax.ppermute(send, 'pitch', flip_pairs(slabs, 1 << step)))  2.81 us
    ppermute x1, starting transfers between devices, shards(): lax.ppermute(corner_1, ('blk', 'pitch'), diagonal_pairs(slabs, blocks, 0))  2.65 us
    ppermute x1, starting transfers between devices, shards(): edge = lax.ppermute(edge, 'blk', swap_pairs(blocks, 1))  2.5 us
    ppermute x1, waiting for transfers between devices, shards(): gathered, step = ([lax.ppermute(send, 'pitch', flip_pairs(slabs, 1))], 1)  2.12 us
  transfers between devices with their start and end apart: 11, of which 4 were waited for; matrix products, arithmetic and copies ran while one was open for 0% of the time, Pallas kernels for 8%

profile of v2, /device:TPU:4, one launch (start us, length us, event | category | flops | bytes accessed | tf_op | source)
XLA Modules:
  0.0 43.3 jit_solution(5106790809218216133)
XLA Ops:
  0.6 1.2 %shard_map.76 = (f32[5,20,32,128]{3,2,1,0:T(8,128)S(1)}, f32[5,16,32,128]{3,2,1,0:T(8,128)S(1)}, f32[5,10,16,128]{3,2,1,0:T(8,128)S(1)}, f32[5,10,16,128]{3,2,1,0:T(8,128)S(1)}) custom-call(f32[5,8,16,128]{3,2,1,0:T(8,128)} %flow_hbm.1, f32[5,8,16,128]{3,2,1,0:T(8,128)} %prior_hbm.1), custom_call_target="tpu_custom_call" | custom-call | flops 1 | bytes 4423680 | tf_op jit(solution)/shard_map/pallas_call | solution.py:37
  1.8 0.0 copy-start
  1.9 0.0 copy-start.1
  1.9 0.0 copy-start.2
  1.9 1.6 %collective-permute-start = (f32[5,10,16,128]{3,2,1,0:T(8,128)S(1)}, f32[5,10,16,128]{3,2,1,0:T(8,128)S(1)}, u32[]{:S(2)}, u32[]{:S(2)}) collective-permute-start(f32[5,10,16,128]{3,2,1,0:T(8,128)S(1)} %get-tuple-element.34), channel_id=1, source_target_pairs={{0,1},{2,3},{1,0},{3,2},{4,5},{6,7},{5,4},{7,6},{8,9},{10,11},{9,8... | collective-permute-start | bytes 1228808 | tf_op jit(solution)/shard_map/ppermute | solution.py:536
  3.5 0.7 %collective-permute-start.1 = (f32[5,10,16,128]{3,2,1,0:T(8,128)S(1)}, f32[5,10,16,128]{3,2,1,0:T(8,128)S(1)}, u32[]{:S(2)}, u32[]{:S(2)}) collective-permute-start(f32[5,10,16,128]{3,2,1,0:T(8,128)S(1)} %get-tuple-element.35), channel_id=1, source_target_pairs={{1,2},{2,1},{5,6},{6,5},{9,10},{10,9},{13,14},{14,13},{17,18},{18,... | collective-permute-start | bytes 1228808 | tf_op jit(solution)/shard_map/ppermute | solution.py:537
  4.2 0.1 shard_map.77
  4.3 2.5 %collective-permute-start.2 = (f32[400,128]{1,0:T(8,128)S(1)}, f32[400,128]{1,0:T(8,128)S(1)}, u32[]{:S(2)}, u32[]{:S(2)}) collective-permute-start(f32[400,128]{1,0:T(8,128)S(1)} %get-tuple-element.36), channel_id=1, source_target_pairs={{4,8},{12,16},{20,24},{8,4},{16,12},{24,20},{5,9},{13,17},{21,25},... | collective-permute-start | bytes 614408 | tf_op jit(solution)/shard_map/ppermute | solution.py:549
  6.8 0.0 copy-done
  6.8 0.0 copy-done.1
  6.8 0.0 copy-done.2
  6.8 0.2 shard_map.78
  7.1 4.2 %collective-permute-start.4 = (f32[1,5,8,128]{3,2,1,0:T(8,128)S(1)}, f32[1,5,8,128]{3,2,1,0:T(8,128)S(1)}, u32[]{:S(2)}, u32[]{:S(2)}) collective-permute-start(f32[1,5,8,128]{3,2,1,0:T(8,128)S(1)} %get-tuple-element.39), channel_id=1, source_target_pairs={{0,1},{1,0},{2,3},{3,2},{4,5},{5,4},{6,7},{7,6},{8,9},{9,8},{10,11... | collective-permute-start | bytes 61448 | tf_op jit(solution)/shard_map/ppermute | solution.py:542
  11.2 2.1 %collective-permute-done.4.refs_0_ = f32[1,5,8,128]{3,2,1,0:T(8,128)S(1)} collective-permute-done((f32[1,5,8,128]{3,2,1,0:T(8,128)S(1)}, f32[1,5,8,128]{3,2,1,0:T(8,128)S(1)}, u32[]{:S(2)}, u32[]{:S(2)}) %collective-permute-start.4) | collective-permute-done | bytes 20512 | tf_op jit(solution)/shard_map/ppermute | solution.py:542
  13.4 2.8 %collective-permute-start.5 = (f32[2,5,8,128]{3,2,1,0:T(8,128)S(1)}, f32[2,5,8,128]{3,2,1,0:T(8,128)S(1)}, u32[]{:S(2)}, u32[]{:S(2)}) collective-permute-start(f32[2,5,8,128]{3,2,1,0:T(8,128)S(1)} %shard_map.79), channel_id=1, source_target_pairs={{0,2},{1,3},{2,0},{3,1},{4,6},{5,7},{6,4},{7,5},{8,10},{9,11},{10,... | collective-permute-start | bytes 122888 | tf_op jit(solution)/shard_map/ppermute | solution.py:555
  16.2 2.6 %collective-permute-start.3 = (f32[112,128]{1,0:T(8,128)S(1)}, f32[112,128]{1,0:T(8,128)S(1)}, u32[]{:S(2)}, u32[]{:S(2)}) collective-permute-start(f32[112,128]{1,0:T(8,128)S(1)} %get-tuple-element.37), channel_id=1, source_target_pairs={{4,9},{5,8},{6,11},{7,10},{12,17},{13,16},{14,19},{15,18},{20,25},... | collective-permute-start | bytes 172040 | tf_op jit(solution)/shard_map/ppermute | solution.py:550
  18.8 0.0 collective-permute-done.5.refs_1_
  18.9 4.8 %collective-permute-start.6 = (f32[112,128]{1,0:T(8,128)S(1)}, f32[112,128]{1,0:T(8,128)S(1)}, u32[]{:S(2)}, u32[]{:S(2)}) collective-permute-start(f32[112,128]{1,0:T(8,128)S(1)} %get-tuple-element.40), channel_id=1, source_target_pairs={{4,8},{5,10},{6,9},{7,11},{12,16},{13,18},{14,17},{15,19},{20,24},... | collective-permute-start | bytes 172040 | tf_op jit(solution)/shard_map/ppermute | solution.py:565
  23.7 0.3 shard_map.81
  24.0 0.0 collective-permute-done.3.refs_5_
  24.0 1.5 %collective-permute-done.6.refs_6_ = f32[112,128]{1,0:T(8,128)S(1)} collective-permute-done((f32[112,128]{1,0:T(8,128)S(1)}, f32[112,128]{1,0:T(8,128)S(1)}, u32[]{:S(2)}, u32[]{:S(2)}) %collective-permute-start.6) | collective-permute-done | bytes 57376 | tf_op jit(solution)/shard_map/ppermute | solution.py:565
  25.6 0.0 collective-permute-done.2.refs_4_
  25.6 0.0 collective-permute-done.refs_2_
  25.6 0.0 collective-permute-done.1.refs_3_
  25.6 0.2 shard_map.82
  25.8 0.8 %collective-permute-start.7 = (f32[616,128]{1,0:T(8,128)S(1)}, f32[616,128]{1,0:T(8,128)S(1)}, u32[]{:S(2)}, u32[]{:S(2)}) collective-permute-start(f32[616,128]{1,0:T(8,128)S(1)} %get-tuple-element.45), channel_id=1, source_target_pairs={{0,4},{8,12},{16,20},{24,28},{4,0},{12,8},{20,16},{28,24},{1,5},{9... | collective-permute-start | bytes 946184 | tf_op jit(solution)/shard_map/ppermute | solution.py:588
  26.6 1.2 %collective-permute-done.7.refs_2_ = f32[616,128]{1,0:T(8,128)S(1)} collective-permute-done((f32[616,128]{1,0:T(8,128)S(1)}, f32[616,128]{1,0:T(8,128)S(1)}, u32[]{:S(2)}, u32[]{:S(2)}) %collective-permute-start.7) | collective-permute-done | bytes 315424 | tf_op jit(solution)/shard_map/ppermute | solution.py:588
  27.8 2.2 %shard_map.83 = (f32[5,20,32,128]{3,2,1,0:T(8,128)S(1)}, f32[5,16,32,128]{3,2,1,0:T(8,128)S(1)}, f32[5,16,32,128]{3,2,1,0:T(8,128)S(1)}, f32[5,12,32,128]{3,2,1,...) custom-call(f32[5,20,32,128]{3,2,1,0:T(8,128)S(1)} %get-tuple-elemen, ...), custom_call_target="tpu_custom_call", output_to_operand_aliasing={{0}: (0, {}), {1}: (1, {})} | custom-call | bytes 8916992 | tf_op jit(solution)/shard_map/pallas_call | solution.py:37
  30.0 1.3 %collective-permute-start.8 = (f32[5,8,128]{2,1,0:T(8,128)S(1)}, f32[5,8,128]{2,1,0:T(8,128)S(1)}, u32[]{:S(2)}, u32[]{:S(2)}) collective-permute-start(f32[5,8,128]{2,1,0:T(8,128)S(1)} %get-tuple-element.55), channel_id=1, source_target_pairs={{0,1},{3,2},{4,5},{7,6},{8,9},{11,10},{12,13},{15,14},{16,17},{19,... | collective-permute-start | bytes 61448 | tf_op jit(solution)/shard_map/ppermute | solution.py:608
  31.4 2.3 %collective-permute-start.9 = (f32[5,8,128]{2,1,0:T(8,128)S(1)}, f32[5,8,128]{2,1,0:T(8,128)S(1)}, u32[]{:S(2)}, u32[]{:S(2)}) collective-permute-start(f32[5,8,128]{2,1,0:T(8,128)S(1)} %get-tuple-element.56), channel_id=1, source_target_pairs={{0,2},{3,1},{4,6},{7,5},{8,10},{11,9},{12,14},{15,13},{16,18},{19,... | collective-permute-start | bytes 61448 | tf_op jit(solution)/shard_map/ppermute | solution.py:608
  33.7 3.8 %collective-permute-start.10 = (f32[5,8,128]{2,1,0:T(8,128)S(1)}, f32[5,8,128]{2,1,0:T(8,128)S(1)}, u32[]{:S(2)}, u32[]{:S(2)}) collective-permute-start(f32[5,8,128]{2,1,0:T(8,128)S(1)} %get-tuple-element.57), channel_id=1, source_target_pairs={{0,3},{3,0},{4,7},{7,4},{8,11},{11,8},{12,15},{15,12},{16,19},{19,... | collective-permute-start | bytes 61448 | tf_op jit(solution)/shard_map/ppermute | solution.py:608
  37.5 2.9 %shard_map.84 = (f32[5,16,32,128]{3,2,1,0:T(8,128)S(1)}, f32[5,12,32,128]{3,2,1,0:T(8,128)S(1)}, f32[5,8,16,128]{3,2,1,0:T(8,128)S(1)}) custom-call(f32[5,20,32,128]{3,2,1,0:T(8,128)S(1)} %get-tuple-element.46.refs_0_, f32[5,16,32,128]{3,2,1,0:T(8,128)S(1)} %get-tuple-element.47.refs_1_, ...), custom_call_target="tpu_custom_call", output_to_operand_aliasing={{0}: (2, {}), {1}: (3, {}), {2}: (4, {})} | custom-call | bytes 8192000 | tf_op jit(solution)/shard_map/pallas_call | solution.py:37
  40.4 0.0 collective-permute-done.8.refs_6_
  40.5 0.0 collective-permute-done.9.refs_7_
  40.5 0.7 %collective-permute-done.10.refs_8_ = f32[5,8,128]{2,1,0:T(8,128)S(1)} collective-permute-done((f32[5,8,128]{2,1,0:T(8,128)S(1)}, f32[5,8,128]{2,1,0:T(8,128)S(1)}, u32[]{:S(2)}, u32[]{:S(2)}) %collective-permute-start.10) | collective-permute-done | bytes 20512 | tf_op jit(solution)/shard_map/ppermute | solution.py:608
  41.2 2.1 %shard_map.85 = (f32[5,8,16,128]{3,2,1,0:T(8,128)}, f32[2,49,5,8,128]{4,3,2,1,0:T(8,128)}, f32[2,5,8,128]{3,2,1,0:T(8,128)}) custom-call(f32[5,8,16,128]{3,2,1,0:T(8,128)S(1)} %get-tuple-element.51.refs_0_, f32[2,49,5,8,128]{4,3,2,1,0:T(8,128)S(1)} %bitcast.5, f32[2,48,8,128]{3,2,1,0:T(8,128)S(1)} %get-tuple-element.52.refs_2_, ...), custom_call_target="tpu_custom_call" | custom-call | bytes 5230592 | tf_op jit(solution)/shard_map/pallas_call | solution.py:37
  (2 shorter events, 0.0 us)
Async XLA Ops:
  1.8 5.0 %copy-start = (f32[2,49,10,4,128]{4,3,2,1,0:T(4,128)S(1)}, f32[2,49,10,4,128]{4,3,2,1,0:T(4,128)}, u32[]{:S(2)}) copy-start(f32[2,49,10,4,128]{4,3,2,1,0:T(4,128)} %param.7) | copy-start | bytes 6021124
  1.9 5.0 %copy-start.1 = (s32[2,4,128]{2,1,0:T(4,128)S(1)}, s32[2,4,128]{2,1,0:T(4,128)}, u32[]{:S(2)}) copy-start(s32[2,4,128]{2,1,0:T(4,128)} %times_ref.3) | copy-start | bytes 12292
  1.9 5.0 %copy-start.2 = (s32[4,128]{1,0:T(4,128)S(1)}, s32[4,128]{1,0:T(4,128)}, u32[]{:S(2)}) copy-start(s32[4,128]{1,0:T(4,128)} %active_ref.3) | copy-start | bytes 6148
  1.9 23.7 %collective-permute-start = (f32[5,10,16,128]{3,2,1,0:T(8,128)S(1)}, f32[5,10,16,128]{3,2,1,0:T(8,128)S(1)}, u32[]{:S(2)}, u32[]{:S(2)}) collective-permute-start(f32[5,10,16,128]{3,2,1,0:T(8,128)S(1)} %get-tuple-element.34), channel_id=1, source_target_pairs={{0,1},{2,3},{1,0},{3,2},{4,5},{6,7},{5,4},{7,6},{8,9},{10,11},{9,8... | collective-permute-start | bytes 1228808 | tf_op jit(solution)/shard_map/ppermute | solution.py:536
  3.5 22.1 %collective-permute-start.1 = (f32[5,10,16,128]{3,2,1,0:T(8,128)S(1)}, f32[5,10,16,128]{3,2,1,0:T(8,128)S(1)}, u32[]{:S(2)}, u32[]{:S(2)}) collective-permute-start(f32[5,10,16,128]{3,2,1,0:T(8,128)S(1)} %get-tuple-element.35), channel_id=1, source_target_pairs={{1,2},{2,1},{5,6},{6,5},{9,10},{10,9},{13,14},{14,13},{17,18},{18,... | collective-permute-start | bytes 1228808 | tf_op jit(solution)/shard_map/ppermute | solution.py:537
  4.3 21.3 %collective-permute-start.2 = (f32[400,128]{1,0:T(8,128)S(1)}, f32[400,128]{1,0:T(8,128)S(1)}, u32[]{:S(2)}, u32[]{:S(2)}) collective-permute-start(f32[400,128]{1,0:T(8,128)S(1)} %get-tuple-element.36), channel_id=1, source_target_pairs={{4,8},{12,16},{20,24},{8,4},{16,12},{24,20},{5,9},{13,17},{21,25},... | collective-permute-start | bytes 614408 | tf_op jit(solution)/shard_map/ppermute | solution.py:549
  7.1 6.3 %collective-permute-start.4 = (f32[1,5,8,128]{3,2,1,0:T(8,128)S(1)}, f32[1,5,8,128]{3,2,1,0:T(8,128)S(1)}, u32[]{:S(2)}, u32[]{:S(2)}) collective-permute-start(f32[1,5,8,128]{3,2,1,0:T(8,128)S(1)} %get-tuple-element.39), channel_id=1, source_target_pairs={{0,1},{1,0},{2,3},{3,2},{4,5},{5,4},{6,7},{7,6},{8,9},{9,8},{10,11... | collective-permute-start | bytes 61448 | tf_op jit(solution)/shard_map/ppermute | solution.py:542
  13.4 5.5 %collective-permute-start.5 = (f32[2,5,8,128]{3,2,1,0:T(8,128)S(1)}, f32[2,5,8,128]{3,2,1,0:T(8,128)S(1)}, u32[]{:S(2)}, u32[]{:S(2)}) collective-permute-start(f32[2,5,8,128]{3,2,1,0:T(8,128)S(1)} %shard_map.79), channel_id=1, source_target_pairs={{0,2},{1,3},{2,0},{3,1},{4,6},{5,7},{6,4},{7,5},{8,10},{9,11},{10,... | collective-permute-start | bytes 122888 | tf_op jit(solution)/shard_map/ppermute | solution.py:555
  16.2 7.8 %collective-permute-start.3 = (f32[112,128]{1,0:T(8,128)S(1)}, f32[112,128]{1,0:T(8,128)S(1)}, u32[]{:S(2)}, u32[]{:S(2)}) collective-permute-start(f32[112,128]{1,0:T(8,128)S(1)} %get-tuple-element.37), channel_id=1, source_target_pairs={{4,9},{5,8},{6,11},{7,10},{12,17},{13,16},{14,19},{15,18},{20,25},... | collective-permute-start | bytes 172040 | tf_op jit(solution)/shard_map/ppermute | solution.py:550
  18.9 6.7 %collective-permute-start.6 = (f32[112,128]{1,0:T(8,128)S(1)}, f32[112,128]{1,0:T(8,128)S(1)}, u32[]{:S(2)}, u32[]{:S(2)}) collective-permute-start(f32[112,128]{1,0:T(8,128)S(1)} %get-tuple-element.40), channel_id=1, source_target_pairs={{4,8},{5,10},{6,9},{7,11},{12,16},{13,18},{14,17},{15,19},{20,24},... | collective-permute-start | bytes 172040 | tf_op jit(solution)/shard_map/ppermute | solution.py:565
  25.8 2.0 %collective-permute-start.7 = (f32[616,128]{1,0:T(8,128)S(1)}, f32[616,128]{1,0:T(8,128)S(1)}, u32[]{:S(2)}, u32[]{:S(2)}) collective-permute-start(f32[616,128]{1,0:T(8,128)S(1)} %get-tuple-element.45), channel_id=1, source_target_pairs={{0,4},{8,12},{16,20},{24,28},{4,0},{12,8},{20,16},{28,24},{1,5},{9... | collective-permute-start | bytes 946184 | tf_op jit(solution)/shard_map/ppermute | solution.py:588
  30.0 10.4 %collective-permute-start.8 = (f32[5,8,128]{2,1,0:T(8,128)S(1)}, f32[5,8,128]{2,1,0:T(8,128)S(1)}, u32[]{:S(2)}, u32[]{:S(2)}) collective-permute-start(f32[5,8,128]{2,1,0:T(8,128)S(1)} %get-tuple-element.55), channel_id=1, source_target_pairs={{0,1},{3,2},{4,5},{7,6},{8,9},{11,10},{12,13},{15,14},{16,17},{19,... | collective-permute-start | bytes 61448 | tf_op jit(solution)/shard_map/ppermute | solution.py:608
  31.4 9.1 %collective-permute-start.9 = (f32[5,8,128]{2,1,0:T(8,128)S(1)}, f32[5,8,128]{2,1,0:T(8,128)S(1)}, u32[]{:S(2)}, u32[]{:S(2)}) collective-permute-start(f32[5,8,128]{2,1,0:T(8,128)S(1)} %get-tuple-element.56), channel_id=1, source_target_pairs={{0,2},{3,1},{4,6},{7,5},{8,10},{11,9},{12,14},{15,13},{16,18},{19,... | collective-permute-start | bytes 61448 | tf_op jit(solution)/shard_map/ppermute | solution.py:608
  33.7 7.5 %collective-permute-start.10 = (f32[5,8,128]{2,1,0:T(8,128)S(1)}, f32[5,8,128]{2,1,0:T(8,128)S(1)}, u32[]{:S(2)}, u32[]{:S(2)}) collective-permute-start(f32[5,8,128]{2,1,0:T(8,128)S(1)} %get-tuple-element.57), channel_id=1, source_target_pairs={{0,3},{3,0},{4,7},{7,4},{8,11},{11,8},{12,15},{15,12},{16,19},{19,... | collective-permute-start | bytes 61448 | tf_op jit(solution)/shard_map/ppermute | solution.py:608

commit v3 on v2

--- a/solution.py
+++ b/solution.py
@@ -7,6 +7,7 @@
 from jax.experimental import pallas as pl
 from jax.experimental.pallas import tpu as pltpu
 from jax.sharding import PartitionSpec as P
+
 
 NT = 96
 
@@ -31,8 +32,8 @@
 HBM = pl.BlockSpec(memory_space=pltpu.MemorySpace.HBM)
 
 
-def call(body, outs, *args, scratch=(), aliases=None, in_specs=None, out_specs=None, cost=0, limit=8):
-    outs = [jax.ShapeDtypeStruct(shape, F32) for shape in outs]
+def call(body, outs, *args, scratch=(), aliases=None, in_specs=None, out_specs=None, types=None, cost=0, limit=8):
+    outs = [jax.ShapeDtypeStruct(shape, kind) for shape, kind in zip(outs, types or [F32] * len(outs))]
     moved = 4 * sum(math.prod(a.shape) for a in list(args) + outs)
     return pl.pallas_call(
         body,
@@ -54,18 +55,8 @@
     return (2.0 / physical_step) * flow - (0.5 / physical_step) * prior
 
 
-def start_block(flow_hbm, prior_hbm, state_ref, source_ref, first_ref, second_ref, prior_ref, sems):
-    cells, rows = flow_hbm.shape[1:3]
+def pack_pitch(cells, rows, state_ref, prior_ref, source_ref, first_ref, second_ref):
     own_rows = slice(PAD, PAD + rows)
-    flow_ref = state_ref.at[:, pl.ds(HF, cells), pl.ds(PAD, rows)]
-    copies = [
-        pltpu.make_async_copy(flow_hbm, flow_ref, sems.at[0]),
-        pltpu.make_async_copy(prior_hbm, prior_ref, sems.at[1]),
-    ]
-    for copy in copies:
-        copy.start()
-    for copy in copies:
-        copy.wait()
     even = is_even("pitch")
     source_ref[:, HP : HP + cells, own_rows] = source_of(
         state_ref[:, HF : HF + cells, own_rows], prior_ref[...]
@@ -116,7 +107,27 @@
     return jnp.where(lax.axis_index("pitch") % (2 << step) == 1 << step, 0, 1)
 
 
-def rebuild_shares(store_ref, times_ref, active_ref, share_ref, send_ref):
+def rebuild_shares(*refs):
+    store_hbm, times_hbm, active_hbm, flow_hbm, prior_hbm = refs[:5]
+    store_ref, times_ref, active_ref, state_ref, prior_ref, share_ref, send_ref, sems = refs[5:]
+    cells, rows = flow_hbm.shape[1:3]
+    copies = [
+        pltpu.make_async_copy(from_ref, to_ref, sems.at[i])
+        for i, (from_ref, to_ref) in enumerate(
+            (
+                (times_hbm, times_ref),
+                (active_hbm, active_ref),
+                (store_hbm.at[0], store_ref.at[0]),
+                (store_hbm.at[1], store_ref.at[1]),
+                (flow_hbm, state_ref.at[:, pl.ds(HF, cells), pl.ds(PAD, rows)]),
+                (prior_hbm, prior_ref),
+            )
+        )
+    ]
+    for copy in copies:
+        copy.start()
+    copies[0].wait()
+    copies[1].wait()
     harm_count = (store_ref.shape[1] - 1) // 2
     signals = store_ref.shape[2]
     active = doubled(active_ref[...])
@@ -124,6 +135,7 @@
         angle = doubled(times_ref[which]).astype(F32) * period
         angle = angle - phase_lag if which == 0 else angle + phase_lag
         cos_1, sin_1 = jnp.cos(angle), jnp.sin(angle)
+        copies[2 + which].wait()
         cos_k, sin_k = cos_1, sin_1
         totals = [store_ref[which, 0, v] for v in range(signals)]
         for k in range(1, harm_count + 1):
@@ -137,6 +149,8 @@
         for v in range(signals):
             share_ref[which, v] = totals[v]
     send_ref[0] = share_ref[share_sent(0)]
+    copies[4].wait()
+    copies[5].wait()
 
 
 def join_shares(step, share_ref, *refs):
@@ -403,8 +417,8 @@
 
 def start_sections(cells, rows, slabs, blocks, *refs):
     got_ref = refs[2]
-    state_ref, source_ref, mid_1, mid_2, new_ref, own_ref = refs[3:9]
-    send_refs, flux_refs = refs[9 : 8 + slabs], refs[8 + slabs :]
+    state_ref, source_ref, mid_1, mid_2, new_ref, kept_ref, sent_ref = refs[3:10]
+    flux_refs = refs[10:]
     block = Block(cells, rows, slabs, blocks, state_ref, source_ref, flux_refs)
     variables = state_ref.shape[0]
     parts, _ = edge_layout(variables, cells, HF)
@@ -435,10 +449,11 @@
 
         @pl.when(block.pitch_at == end)
         def _():
-            for j, out_ref in enumerate((own_ref,) + tuple(send_refs)):
+            for j in range(slabs):
+                out_ref, i = (kept_ref, j) if 2 * j < slabs else (sent_ref, j - slabs // 2)
                 at = (end ^ j) * part
                 for layer in range(2):
-                    out_ref[:, layer * part : (layer + 1) * part] = new_ref[
+                    out_ref[i, :, layer * part : (layer + 1) * part] = new_ref[
                         :, plane + layer, at : at + part
                     ]
 
@@ -458,12 +473,36 @@
         block.advance(step, from_ref, to_ref, lo, hi)
 
 
-def close(chunks, *refs):
-    new_ref, store_ref, table_ref, base_ref, gain_ref, own_ref = refs[:6]
-    got_refs = refs[6:-5]
-    state_hbm, out_ref, ghost_ref, fresh_ref, sems = refs[-5:]
-    slabs = len(got_refs) + 1
-    at = lax.axis_index("pitch")
+def pass_on(step, held_ref, got_ref, after_ref, kept_ref, sent_ref):
+    del after_ref
+    at = lax.axis_index("pitch") % (2 << step)
+    half = kept_ref.shape[0]
+    got = (at == 1 << step) | (at == (1 << step) - 1)
+
+    @pl.when(got)
+    def _():
+        kept_ref[...] = got_ref[:half]
+        sent_ref[...] = got_ref[half:]
+
+    @pl.when(jnp.logical_not(got))
+    def _():
+        kept_ref[...] = held_ref[:half]
+        sent_ref[...] = held_ref[half:]
+
+
+def refresh_half(pieces, which, sample_ref, store_ref, table_ref, fresh_ref, out_ref, send):
+    keep = 1.0 - relax_rate
+    sample = [sample_ref[0, v] for v in range(store_ref.shape[2])]
+    for lo, hi in zip(pieces[:-1], pieces[1:]):
+        for k in range(lo, hi):
+            weight = relax_rate if k == 0 else table_ref[which, k - 1]
+            for v, value in enumerate(sample):
+                fresh_ref[k, v] = keep * store_ref[which, k, v] + weight * value
+        window = pl.ds(lo, hi - lo)
+        send(fresh_ref.at[window], out_ref.at[which, window])
+
+
+def sender(sems):
     copies = []
 
     def send(from_ref, to_ref):
@@ -471,23 +510,28 @@
         copy.start()
         copies.append(copy)
 
+    return copies, send
+
+
+def close_first(pieces, new_ref, store_ref, table_ref, sample_ref, state_hbm, out_ref, fresh_ref, sems):
+    copies, send = sender(sems)
     send(new_ref, state_hbm)
-    top, bottom = own_ref[...], own_ref[...]
-    for j in range(1, slabs):
-        got = got_refs[j - 1][...]
-        top = jnp.where(at == slabs - 1 - j, got, top)
-        bottom = jnp.where(at == j, got, bottom)
-    keep = 1.0 - relax_rate
-    signals = store_ref.shape[2]
-    for which, sample in enumerate((top, bottom)):
-        for lo, hi in zip(chunks[:-1], chunks[1:]):
-            for k in range(lo, hi):
-                weight = relax_rate if k == 0 else table_ref[which, k - 1]
-                for v in range(signals):
-                    fresh_ref[which, k, v] = keep * store_ref[which, k, v] + weight * sample[v]
-            window = pl.ds(lo, hi - lo)
-            send(fresh_ref.at[which, window], out_ref.at[which, window])
-        ghost_ref[which] = base_ref[which] + sample * gain_ref[...][None]
+    which = 1 - lax.axis_index("pitch") % 2
+    refresh_half(pieces, which, sample_ref, store_ref, table_ref, fresh_ref, out_ref, send)
+    for copy in copies:
+        copy.wait()
+
+
+def close_second(pieces, *refs):
+    store_ref, table_ref, base_ref, gain_ref, first_ref, second_ref = refs[1:7]
+    out_ref, ghost_hbm, fresh_ref, ghost_ref, sems = refs[7:]
+    copies, send = sender(sems)
+    which = lax.axis_index("pitch") % 2
+    gain = gain_ref[...]
+    for at, sample_ref in ((1 - which, first_ref), (which, second_ref)):
+        ghost_ref[at] = base_ref[at] + sample_ref[0] * gain[None]
+    send(ghost_ref, ghost_hbm)
+    refresh_half(pieces, which, second_ref, store_ref, table_ref, fresh_ref, out_ref, send)
     for copy in copies:
         copy.wait()
 
@@ -524,36 +568,36 @@
     source_shape = (variables, cells + 2 * HP, long_rows, lanes)
     corner = (corner_layout(variables)[1], lanes)
 
-    state, source, first, second = call(
-        start_block,
-        [state_shape, source_shape, halo, halo],
-        pltpu.with_memory_space_constraint(flow_state, pltpu.MemorySpace.HBM),
-        pltpu.with_memory_space_constraint(prior_state, pltpu.MemorySpace.HBM),
-        scratch=[pltpu.VMEM(flow_state.shape, F32), pltpu.SemaphoreType.DMA((2,))],
-        in_specs=[HBM, HBM],
-        cost=1,
+    inputs = (store, sample_times, harmonics, flow_state, prior_state)
+    shapes = [store.shape, sample_times.shape, harmonics.shape, state_shape, flow_state.shape]
+    store, times, active, state, prior, share, send = call(
+        rebuild_shares,
+        shapes + [(2,) + face, (1,) + face],
+        *[pltpu.with_memory_space_constraint(a, pltpu.MemorySpace.HBM) for a in inputs],
+        types=(F32, jnp.int32, jnp.int32, F32, F32, F32, F32),
+        scratch=[pltpu.SemaphoreType.DMA((len(inputs) + 1,))],
+        in_specs=[HBM] * len(inputs),
+    )
+    gathered, step = [lax.ppermute(send, "pitch", flip_pairs(slabs, 1))], 1
+    source, first, second = call(
+        functools.partial(pack_pitch, cells, rows), [source_shape, halo, halo], state, prior
     )
     first = lax.ppermute(first, "pitch", swap_pairs(slabs, 0))
-    second = lax.ppermute(second, "pitch", swap_pairs(slabs, 1))
-
-    share, send = call(
-        rebuild_shares, [(2,) + face, (1,) + face], store, sample_times, harmonics
-    )
-    gathered, step = [lax.ppermute(send, "pitch", flip_pairs(slabs, 1))], 1
-    edge, corner_1 = call(
-        functools.partial(pack_axial, cells, rows),
-        [(edge_layout(variables, cells, 0)[1], lanes), corner],
-        state,
-        source,
-    )
-    edge = lax.ppermute(edge, "blk", swap_pairs(blocks, 1))
-    corner_1 = lax.ppermute(corner_1, ("blk", "pitch"), diagonal_pairs(slabs, blocks, 0))
     while 1 << step < slabs:
         [send] = call(
             functools.partial(join_shares, step), [(1 << step,) + face], share, *gathered
         )
         gathered.append(lax.ppermute(send, "pitch", flip_pairs(slabs, 1 << step)))
         step += 1
+    second = lax.ppermute(second, "pitch", swap_pairs(slabs, 1))
+    edge, corner_1 = call(
+        functools.partial(pack_axial, cells, rows),
+        [(edge_layout(variables, cells, 0)[1], lanes), corner],
+        state,
+        source,
+    )
+    edge = lax.ppermute(edge, "blk", swap_pairs(blocks, 1))
+    corner_1 = lax.ppermute(corner_1, ("blk", "pitch"), diagonal_pairs(slabs, blocks, 0))
     ghost, corner_2 = call(
         functools.partial(join_ghosts, cells, rows, slabs),
         [(variables, 2, rows, lanes), corner],
@@ -567,8 +611,8 @@
         prepare_close,
         [(2, orders - 1, 2 * part, lanes), (2,) + face, (2 * part, lanes)],
         store,
-        sample_times,
-        harmonics,
+        times,
+        active,
     )
 
     state, source, out = call(
@@ -593,9 +637,10 @@
     flux_shape = (variables - 1, cells + 2 * HP + 2, long_rows, lanes)
     flux_scratch = [pltpu.VMEM(flux_shape, F32)] * 3
     sizes = (cells, rows, slabs, blocks)
-    state, source, mid_1, mid_2, new, own, *sends = call(
+    half_faces = (slabs // 2,) + face
+    state, source, mid_1, mid_2, new, held, send = call(
         functools.partial(start_sections, *sizes),
-        [state_shape, source_shape] + mid_shapes + [flow_state.shape] + [face] * slabs,
+        [state_shape, source_shape] + mid_shapes + [flow_state.shape, half_faces, half_faces],
         state,
         source,
         got,
@@ -603,11 +648,12 @@
         aliases={0: 0, 1: 1},
         limit=12,
     )
-    samples = [None] * (slabs - 1)
-    for j in range(slabs - 1, 0, -1):
-        samples[j - 1] = lax.ppermute(
-            sends[j - 1], "pitch", [(0, j), (slabs - 1, slabs - 1 - j)]
-        )
+    step = slabs.bit_length() - 2
+    spread = []
+    if step > 0:
+        low = [(i, i + (1 << step)) for i in range(0, slabs, 2 << step)]
+        pairs = low + [(slabs - 1 - i, slabs - 1 - j) for i, j in low]
+        spread.append(lax.ppermute(send, "pitch", pairs))
     _, _, new = call(
         functools.partial(finish_sections, *sizes),
         mid_shapes + [flow_state.shape],
@@ -620,20 +666,44 @@
         aliases={2: 0, 3: 1, 4: 2},
         limit=12,
     )
-    pieces = 7
-    chunks = [orders * i // pieces for i in range(pieces + 1)]
-    new_state, new_store, new_ghosts = call(
-        functools.partial(close, chunks),
-        [flow_state.shape, store.shape, (2,) + face],
+    while step > 0:
+        half_faces = (held.shape[0] // 2,) + face
+        held, send = call(
+            functools.partial(pass_on, step), [half_faces, half_faces], held, spread[-1], new
+        )
+        step -= 1
+        if step > 0:
+            low = [(i, i + (1 << step)) for i in range(0, slabs, 2 << step)]
+            pairs = low + [(slabs - 1 - i, slabs - 1 - j) for i, j in low]
+            spread.append(lax.ppermute(send, "pitch", pairs))
+    second_sample = lax.ppermute(send, "pitch", flip_pairs(slabs, 1))
+    parts = 4
+    pieces = [orders * i // parts for i in range(parts + 1)]
+    half_store = pltpu.VMEM(store.shape[1:], F32)
+    new_state, new_store = call(
+        functools.partial(close_first, pieces),
+        [flow_state.shape, store.shape],
         new,
+        store,
+        table,
+        held,
+        scratch=[half_store, pltpu.SemaphoreType.DMA((parts + 1,))],
+        out_specs=[HBM, HBM],
+    )
+    new_store, new_ghosts = call(
+        functools.partial(close_second, pieces),
+        [store.shape, (2,) + face],
+        new_store,
         store,
         table,
         base,
         gain,
-        own,
-        *samples,
-        scratch=[pltpu.VMEM(store.shape, F32), pltpu.SemaphoreType.DMA((2 * pieces + 1,))],
-        out_specs=[HBM, HBM, VMEM],
+        held,
+        second_sample,
+        scratch=[half_store, pltpu.VMEM((2,) + face, F32), pltpu.SemaphoreType.DMA((parts + 1,))],
+        in_specs=[HBM] + [VMEM] * 6,
+        out_specs=[HBM, HBM],
+        aliases={0: 0},
     )
     return (
         new_state,

time: 44.1 us -> 42.2 us (0.957)
  the two profiles are of different devices: /device:TPU:4 before, /device:TPU:0 now
where the time goes in v3:
time: 42.2 us; the launch traced here: 41.9 us
  starting transfers between devices  23.8 us (56%)
  Pallas kernels  10.2 us (24%)
  waiting for transfers between devices  7.14 us (17%)
  between operations  0.79 us (2%)
    pallas_call x12, Pallas kernels, call(): pl.pallas_call(body, out_shape=outs, in_specs=in_specs or [VMEM] * len(ar...  10.2 us
    ppermute x1, starting transfers between devices, shards(): got = lax.ppermute(out, 'blk', swap_pairs(blocks, 0))  7.07 us
    ppermute x1, starting transfers between devices, shards(): gathered, step = ([lax.ppermute(send, 'pitch', flip_pairs(slabs, 1))], 1)  4.44 us
    ppermute x1, waiting for transfers between devices, shards(): gathered, step = ([lax.ppermute(send, 'pitch', flip_pairs(slabs, 1))], 1)  3.87 us
    ppermute x1, starting transfers between devices, shards(): first = lax.ppermute(first, 'pitch', swap_pairs(slabs, 0))  3.12 us
    ppermute x1, starting transfers between devices, shards(): gathered.append(lax.ppermute(send, 'pitch', flip_pairs(slabs, 1 << step)))  2.88 us
    ppermute x1, starting transfers between devices, shards(): second_sample = lax.ppermute(send, 'pitch', flip_pairs(slabs, 1))  2.32 us
    ppermute x1, waiting for transfers between devices, shards(): gathered.append(lax.ppermute(send, 'pitch', flip_pairs(slabs, 1 << step)))  1.36 us
  transfers between devices with their start and end apart: 10, of which 4 were waited for; matrix products, arithmetic and copies ran while one was open for 0% of the time, Pallas kernels for 11%

profile of v3, /device:TPU:0, one launch (start us, length us, event | category | flops | bytes accessed | tf_op | source)
XLA Modules:
  0.0 41.9 jit_solution(5543436883596551437)
XLA Ops:
  0.6 1.8 %shard_map.76 = (f32[2,49,5,8,128]{4,3,2,1,0:T(8,128)S(1)}, s32[2,4,128]{2,1,0:T(4,128)S(1)}, s32[4,128]{1,0:T(4,128)S(1)}, f32[5,20,32,128]{3,2,1,0:T(8,128)S(1...) custom-call(f32[2,49,5,8,128]{4,3,2,1,0:T(8,128)} %bitcast.3, ...), custom_call_target="tpu_custom_call" | custom-call | bytes 6709248 | tf_op jit(solution)/shard_map/pallas_call | solution.py:38
  2.4 0.1 shard_map.77
  2.5 3.1 %collective-permute-start = (f32[5,10,16,128]{3,2,1,0:T(8,128)S(1)}, f32[5,10,16,128]{3,2,1,0:T(8,128)S(1)}, u32[]{:S(2)}, u32[]{:S(2)}) collective-permute-start(f32[5,10,16,128]{3,2,1,0:T(8,128)S(1)} %get-tuple-element.40), channel_id=1, source_target_pairs={{0,1},{2,3},{1,0},{3,2},{4,5},{6,7},{5,4},{7,6},{8,9},{10,11},{9,8... | collective-permute-start | bytes 1228808 | tf_op jit(solution)/shard_map/ppermute | solution.py:585
  5.6 0.7 %collective-permute-start.1 = (f32[5,10,16,128]{3,2,1,0:T(8,128)S(1)}, f32[5,10,16,128]{3,2,1,0:T(8,128)S(1)}, u32[]{:S(2)}, u32[]{:S(2)}) collective-permute-start(f32[5,10,16,128]{3,2,1,0:T(8,128)S(1)} %get-tuple-element.41), channel_id=1, source_target_pairs={{1,2},{2,1},{5,6},{6,5},{9,10},{10,9},{13,14},{14,13},{17,18},{18,... | collective-permute-start | bytes 1228808 | tf_op jit(solution)/shard_map/ppermute | solution.py:592
  6.3 0.1 shard_map.78
  6.4 0.7 %collective-permute-start.2 = (f32[400,128]{1,0:T(8,128)S(1)}, f32[400,128]{1,0:T(8,128)S(1)}, u32[]{:S(2)}, u32[]{:S(2)}) collective-permute-start(f32[400,128]{1,0:T(8,128)S(1)} %get-tuple-element.42), channel_id=1, source_target_pairs={{4,8},{12,16},{20,24},{8,4},{16,12},{24,20},{5,9},{13,17},{21,25},... | collective-permute-start | bytes 614408 | tf_op jit(solution)/shard_map/ppermute | solution.py:599
  7.1 4.4 %collective-permute-start.4 = (f32[1,5,8,128]{3,2,1,0:T(8,128)S(1)}, f32[1,5,8,128]{3,2,1,0:T(8,128)S(1)}, u32[]{:S(2)}, u32[]{:S(2)}) collective-permute-start(f32[1,5,8,128]{3,2,1,0:T(8,128)S(1)} %get-tuple-element.45), channel_id=1, source_target_pairs={{0,1},{1,0},{2,3},{3,2},{4,5},{5,4},{6,7},{7,6},{8,9},{9,8},{10,11... | collective-permute-start | bytes 61448 | tf_op jit(solution)/shard_map/ppermute | solution.py:581
  11.5 3.9 %collective-permute-done.4.refs_0_ = f32[1,5,8,128]{3,2,1,0:T(8,128)S(1)} collective-permute-done((f32[1,5,8,128]{3,2,1,0:T(8,128)S(1)}, f32[1,5,8,128]{3,2,1,0:T(8,128)S(1)}, u32[]{:S(2)}, u32[]{:S(2)}) %collective-permute-start.4) | collective-permute-done | bytes 20512 | tf_op jit(solution)/shard_map/ppermute | solution.py:581
  15.4 2.9 %collective-permute-start.5 = (f32[2,5,8,128]{3,2,1,0:T(8,128)S(1)}, f32[2,5,8,128]{3,2,1,0:T(8,128)S(1)}, u32[]{:S(2)}, u32[]{:S(2)}) collective-permute-start(f32[2,5,8,128]{3,2,1,0:T(8,128)S(1)} %shard_map.79), channel_id=1, source_target_pairs={{0,2},{1,3},{2,0},{3,1},{4,6},{5,7},{6,4},{7,5},{8,10},{9,11},{10,... | collective-permute-start | bytes 122888 | tf_op jit(solution)/shard_map/ppermute | solution.py:590
  18.3 0.7 %collective-permute-start.3 = (f32[112,128]{1,0:T(8,128)S(1)}, f32[112,128]{1,0:T(8,128)S(1)}, u32[]{:S(2)}, u32[]{:S(2)}) collective-permute-start(f32[112,128]{1,0:T(8,128)S(1)} %get-tuple-element.43), channel_id=1, source_target_pairs={{4,9},{5,8},{6,11},{7,10},{12,17},{13,16},{14,19},{15,18},{20,25},... | collective-permute-start | bytes 172040 | tf_op jit(solution)/shard_map/ppermute | solution.py:600
  19.0 1.4 %collective-permute-done.5.refs_1_ = f32[2,5,8,128]{3,2,1,0:T(8,128)S(1)} collective-permute-done((f32[2,5,8,128]{3,2,1,0:T(8,128)S(1)}, f32[2,5,8,128]{3,2,1,0:T(8,128)S(1)}, u32[]{:S(2)}, u32[]{:S(2)}) %collective-permute-start.5) | collective-permute-done | bytes 40992 | tf_op jit(solution)/shard_map/ppermute | solution.py:590
  20.4 0.7 %collective-permute-start.6 = (f32[112,128]{1,0:T(8,128)S(1)}, f32[112,128]{1,0:T(8,128)S(1)}, u32[]{:S(2)}, u32[]{:S(2)}) collective-permute-start(f32[112,128]{1,0:T(8,128)S(1)} %get-tuple-element.46), channel_id=1, source_target_pairs={{4,8},{5,10},{6,9},{7,11},{12,16},{13,18},{14,17},{15,19},{20,24},... | collective-permute-start | bytes 172040 | tf_op jit(solution)/shard_map/ppermute | solution.py:609
  21.0 0.3 shard_map.81
  21.3 0.0 collective-permute-done.3.refs_5_
  21.3 0.0 collective-permute-done.6.refs_6_
  21.4 0.0 collective-permute-done.2.refs_4_
  21.4 0.0 collective-permute-done.refs_2_
  21.4 0.0 collective-permute-done.1.refs_3_
  21.4 0.2 shard_map.82
  21.6 7.1 %collective-permute-start.7 = (f32[616,128]{1,0:T(8,128)S(1)}, f32[616,128]{1,0:T(8,128)S(1)}, u32[]{:S(2)}, u32[]{:S(2)}) collective-permute-start(f32[616,128]{1,0:T(8,128)S(1)} %get-tuple-element.54), channel_id=1, source_target_pairs={{0,4},{8,12},{16,20},{24,28},{4,0},{12,8},{20,16},{28,24},{1,5},{9... | collective-permute-start | bytes 946184 | tf_op jit(solution)/shard_map/ppermute | solution.py:632
  28.7 1.2 %collective-permute-done.7.refs_2_ = f32[616,128]{1,0:T(8,128)S(1)} collective-permute-done((f32[616,128]{1,0:T(8,128)S(1)}, f32[616,128]{1,0:T(8,128)S(1)}, u32[]{:S(2)}, u32[]{:S(2)}) %collective-permute-start.7) | collective-permute-done | bytes 315424 | tf_op jit(solution)/shard_map/ppermute | solution.py:632
  29.9 2.4 %shard_map.83 = (f32[5,20,32,128]{3,2,1,0:T(8,128)S(1)}, f32[5,16,32,128]{3,2,1,0:T(8,128)S(1)}, f32[5,16,32,128]{3,2,1,0:T(8,128)S(1)}, f32[5,12,32,128]{3,2,1,...) custom-call(f32[5,20,32,128]{3,2,1,0:T(8,128)S(1)} %get-tuple-elemen, ...), custom_call_target="tpu_custom_call", output_to_operand_aliasing={{0}: (0, {}), {1}: (1, {})} | custom-call | bytes 8916992 | tf_op jit(solution)/shard_map/pallas_call | solution.py:38
  32.3 1.3 %collective-permute-start.8 = (f32[2,5,8,128]{3,2,1,0:T(8,128)S(1)}, f32[2,5,8,128]{3,2,1,0:T(8,128)S(1)}, u32[]{:S(2)}, u32[]{:S(2)}) collective-permute-start(f32[2,5,8,128]{3,2,1,0:T(8,128)S(1)} %get-tuple-element.63), channel_id=1, source_target_pairs={{0,2},{3,1},{4,6},{7,5},{8,10},{11,9},{12,14},{15,13},{16,18},{19,... | collective-permute-start | bytes 122888 | tf_op jit(solution)/shard_map/ppermute | solution.py:656
  33.6 3.1 %shard_map.84 = (f32[5,16,32,128]{3,2,1,0:T(8,128)S(1)}, f32[5,12,32,128]{3,2,1,0:T(8,128)S(1)}, f32[5,8,16,128]{3,2,1,0:T(8,128)S(1)}) custom-call(f32[5,20,32,128]{3,2,1,0:T(8,128)S(1)} %get-tuple-element.55.refs_0_, f32[5,16,32,128]{3,2,1,0:T(8,128)S(1)} %get-tuple-element.56.refs_1_, ...), custom_call_target="tpu_custom_call", output_to_operand_aliasing={{0}: (2, {}), {1}: (3, {}), {2}: (4, {})} | custom-call | bytes 8192000 | tf_op jit(solution)/shard_map/pallas_call | solution.py:38
  36.8 0.0 collective-permute-done.8.got_ref
  36.8 2.3 %collective-permute-start.9 = (f32[1,5,8,128]{3,2,1,0:T(8,128)S(1)}, f32[1,5,8,128]{3,2,1,0:T(8,128)S(1)}, u32[]{:S(2)}, u32[]{:S(2)}) collective-permute-start(f32[1,5,8,128]{3,2,1,0:T(8,128)S(1)} %get-tuple-element.68), channel_id=1, source_target_pairs={{0,1},{1,0},{2,3},{3,2},{4,5},{5,4},{6,7},{7,6},{8,9},{9,8},{10,11... | collective-permute-start | bytes 61448 | tf_op jit(solution)/shard_map/ppermute | solution.py:679
  39.1 1.1 %shard_map.86 = (f32[5,8,16,128]{3,2,1,0:T(8,128)}, f32[2,49,5,8,128]{4,3,2,1,0:T(8,128)}) custom-call(f32[5,8,16,128]{3,2,1,0:T(8,128)S(1)} %get-tuple-element.60.after_ref.new_ref, f32[2,49,5,8,128]{4,3,2,1,0:T(8,128)S(1)} %get-tuple-element.48.store_ref.refs_1_, f32[2,48,8,128]{3,2,1,0:T(8,128)S(1)} %get-tuple-element.61.table_ref.refs_2_, ...), custom_call_target="tpu_custom_call" | custom-call | bytes 5083136 | tf_op jit(solution)/shard_map/pallas_call | solution.py:38
  40.2 0.7 %collective-permute-done.9.refs_6_ = f32[1,5,8,128]{3,2,1,0:T(8,128)S(1)} collective-permute-done((f32[1,5,8,128]{3,2,1,0:T(8,128)S(1)}, f32[1,5,8,128]{3,2,1,0:T(8,128)S(1)}, u32[]{:S(2)}, u32[]{:S(2)}) %collective-permute-start.9) | collective-permute-done | bytes 20512 | tf_op jit(solution)/shard_map/ppermute | solution.py:679
  40.9 1.0 %shard_map.87 = (f32[2,49,5,8,128]{4,3,2,1,0:T(8,128)}, f32[2,5,8,128]{3,2,1,0:T(8,128)}) custom-call(f32[2,49,5,8,128]{4,3,2,1,0:T(8,128)} %get-tuple-element.66.refs_0_, f32[2,49,5,8,128]{4,3,2,1,0:T(8,128)S(1)} %get-tuple-element.48.store_ref.refs_1_, f32[2,48,8,128]{3,2,1,0:T(8,128)S(1)} %get-tuple-element.61.table_ref.refs_2_, ...), custom_call_target="tpu_custom_call", output_to_operand_aliasing={{0}: (0, {})} | custom-call | bytes 6541312 | tf_op jit(solution)/shard_map/pallas_call | solution.py:38
  (3 shorter events, 0.1 us)
Async XLA Ops:
  2.5 18.8 %collective-permute-start = (f32[5,10,16,128]{3,2,1,0:T(8,128)S(1)}, f32[5,10,16,128]{3,2,1,0:T(8,128)S(1)}, u32[]{:S(2)}, u32[]{:S(2)}) collective-permute-start(f32[5,10,16,128]{3,2,1,0:T(8,128)S(1)} %get-tuple-element.40), channel_id=1, source_target_pairs={{0,1},{2,3},{1,0},{3,2},{4,5},{6,7},{5,4},{7,6},{8,9},{10,11},{9,8... | collective-permute-start | bytes 1228808 | tf_op jit(solution)/shard_map/ppermute | solution.py:585
  5.6 15.7 %collective-permute-start.1 = (f32[5,10,16,128]{3,2,1,0:T(8,128)S(1)}, f32[5,10,16,128]{3,2,1,0:T(8,128)S(1)}, u32[]{:S(2)}, u32[]{:S(2)}) collective-permute-start(f32[5,10,16,128]{3,2,1,0:T(8,128)S(1)} %get-tuple-element.41), channel_id=1, source_target_pairs={{1,2},{2,1},{5,6},{6,5},{9,10},{10,9},{13,14},{14,13},{17,18},{18,... | collective-permute-start | bytes 1228808 | tf_op jit(solution)/shard_map/ppermute | solution.py:592
  6.4 14.9 %collective-permute-start.2 = (f32[400,128]{1,0:T(8,128)S(1)}, f32[400,128]{1,0:T(8,128)S(1)}, u32[]{:S(2)}, u32[]{:S(2)}) collective-permute-start(f32[400,128]{1,0:T(8,128)S(1)} %get-tuple-element.42), channel_id=1, source_target_pairs={{4,8},{12,16},{20,24},{8,4},{16,12},{24,20},{5,9},{13,17},{21,25},... | collective-permute-start | bytes 614408 | tf_op jit(solution)/shard_map/ppermute | solution.py:599
  7.1 8.3 %collective-permute-start.4 = (f32[1,5,8,128]{3,2,1,0:T(8,128)S(1)}, f32[1,5,8,128]{3,2,1,0:T(8,128)S(1)}, u32[]{:S(2)}, u32[]{:S(2)}) collective-permute-start(f32[1,5,8,128]{3,2,1,0:T(8,128)S(1)} %get-tuple-element.45), channel_id=1, source_target_pairs={{0,1},{1,0},{2,3},{3,2},{4,5},{5,4},{6,7},{7,6},{8,9},{9,8},{10,11... | collective-permute-start | bytes 61448 | tf_op jit(solution)/shard_map/ppermute | solution.py:581
  15.4 4.9 %collective-permute-start.5 = (f32[2,5,8,128]{3,2,1,0:T(8,128)S(1)}, f32[2,5,8,128]{3,2,1,0:T(8,128)S(1)}, u32[]{:S(2)}, u32[]{:S(2)}) collective-permute-start(f32[2,5,8,128]{3,2,1,0:T(8,128)S(1)} %shard_map.79), channel_id=1, source_target_pairs={{0,2},{1,3},{2,0},{3,1},{4,6},{5,7},{6,4},{7,5},{8,10},{9,11},{10,... | collective-permute-start | bytes 122888 | tf_op jit(solution)/shard_map/ppermute | solution.py:590
  18.3 3.0 %collective-permute-start.3 = (f32[112,128]{1,0:T(8,128)S(1)}, f32[112,128]{1,0:T(8,128)S(1)}, u32[]{:S(2)}, u32[]{:S(2)}) collective-permute-start(f32[112,128]{1,0:T(8,128)S(1)} %get-tuple-element.43), channel_id=1, source_target_pairs={{4,9},{5,8},{6,11},{7,10},{12,17},{13,16},{14,19},{15,18},{20,25},... | collective-permute-start | bytes 172040 | tf_op jit(solution)/shard_map/ppermute | solution.py:600
  20.4 1.0 %collective-permute-start.6 = (f32[112,128]{1,0:T(8,128)S(1)}, f32[112,128]{1,0:T(8,128)S(1)}, u32[]{:S(2)}, u32[]{:S(2)}) collective-permute-start(f32[112,128]{1,0:T(8,128)S(1)} %get-tuple-element.46), channel_id=1, source_target_pairs={{4,8},{5,10},{6,9},{7,11},{12,16},{13,18},{14,17},{15,19},{20,24},... | collective-permute-start | bytes 172040 | tf_op jit(solution)/shard_map/ppermute | solution.py:609
  21.6 8.3 %collective-permute-start.7 = (f32[616,128]{1,0:T(8,128)S(1)}, f32[616,128]{1,0:T(8,128)S(1)}, u32[]{:S(2)}, u32[]{:S(2)}) collective-permute-start(f32[616,128]{1,0:T(8,128)S(1)} %get-tuple-element.54), channel_id=1, source_target_pairs={{0,4},{8,12},{16,20},{24,28},{4,0},{12,8},{20,16},{28,24},{1,5},{9... | collective-permute-start | bytes 946184 | tf_op jit(solution)/shard_map/ppermute | solution.py:632
  32.3 4.4 %collective-permute-start.8 = (f32[2,5,8,128]{3,2,1,0:T(8,128)S(1)}, f32[2,5,8,128]{3,2,1,0:T(8,128)S(1)}, u32[]{:S(2)}, u32[]{:S(2)}) collective-permute-start(f32[2,5,8,128]{3,2,1,0:T(8,128)S(1)} %get-tuple-element.63), channel_id=1, source_target_pairs={{0,2},{3,1},{4,6},{7,5},{8,10},{11,9},{12,14},{15,13},{16,18},{19,... | collective-permute-start | bytes 122888 | tf_op jit(solution)/shard_map/ppermute | solution.py:656
  36.8 4.1 %collective-permute-start.9 = (f32[1,5,8,128]{3,2,1,0:T(8,128)S(1)}, f32[1,5,8,128]{3,2,1,0:T(8,128)S(1)}, u32[]{:S(2)}, u32[]{:S(2)}) collective-permute-start(f32[1,5,8,128]{3,2,1,0:T(8,128)S(1)} %get-tuple-element.68), channel_id=1, source_target_pairs={{0,1},{1,0},{2,3},{3,2},{4,5},{5,4},{6,7},{7,6},{8,9},{9,8},{10,11... | collective-permute-start | bytes 61448 | tf_op jit(solution)/shard_map/ppermute | solution.py:679

commit v4 on v3

--- a/solution.py
+++ b/solution.py
@@ -68,27 +68,23 @@
         out_ref[:, HF:] = source_ref[:, pl.ds(at, HP), own_rows]
 
 
-def pack_axial(cells, rows, state_ref, source_ref, edge_ref, corner_ref):
+def pack_axial(cells, rows, state_ref, source_ref, edge_1, edge_2, corner_ref):
     refs = (state_ref, source_ref)
     edges, _ = edge_layout(state_ref.shape[0], cells, 0)
-    corners, _ = corner_layout(state_ref.shape[0])
+    sides, _ = side_layout(state_ref.shape[0])
     top = is_even("pitch")
 
     def write(up):
-        for v, which, plane, count, place in edges:
-            edge_ref[place : place + count] = refs[which][v, plane, edge_rows(rows, count, up)]
-        for v, which, depth, count, place in corners:
+        for v, which, depth, count, place in sides:
             width = (HF, HP)[which]
             plane = jnp.where(top, width + cells - depth, width + depth - 1)
             corner_ref[place : place + count] = refs[which][v, plane, edge_rows(rows, count, up)]
-
-    @pl.when(is_even("blk"))
-    def _():
-        write(False)
-
-    @pl.when(jnp.logical_not(is_even("blk")))
-    def _():
-        write(True)
+        for v, which, plane, count, place in edges:
+            edge_1[place : place + count] = refs[which][v, plane, edge_rows(rows, count, not up)]
+            edge_2[place : place + count] = refs[which][v, plane, edge_rows(rows, count, up)]
+
+    pl.when(is_even("blk"))(lambda: write(False))
+    pl.when(jnp.logical_not(is_even("blk")))(lambda: write(True))
 
 
 def edge_rows(rows, count, up):
@@ -162,51 +158,30 @@
         at += got_ref.shape[0]
 
 
-def join_ghosts(cells, rows, slabs, state_ref, source_ref, share_ref, *refs):
-    got_refs, (ghost_ref, corner_ref) = refs[:-2], refs[-2:]
-    refs = (state_ref, source_ref)
-    part = rows // slabs
-    pitch_at = lax.axis_index("pitch")
-    blk_even = is_even("blk")
-    corners, _ = corner_layout(state_ref.shape[0])
-
-    for end in range(2):
-
-        @pl.when(pitch_at == end * (slabs - 1))
-        def _():
-            pieces = [share_ref[end]]
-            for got_ref in got_refs:
-                pieces += [got_ref[i] for i in range(got_ref.shape[0])]
-            for distance, piece in enumerate(pieces):
-                at = part * (distance if end == 0 else slabs - 1 - distance)
-                for layer in range(2):
-                    ghost_ref[:, layer, at : at + part] = piece[:, layer * part : (layer + 1) * part]
-
-            def write(up):
-                for v, which, depth, count, place in corners:
-                    if which == 0 and depth <= 2:
-                        at = slice(rows - count, rows) if up else slice(0, count)
-                        layer = depth - 1 if end else 2 - depth
-                        corner_ref[place : place + count] = ghost_ref[v, layer, at]
-
-            pl.when(blk_even)(lambda: write(False))
-            pl.when(jnp.logical_not(blk_even))(lambda: write(True))
-
-    @pl.when((pitch_at > 0) & (pitch_at < slabs - 1))
-    def _():
-        bottom = is_even("pitch")
-
-        def write(up):
-            for v, which, depth, count, place in corners:
-                width = (HF, HP)[which]
-                plane = jnp.where(bottom, width + depth - 1, width + cells - depth)
-                corner_ref[place : place + count] = refs[which][v, plane, edge_rows(rows, count, up)]
-
-        pl.when(blk_even)(lambda: write(False))
-        pl.when(jnp.logical_not(blk_even))(lambda: write(True))
-
-
-def prepare_close(store_ref, times_ref, active_ref, table_ref, base_ref, gain_ref):
+def radial_band(lanes):
+    shape = (2 * lanes, lanes)
+    source = lax.broadcasted_iota(jnp.int32, shape, 0)
+    target = lax.broadcasted_iota(jnp.int32, shape, 1)
+    fluxes = source >= lanes
+    source = jnp.where(fluxes, source - lanes, source)
+
+    def at(ahead):
+        return source == jnp.clip(target + ahead, 0, lanes - 1)
+
+    def entries(pairs):
+        total = jnp.zeros(shape, F32)
+        for ahead, value in pairs:
+            total = total + jnp.where(at(ahead), value, 0.0)
+        return total
+
+    own = 1.5 / physical_step - 18.0 * diss_coeff
+    state = [(1, 4.0), (-1, 4.0), (2, -1.0), (-2, -1.0), (0, own / diss_coeff)]
+    state = entries([(ahead, diss_coeff * value) for ahead, value in state])
+    return jnp.where(fluxes, entries([(1, 1.0), (-1, -1.0)]), state)
+
+
+def prepare_close(store_ref, times_ref, active_ref, table_ref, base_ref, gain_ref, band_ref):
+    band_ref[...] = radial_band(band_ref.shape[1]).astype(band_ref.dtype)
     harm_count = (store_ref.shape[1] - 1) // 2
     signals = store_ref.shape[2]
     active = doubled(active_ref[...])
@@ -249,7 +224,16 @@
     return parts, -(-place // 8) * 8
 
 
-def corner_layout(variables):
+def corner_layout(variables, cells):
+    parts, place = [], 0
+    for v, which, plane, count, _ in edge_layout(variables, cells, HF)[0]:
+        if not 0 <= plane - (HF, HP)[which] < cells:
+            parts.append((v, which, plane, count, place))
+            place += count
+    return parts, -(-place // 8) * 8
+
+
+def side_layout(variables):
     parts, place = [], 0
     for v in range(variables):
         for which, width in ((0, HF), (1, HP)):
@@ -259,9 +243,33 @@
     return parts, -(-place // 8) * 8
 
 
+def halo_plane(cells, which, depth, upper):
+    width = (HF, HP)[which]
+    return jnp.where(upper, width + cells + depth - 1, width - depth)
+
+
+def place_edges(cells, rows, slabs, blocks, *refs):
+    edge_1, edge_2, band_ref = refs[2:5]
+    state_ref, source_ref, mid_1 = refs[5:8]
+    into = (state_ref, source_ref)
+    edges, _ = edge_layout(state_ref.shape[0], cells, 0)
+
+    def move(up):
+        for v, which, plane, count, place in edges:
+            into[which][v, plane, halo_rows(rows, count, not up)] = edge_1[place : place + count]
+            into[which][v, plane, halo_rows(rows, count, up)] = edge_2[place : place + count]
+
+    pl.when(is_even("blk"))(lambda: move(False))
+    pl.when(jnp.logical_not(is_even("blk")))(lambda: move(True))
+    block = Block(cells, rows, slabs, blocks, state_ref, source_ref, band_ref, refs[8:])
+    block.clamp_ends(state_ref)
+    block.advance(0, state_ref, mid_1, 2, cells - 2)
+
+
 def place_halos(cells, rows, slabs, *refs):
-    first_ref, second_ref, edge_ref, corner_1, corner_2, ghost_ref = refs[2:8]
-    state_ref, source_ref, out_ref = refs[-3:]
+    first_ref, second_ref, share_ref = refs[2:5]
+    got_refs = refs[5:-4]
+    state_ref, source_ref, out_ref, corner_ref = refs[-4:]
     refs = (state_ref, source_ref)
     pitch_at = lax.axis_index("pitch")
     even = is_even("pitch")
@@ -274,37 +282,40 @@
         at = jnp.where(upper, HP + cells, 0)
         source_ref[:, pl.ds(at, HP), own_rows] = halo_ref[:, HF:]
 
-    @pl.when(pitch_at == 0)
-    def _():
-        state_ref[:, HF - 2 : HF, own_rows] = ghost_ref[...]
-
-    @pl.when(pitch_at == slabs - 1)
-    def _():
-        state_ref[:, HF + cells : HF + cells + 2, own_rows] = ghost_ref[...]
-
-    edges, _ = edge_layout(variables, cells, 0)
-    corners, _ = corner_layout(variables)
-    parts, _ = edge_layout(variables, cells, HF)
+    part = rows // slabs
+    for end, plane in ((0, HF - 2), (1, HF + cells)):
+
+        @pl.when(pitch_at == end * (slabs - 1))
+        def _():
+            pieces = [share_ref[end]]
+            for got_ref in got_refs:
+                pieces += [got_ref[i] for i in range(got_ref.shape[0])]
+            for distance, piece in enumerate(pieces):
+                at = PAD + part * (distance if end == 0 else slabs - 1 - distance)
+                for layer in range(2):
+                    state_ref[:, plane + layer, at : at + part] = piece[
+                        :, layer * part : (layer + 1) * part
+                    ]
+
+    sides, _ = side_layout(variables)
+    corners, _ = corner_layout(variables, cells)
 
     def move(up):
-        for v, which, plane, count, place in parts:
+        for v, which, depth, count, place in sides:
+            plane = halo_plane(cells, which, depth, jnp.logical_not(even))
+            corner_ref[place : place + count] = refs[which][v, plane, edge_rows(rows, count, up)]
+        for v, which, plane, count, place in corners:
             out_ref[place : place + count] = refs[which][v, plane, edge_rows(rows, count, not up)]
-        for v, which, plane, count, place in edges:
-            refs[which][v, plane, halo_rows(rows, count, up)] = edge_ref[place : place + count]
-        for corner_ref, upper in ((corner_1, even), (corner_2, jnp.logical_not(even))):
-            for v, which, depth, count, place in corners:
-                width = (HF, HP)[which]
-                plane = jnp.where(upper, width + cells + depth - 1, width - depth)
-                refs[which][v, plane, halo_rows(rows, count, up)] = corner_ref[place : place + count]
 
     pl.when(blk_even)(lambda: move(False))
     pl.when(jnp.logical_not(blk_even))(lambda: move(True))
 
 
 class Block:
-    def __init__(self, cells, rows, slabs, blocks, state_ref, source_ref, flux_refs):
+    def __init__(self, cells, rows, slabs, blocks, state_ref, source_ref, band_ref, flux_refs):
         self.cells, self.rows, self.slabs, self.blocks = cells, rows, slabs, blocks
         self.state_ref, self.source_ref, self.flux_refs = state_ref, source_ref, flux_refs
+        self.band_ref = band_ref
         self.variables, _, _, self.lanes = state_ref.shape
         self.pitch_at = lax.axis_index("pitch")
         self.blk_at = lax.axis_index("blk")
@@ -329,12 +340,6 @@
             @pl.when(self.pitch_at == end)
             def _():
                 ref[:, width - 2 + at : width + at] = self.state_ref[:, HF - 2 + at : HF + at]
-
-    def shift_down(self, values, lane):
-        return jnp.where(lane == self.lanes - 1, values, pltpu.roll(values, self.lanes - 1, 1))
-
-    def shift_up(self, values, lane):
-        return jnp.where(lane == 0, values, pltpu.roll(values, 1, 1))
 
     def advance(self, step, from_ref, to_ref, lo, hi):
         width = HF - 2 * step
@@ -353,17 +358,28 @@
             pressure = gamma_less * (
                 u[4] - 0.5 * (u[1] * speed[0] + u[2] * speed[1] + u[3] * speed[2])
             )
-            half = (0.5 * scale) * pressure
+            half = 0.5 * pressure
             total = u[4] + pressure
             for d, flux_ref in enumerate((pitch_ref, axial_ref, radial_ref)):
-                w = (0.5 * scale) * speed[d]
+                w = 0.5 * speed[d]
                 for v in (1, 2, 3):
                     flux = u[v] * w
                     flux_ref[v - 1, plane + HP + 1] = flux + half if v == d + 1 else flux
                 flux_ref[3, plane + HP + 1] = total * w
 
         def update(plane):
-            lane = lax.broadcasted_iota(jnp.int32, (count, lanes), 1)
+            at = slice(row_at, row_at + count)
+            here = [from_ref[v, plane + width, at] for v in range(variables)]
+            along = [0.5 * here[3]] + [radial_ref[v, plane + HP + 1, at] for v in range(variables - 1)]
+            values = jnp.concatenate(
+                [jnp.concatenate(pair, axis=1) for pair in zip(here, along)], axis=0
+            )
+            coarse = values.astype(jnp.bfloat16)
+            fine = (values - coarse.astype(F32)).astype(jnp.bfloat16)
+            band = self.band_ref[...]
+            radial = jnp.dot(coarse, band, preferred_element_type=F32) + jnp.dot(
+                fine, band, preferred_element_type=F32
+            )
             for v in range(variables):
 
                 def state(ahead, over):
@@ -379,26 +395,17 @@
 
                     return flux(1) - flux(-1)
 
-                here = state(0, 0)
                 change = change_of(pitch_ref, 1, 1, 0) + change_of(axial_ref, 2, 0, 1)
-                along = from_ref[3, plane + width, row_at : row_at + count] if v == 0 else (
-                    radial_ref[v - 1, plane + HP + 1, row_at : row_at + count]
-                )
                 if v == 0:
-                    change = (0.5 * scale) * change
-                    along = (0.5 * scale) * along
+                    change = 0.5 * change
                 near = (state(1, 0) + state(-1, 0)) + (state(0, 1) + state(0, -1))
                 far = (state(2, 0) + state(-2, 0)) + (state(0, 2) + state(0, -2))
-                scaled = (scale * diss_coeff) * here
-                near_here = 4.0 * scaled
-                ahead = self.shift_down(near_here + along - self.shift_down(scaled, lane), lane)
-                behind = self.shift_up(near_here - along - self.shift_up(scaled, lane), lane)
-                change = change + (ahead + behind) + (scale * diss_coeff) * (4.0 * near - far)
-                change = change + (scale * (1.5 / physical_step - 18.0 * diss_coeff)) * here
-                source = self.source_ref[v, plane + HP, row_at : row_at + count]
-                flow = self.state_ref[v, plane + HF, row_at : row_at + count]
+                change = change + ((4.0 * diss_coeff) * near - diss_coeff * far)
+                change = change + radial[v * count : (v + 1) * count]
+                source = self.source_ref[v, plane + HP, at]
+                flow = self.state_ref[v, plane + HF, at]
                 to_at = row_at - PAD if last else row_at
-                to_ref[v, plane + out_width, to_at : to_at + count] = (flow + scale * source) - change
+                to_ref[v, plane + out_width, to_at : to_at + count] = flow + scale * (source - change)
 
         def pairs(body, start, stop):
             def both(index, carry):
@@ -416,20 +423,26 @@
 
 
 def start_sections(cells, rows, slabs, blocks, *refs):
-    got_ref = refs[2]
-    state_ref, source_ref, mid_1, mid_2, new_ref, kept_ref, sent_ref = refs[3:10]
-    flux_refs = refs[10:]
-    block = Block(cells, rows, slabs, blocks, state_ref, source_ref, flux_refs)
+    got_ref, corner_1, corner_2, band_ref = refs[2:6]
+    state_ref, source_ref, mid_1, mid_2, new_ref, kept_ref, sent_ref = refs[7:14]
+    flux_refs = refs[14:]
+    block = Block(cells, rows, slabs, blocks, state_ref, source_ref, band_ref, flux_refs)
     variables = state_ref.shape[0]
-    parts, _ = edge_layout(variables, cells, HF)
+    even = is_even("pitch")
+    sides, _ = side_layout(variables)
+    corners, _ = corner_layout(variables, cells)
     into = (state_ref, source_ref)
 
     def unpack(up):
-        for v, which, plane, count, place in parts:
-            into[which][v, plane, halo_rows(rows, count, up)] = got_ref[place : place + count]
-
-    pl.when(is_even("blk"))(lambda: unpack(True))
-    pl.when(jnp.logical_not(is_even("blk")))(lambda: unpack(False))
+        for v, which, plane, count, place in corners:
+            into[which][v, plane, halo_rows(rows, count, not up)] = got_ref[place : place + count]
+        for corner_ref, upper in ((corner_1, even), (corner_2, jnp.logical_not(even))):
+            for v, which, depth, count, place in sides:
+                plane = halo_plane(cells, which, depth, upper)
+                into[which][v, plane, halo_rows(rows, count, up)] = corner_ref[place : place + count]
+
+    pl.when(is_even("blk"))(lambda: unpack(False))
+    pl.when(jnp.logical_not(is_even("blk")))(lambda: unpack(True))
     block.clamp_ends(state_ref)
     block.keep_ghosts(mid_1, HF - 2)
     block.keep_ghosts(mid_2, HF - 4)
@@ -441,7 +454,7 @@
         for step, (from_ref, to_ref) in enumerate(
             ((state_ref, mid_1), (mid_1, mid_2), (mid_2, new_ref))
         ):
-            planes = HF - 2 * step
+            planes = 2 if step == 0 else HF - 2 * step
             lo = jnp.where(high, cells - planes, 0)
             block.advance(step, from_ref, to_ref, lo, lo + planes)
 
@@ -459,13 +472,16 @@
 
 
 def finish_sections(cells, rows, slabs, blocks, *refs):
-    state_ref, source_ref = refs[:2]
-    mid_1, mid_2, new_ref = refs[5:8]
-    block = Block(cells, rows, slabs, blocks, state_ref, source_ref, refs[8:])
+    state_ref, source_ref, band_ref = refs[:3]
+    mid_1, mid_2, new_ref = refs[6:9]
+    block = Block(cells, rows, slabs, blocks, state_ref, source_ref, band_ref, refs[9:])
     low, high = block.pitch_at == 0, block.pitch_at == slabs - 1
-    for step, (from_ref, to_ref) in enumerate(
-        ((state_ref, mid_1), (mid_1, mid_2), (mid_2, new_ref))
-    ):
+    width = HF - 2
+    pl.when(jnp.logical_not(low))(lambda: block.advance(0, state_ref, mid_1, -width, 2))
+    pl.when(jnp.logical_not(high))(
+        lambda: block.advance(0, state_ref, mid_1, cells - 2, cells + width)
+    )
+    for step, from_ref, to_ref in ((1, mid_1, mid_2), (2, mid_2, new_ref)):
         done = HF - 2 * step
         out_width = done - 2
         lo = jnp.where(low, done, -out_width)
@@ -566,7 +582,6 @@
     long_rows = rows + 2 * PAD
     state_shape = (variables, cells + 2 * HF, long_rows, lanes)
     source_shape = (variables, cells + 2 * HP, long_rows, lanes)
-    corner = (corner_layout(variables)[1], lanes)
 
     inputs = (store, sample_times, harmonics, flow_state, prior_state)
     shapes = [store.shape, sample_times.shape, harmonics.shape, state_shape, flow_state.shape]
@@ -583,69 +598,80 @@
         functools.partial(pack_pitch, cells, rows), [source_shape, halo, halo], state, prior
     )
     first = lax.ppermute(first, "pitch", swap_pairs(slabs, 0))
+    second = lax.ppermute(second, "pitch", swap_pairs(slabs, 1))
+    edge_shape = (edge_layout(variables, cells, 0)[1], lanes)
+    side_shape = (side_layout(variables)[1], lanes)
+    edge_1, edge_2, corner_1 = call(
+        functools.partial(pack_axial, cells, rows),
+        [edge_shape, edge_shape, side_shape],
+        state,
+        source,
+    )
+    edge_2 = lax.ppermute(edge_2, "blk", swap_pairs(blocks, 1))
+    edge_1 = lax.ppermute(edge_1, "blk", swap_pairs(blocks, 0))
+    corner_1 = lax.ppermute(corner_1, ("blk", "pitch"), diagonal_pairs(slabs, blocks, 0))
     while 1 << step < slabs:
         [send] = call(
             functools.partial(join_shares, step), [(1 << step,) + face], share, *gathered
         )
         gathered.append(lax.ppermute(send, "pitch", flip_pairs(slabs, 1 << step)))
         step += 1
-    second = lax.ppermute(second, "pitch", swap_pairs(slabs, 1))
-    edge, corner_1 = call(
-        functools.partial(pack_axial, cells, rows),
-        [(edge_layout(variables, cells, 0)[1], lanes), corner],
-        state,
-        source,
-    )
-    edge = lax.ppermute(edge, "blk", swap_pairs(blocks, 1))
-    corner_1 = lax.ppermute(corner_1, ("blk", "pitch"), diagonal_pairs(slabs, blocks, 0))
-    ghost, corner_2 = call(
-        functools.partial(join_ghosts, cells, rows, slabs),
-        [(variables, 2, rows, lanes), corner],
-        state,
-        source,
-        share,
-        *gathered,
-    )
-    corner_2 = lax.ppermute(corner_2, ("blk", "pitch"), diagonal_pairs(slabs, blocks, 1))
-    table, base, gain = call(
+    table, base, gain, band = call(
         prepare_close,
-        [(2, orders - 1, 2 * part, lanes), (2,) + face, (2 * part, lanes)],
+        [(2, orders - 1, 2 * part, lanes), (2,) + face, (2 * part, lanes), (2 * lanes, lanes)],
         store,
         times,
         active,
-    )
-
-    state, source, out = call(
-        functools.partial(place_halos, cells, rows, slabs),
-        [state_shape, source_shape, (edge_layout(variables, cells, HF)[1], lanes)],
-        state,
-        source,
-        first,
-        second,
-        edge,
-        corner_1,
-        corner_2,
-        ghost,
-        gain,
-        aliases={0: 0, 1: 1},
-    )
-    got = lax.ppermute(out, "blk", swap_pairs(blocks, 0))
+        types=[F32, F32, F32, jnp.bfloat16],
+    )
+
+    sizes = (cells, rows, slabs, blocks)
     mid_shapes = [
         (variables, cells + 2 * HP, long_rows, lanes),
         (variables, cells + 2 * HP - 4, long_rows, lanes),
     ]
     flux_shape = (variables - 1, cells + 2 * HP + 2, long_rows, lanes)
     flux_scratch = [pltpu.VMEM(flux_shape, F32)] * 3
-    sizes = (cells, rows, slabs, blocks)
+    state, source, mid_1 = call(
+        functools.partial(place_edges, *sizes),
+        [state_shape, source_shape, mid_shapes[0]],
+        state,
+        source,
+        edge_1,
+        edge_2,
+        band,
+        scratch=flux_scratch,
+        aliases={0: 0, 1: 1},
+        limit=12,
+    )
+    state, source, out, corner_2 = call(
+        functools.partial(place_halos, *sizes[:3]),
+        [state_shape, source_shape, (corner_layout(variables, cells)[1], lanes), side_shape],
+        state,
+        source,
+        first,
+        second,
+        share,
+        *gathered,
+        aliases={0: 0, 1: 1},
+    )
+    corner_2 = lax.ppermute(corner_2, "blk", swap_pairs(blocks, 1))
+    got = lax.ppermute(out, "blk", swap_pairs(blocks, 0))
     half_faces = (slabs // 2,) + face
     state, source, mid_1, mid_2, new, held, send = call(
         functools.partial(start_sections, *sizes),
-        [state_shape, source_shape] + mid_shapes + [flow_state.shape, half_faces, half_faces],
+        [state_shape, source_shape]
+        + mid_shapes
+        + [flow_state.shape, half_faces, half_faces],
         state,
         source,
         got,
+        corner_1,
+        corner_2,
+        band,
+        mid_1,
         scratch=flux_scratch,
-        aliases={0: 0, 1: 1},
+        aliases={0: 0, 1: 1, 6: 2},
         limit=12,
     )
     step = slabs.bit_length() - 2
@@ -659,11 +685,12 @@
         mid_shapes + [flow_state.shape],
         state,
         source,
+        band,
         mid_1,
         mid_2,
         new,
         scratch=flux_scratch,
-        aliases={2: 0, 3: 1, 4: 2},
+        aliases={3: 0, 4: 1, 5: 2},
         limit=12,
     )
     while step > 0:

time: 42.2 us -> 42.9 us (1.017)
  the two profiles are of different devices: /device:TPU:0 before, /device:TPU:4 now
where the time goes in v4:
time: 42.9 us; the launch traced here: 42.7 us
  starting transfers between devices  23.7 us (55%)
  Pallas kernels  9.28 us (22%)
  waiting for transfers between devices  8.89 us (21%)
  between operations  0.79 us (2%)
    pallas_call x12, Pallas kernels, call(): pl.pallas_call(body, out_shape=outs, in_specs=in_specs or [VMEM] * len(ar...  9.28 us
    ppermute x1, starting transfers between devices, shards(): gathered, step = ([lax.ppermute(send, 'pitch', flip_pairs(slabs, 1))], 1)  4.44 us
    ppermute x1, starting transfers between devices, shards(): lax.ppermute(corner_1, ('blk', 'pitch'), diagonal_pairs(slabs, blocks, 0))  4.03 us
    ppermute x1, starting transfers between devices, shards(): corner_2 = lax.ppermute(corner_2, 'blk', swap_pairs(blocks, 1))  3.73 us
    ppermute x1, starting transfers between devices, shards(): edge_2 = lax.ppermute(edge_2, 'blk', swap_pairs(blocks, 1))  3.43 us
    ppermute x1, starting transfers between devices, shards(): spread.append(lax.ppermute(send, 'pitch', pairs))  3.4 us
    ppermute x1, waiting for transfers between devices, shards(): corner_2 = lax.ppermute(corner_2, 'blk', swap_pairs(blocks, 1))  2.65 us
    ppermute x1, waiting for transfers between devices, shards(): second_sample = lax.ppermute(send, 'pitch', flip_pairs(slabs, 1))  2.63 us
  transfers between devices with their start and end apart: 11, of which 4 were waited for; matrix products, arithmetic and copies ran while one was open for 0% of the time, Pallas kernels for 11%

profile of v4, /device:TPU:4, one launch (start us, length us, event | category | flops | bytes accessed | tf_op | source)
XLA Modules:
  0.0 42.7 jit_solution(12927057491952307174)
XLA Ops:
  0.6 1.8 %shard_map.76 = (f32[2,49,5,8,128]{4,3,2,1,0:T(8,128)S(1)}, s32[2,4,128]{2,1,0:T(4,128)S(1)}, s32[4,128]{1,0:T(4,128)S(1)}, f32[5,20,32,128]{3,2,1,0:T(8,128)S(1...) custom-call(f32[2,49,5,8,128]{4,3,2,1,0:T(8,128)} %bitcast.3, ...), custom_call_target="tpu_custom_call" | custom-call | bytes 6709248 | tf_op jit(solution)/shard_map/pallas_call | solution.py:38
  2.4 0.1 shard_map.77
  2.5 1.6 %collective-permute-start.2 = (f32[5,10,16,128]{3,2,1,0:T(8,128)S(1)}, f32[5,10,16,128]{3,2,1,0:T(8,128)S(1)}, u32[]{:S(2)}, u32[]{:S(2)}) collective-permute-start(f32[5,10,16,128]{3,2,1,0:T(8,128)S(1)} %get-tuple-element.52), channel_id=1, source_target_pairs={{0,1},{2,3},{1,0},{3,2},{4,5},{6,7},{5,4},{7,6},{8,9},{10,11},{9,8... | collective-permute-start | bytes 1228808 | tf_op jit(solution)/shard_map/ppermute | solution.py:600
  4.2 0.7 %collective-permute-start.3 = (f32[5,10,16,128]{3,2,1,0:T(8,128)S(1)}, f32[5,10,16,128]{3,2,1,0:T(8,128)S(1)}, u32[]{:S(2)}, u32[]{:S(2)}) collective-permute-start(f32[5,10,16,128]{3,2,1,0:T(8,128)S(1)} %get-tuple-element.53), channel_id=1, source_target_pairs={{1,2},{2,1},{5,6},{6,5},{9,10},{10,9},{13,14},{14,13},{17,18},{18,... | collective-permute-start | bytes 1228808 | tf_op jit(solution)/shard_map/ppermute | solution.py:601
  4.9 0.1 shard_map.78
  5.0 0.1 collective-permute-start
  5.0 3.4 %collective-permute-start.1 = (f32[400,128]{1,0:T(8,128)S(1)}, f32[400,128]{1,0:T(8,128)S(1)}, u32[]{:S(2)}, u32[]{:S(2)}) collective-permute-start(f32[400,128]{1,0:T(8,128)S(1)} %get-tuple-element.45), channel_id=1, source_target_pairs={{4,8},{12,16},{20,24},{8,4},{16,12},{24,20},{5,9},{13,17},{21,25},... | collective-permute-start | bytes 614408 | tf_op jit(solution)/shard_map/ppermute | solution.py:610
  8.5 4.4 %collective-permute-start.4 = (f32[1,5,8,128]{3,2,1,0:T(8,128)S(1)}, f32[1,5,8,128]{3,2,1,0:T(8,128)S(1)}, u32[]{:S(2)}, u32[]{:S(2)}) collective-permute-start(f32[1,5,8,128]{3,2,1,0:T(8,128)S(1)} %get-tuple-element.55), channel_id=1, source_target_pairs={{0,1},{1,0},{2,3},{3,2},{4,5},{5,4},{6,7},{7,6},{8,9},{9,8},{10,11... | collective-permute-start | bytes 61448 | tf_op jit(solution)/shard_map/ppermute | solution.py:596
  12.9 1.8 %collective-permute-done.4.refs_0_.refs_5_ = f32[1,5,8,128]{3,2,1,0:T(8,128)S(1)} collective-permute-done((f32[1,5,8,128]{3,2,1,0:T(8,128)S(1)}, f32[1,5,8,128]{3,2,1,0:T(8,128)S(1)}, u32[]{:S(2)}, u32[]{:S(2)}) %collective-permute-start.4) | collective-permute-done | bytes 20512 | tf_op jit(solution)/shard_map/ppermute | solution.py:596
  14.7 2.1 %collective-permute-start.5 = (f32[2,5,8,128]{3,2,1,0:T(8,128)S(1)}, f32[2,5,8,128]{3,2,1,0:T(8,128)S(1)}, u32[]{:S(2)}, u32[]{:S(2)}) collective-permute-start(f32[2,5,8,128]{3,2,1,0:T(8,128)S(1)} %shard_map.81), channel_id=1, source_target_pairs={{0,2},{1,3},{2,0},{3,1},{4,6},{5,7},{6,4},{7,5},{8,10},{9,11},{10,... | collective-permute-start | bytes 122888 | tf_op jit(solution)/shard_map/ppermute | solution.py:617
  16.8 0.4 shard_map.79
  17.2 0.0 collective-permute-done.refs_2_
  17.2 0.0 collective-permute-done.1.refs_3_
  17.2 0.7 %shard_map.80 = (f32[5,20,32,128]{3,2,1,0:T(8,128)S(1)}, f32[5,16,32,128]{3,2,1,0:T(8,128)S(1)}, f32[5,16,32,128]{3,2,1,0:T(8,128)S(1)}) custom-call(f32[5,20,32,128]{3,2,1,0:T(8,128)S(1)} %get-tuple-element.41.state_ref.refs_0_, f32[5,16,32,128]{3,2,1,0:T(8,128)S(1)} %get-tuple-element.43.source_ref.refs_1_, ...), custom_call_target="tpu_custom_call", output_to_operand_aliasing={{0}: (0, {}), {1}: (1, {})} | custom-call | bytes 7749632 | tf_op jit(solution)/shard_map/pallas_call | solution.py:38
  17.9 1.8 %collective-permute-done.5.refs_6_ = f32[2,5,8,128]{3,2,1,0:T(8,128)S(1)} collective-permute-done((f32[2,5,8,128]{3,2,1,0:T(8,128)S(1)}, f32[2,5,8,128]{3,2,1,0:T(8,128)S(1)}, u32[]{:S(2)}, u32[]{:S(2)}) %collective-permute-start.5) | collective-permute-done | bytes 40992 | tf_op jit(solution)/shard_map/ppermute | solution.py:617
  19.7 0.0 collective-permute-done.2.refs_2_
  19.7 0.0 collective-permute-done.3.refs_3_
  19.7 0.2 shard_map.82
  19.9 0.1 collective-permute-start.6
  20.0 4.0 %collective-permute-start.7 = (f32[112,128]{1,0:T(8,128)S(1)}, f32[112,128]{1,0:T(8,128)S(1)}, u32[]{:S(2)}, u32[]{:S(2)}) collective-permute-start(f32[112,128]{1,0:T(8,128)S(1)} %get-tuple-element.59), channel_id=1, source_target_pairs={{4,9},{5,8},{6,11},{7,10},{12,17},{13,16},{14,19},{15,18},{20,25},... | collective-permute-start | bytes 172040 | tf_op jit(solution)/shard_map/ppermute | solution.py:612
  24.0 3.7 %collective-permute-start.8 = (f32[112,128]{1,0:T(8,128)S(1)}, f32[112,128]{1,0:T(8,128)S(1)}, u32[]{:S(2)}, u32[]{:S(2)}) collective-permute-start(f32[112,128]{1,0:T(8,128)S(1)} %get-tuple-element.60), channel_id=1, source_target_pairs={{4,8},{12,16},{20,24},{8,4},{16,12},{24,20},{5,9},{13,17},{21,25},... | collective-permute-start | bytes 172040 | tf_op jit(solution)/shard_map/ppermute | solution.py:658
  27.8 0.0 collective-permute-done.7.refs_3_
  27.8 2.7 %collective-permute-done.8.refs_4_ = f32[112,128]{1,0:T(8,128)S(1)} collective-permute-done((f32[112,128]{1,0:T(8,128)S(1)}, f32[112,128]{1,0:T(8,128)S(1)}, u32[]{:S(2)}, u32[]{:S(2)}) %collective-permute-start.8) | collective-permute-done | bytes 57376 | tf_op jit(solution)/shard_map/ppermute | solution.py:658
  30.4 0.0 collective-permute-done.6.refs_2_
  30.4 1.4 %shard_map.83 = (f32[5,20,32,128]{3,2,1,0:T(8,128)S(1)}, f32[5,16,32,128]{3,2,1,0:T(8,128)S(1)}, f32[5,16,32,128]{3,2,1,0:T(8,128)S(1)}, f32[5,12,32,128]{3,2,1,...) custom-call(f32[5,20,32,128]{3,2,1,0:T(8,128)S(1)} %get-tuple-elemen, ...), custom_call_target="tpu_custom_call", output_to_operand_aliasing={{0}: (0, {}), {1}: (1, {}), {2}: (6, {})} | custom-call | bytes 10268672 | tf_op jit(solution)/shard_map/pallas_call | solution.py:38
  31.8 3.4 %collective-permute-start.9 = (f32[2,5,8,128]{3,2,1,0:T(8,128)S(1)}, f32[2,5,8,128]{3,2,1,0:T(8,128)S(1)}, u32[]{:S(2)}, u32[]{:S(2)}) collective-permute-start(f32[2,5,8,128]{3,2,1,0:T(8,128)S(1)} %get-tuple-element.70), channel_id=1, source_target_pairs={{0,2},{3,1},{4,6},{7,5},{8,10},{11,9},{12,14},{15,13},{16,18},{19,... | collective-permute-start | bytes 122888 | tf_op jit(solution)/shard_map/ppermute | solution.py:682
  35.2 2.6 %shard_map.84 = (f32[5,16,32,128]{3,2,1,0:T(8,128)S(1)}, f32[5,12,32,128]{3,2,1,0:T(8,128)S(1)}, f32[5,8,16,128]{3,2,1,0:T(8,128)S(1)}) custom-call(f32[5,20,32,128]{3,2,1,0:T(8,128)S(1)} %get-tuple-element.62.refs_0_, f32[5,16,32,128]{3,2,1,0:T(8,128)S(1)} %get-tuple-element.63.refs_1_, ...), custom_call_target="tpu_custom_call", output_to_operand_aliasing={{0}: (3, {}), {1}: (4, {}), {2}: (5, {})} | custom-call | bytes 8323072 | tf_op jit(solution)/shard_map/pallas_call | solution.py:38
  37.8 0.0 collective-permute-done.9.got_ref
  37.8 0.1 collective-permute-start.10
  37.9 1.1 %shard_map.86 = (f32[5,8,16,128]{3,2,1,0:T(8,128)}, f32[2,49,5,8,128]{4,3,2,1,0:T(8,128)}) custom-call(f32[5,8,16,128]{3,2,1,0:T(8,128)S(1)} %get-tuple-element.67.after_ref.new_ref, f32[2,49,5,8,128]{4,3,2,1,0:T(8,128)S(1)} %get-tuple-element.46.store_ref.refs_1_, f32[2,48,8,128]{3,2,1,0:T(8,128)S(1)} %get-tuple-element.68.table_ref.refs_2_, ...), custom_call_target="tpu_custom_call" | custom-call | bytes 5083136 | tf_op jit(solution)/shard_map/pallas_call | solution.py:38
  39.0 2.6 %collective-permute-done.10.refs_6_ = f32[1,5,8,128]{3,2,1,0:T(8,128)S(1)} collective-permute-done((f32[1,5,8,128]{3,2,1,0:T(8,128)S(1)}, f32[1,5,8,128]{3,2,1,0:T(8,128)S(1)}, u32[]{:S(2)}, u32[]{:S(2)}) %collective-permute-start.10) | collective-permute-done | bytes 20512 | tf_op jit(solution)/shard_map/ppermute | solution.py:706
  41.7 1.0 %shard_map.87 = (f32[2,49,5,8,128]{4,3,2,1,0:T(8,128)}, f32[2,5,8,128]{3,2,1,0:T(8,128)}) custom-call(f32[2,49,5,8,128]{4,3,2,1,0:T(8,128)} %get-tuple-element.73.refs_0_, f32[2,49,5,8,128]{4,3,2,1,0:T(8,128)S(1)} %get-tuple-element.46.store_ref.refs_1_, f32[2,48,8,128]{3,2,1,0:T(8,128)S(1)} %get-tuple-element.68.table_ref.refs_2_, ...), custom_call_target="tpu_custom_call", output_to_operand_aliasing={{0}: (0, {})} | custom-call | bytes 6541312 | tf_op jit(solution)/shard_map/pallas_call | solution.py:38
  (2 shorter events, 0.0 us)
Async XLA Ops:
  2.5 17.2 %collective-permute-start.2 = (f32[5,10,16,128]{3,2,1,0:T(8,128)S(1)}, f32[5,10,16,128]{3,2,1,0:T(8,128)S(1)}, u32[]{:S(2)}, u32[]{:S(2)}) collective-permute-start(f32[5,10,16,128]{3,2,1,0:T(8,128)S(1)} %get-tuple-element.52), channel_id=1, source_target_pairs={{0,1},{2,3},{1,0},{3,2},{4,5},{6,7},{5,4},{7,6},{8,9},{10,11},{9,8... | collective-permute-start | bytes 1228808 | tf_op jit(solution)/shard_map/ppermute | solution.py:600
  4.2 15.6 %collective-permute-start.3 = (f32[5,10,16,128]{3,2,1,0:T(8,128)S(1)}, f32[5,10,16,128]{3,2,1,0:T(8,128)S(1)}, u32[]{:S(2)}, u32[]{:S(2)}) collective-permute-start(f32[5,10,16,128]{3,2,1,0:T(8,128)S(1)} %get-tuple-element.53), channel_id=1, source_target_pairs={{1,2},{2,1},{5,6},{6,5},{9,10},{10,9},{13,14},{14,13},{17,18},{18,... | collective-permute-start | bytes 1228808 | tf_op jit(solution)/shard_map/ppermute | solution.py:601
  5.0 12.2 %collective-permute-start = (f32[400,128]{1,0:T(8,128)S(1)}, f32[400,128]{1,0:T(8,128)S(1)}, u32[]{:S(2)}, u32[]{:S(2)}) collective-permute-start(f32[400,128]{1,0:T(8,128)S(1)} %get-tuple-element.44), channel_id=1, source_target_pairs={{0,4},{8,12},{16,20},{24,28},{4,0},{12,8},{20,16},{28,24},{1,5},{9... | collective-permute-start | bytes 614408 | tf_op jit(solution)/shard_map/ppermute | solution.py:611
  5.0 12.2 %collective-permute-start.1 = (f32[400,128]{1,0:T(8,128)S(1)}, f32[400,128]{1,0:T(8,128)S(1)}, u32[]{:S(2)}, u32[]{:S(2)}) collective-permute-start(f32[400,128]{1,0:T(8,128)S(1)} %get-tuple-element.45), channel_id=1, source_target_pairs={{4,8},{12,16},{20,24},{8,4},{16,12},{24,20},{5,9},{13,17},{21,25},... | collective-permute-start | bytes 614408 | tf_op jit(solution)/shard_map/ppermute | solution.py:610
  8.5 6.2 %collective-permute-start.4 = (f32[1,5,8,128]{3,2,1,0:T(8,128)S(1)}, f32[1,5,8,128]{3,2,1,0:T(8,128)S(1)}, u32[]{:S(2)}, u32[]{:S(2)}) collective-permute-start(f32[1,5,8,128]{3,2,1,0:T(8,128)S(1)} %get-tuple-element.55), channel_id=1, source_target_pairs={{0,1},{1,0},{2,3},{3,2},{4,5},{5,4},{6,7},{7,6},{8,9},{9,8},{10,11... | collective-permute-start | bytes 61448 | tf_op jit(solution)/shard_map/ppermute | solution.py:596
  14.7 5.1 %collective-permute-start.5 = (f32[2,5,8,128]{3,2,1,0:T(8,128)S(1)}, f32[2,5,8,128]{3,2,1,0:T(8,128)S(1)}, u32[]{:S(2)}, u32[]{:S(2)}) collective-permute-start(f32[2,5,8,128]{3,2,1,0:T(8,128)S(1)} %shard_map.81), channel_id=1, source_target_pairs={{0,2},{1,3},{2,0},{3,1},{4,6},{5,7},{6,4},{7,5},{8,10},{9,11},{10,... | collective-permute-start | bytes 122888 | tf_op jit(solution)/shard_map/ppermute | solution.py:617
  19.9 10.5 %collective-permute-start.6 = (f32[216,128]{1,0:T(8,128)S(1)}, f32[216,128]{1,0:T(8,128)S(1)}, u32[]{:S(2)}, u32[]{:S(2)}) collective-permute-start(f32[216,128]{1,0:T(8,128)S(1)} %get-tuple-element.58), channel_id=1, source_target_pairs={{0,4},{8,12},{16,20},{24,28},{4,0},{12,8},{20,16},{28,24},{1,5},{9... | collective-permute-start | bytes 331784 | tf_op jit(solution)/shard_map/ppermute | solution.py:659
  20.0 7.8 %collective-permute-start.7 = (f32[112,128]{1,0:T(8,128)S(1)}, f32[112,128]{1,0:T(8,128)S(1)}, u32[]{:S(2)}, u32[]{:S(2)}) collective-permute-start(f32[112,128]{1,0:T(8,128)S(1)} %get-tuple-element.59), channel_id=1, source_target_pairs={{4,9},{5,8},{6,11},{7,10},{12,17},{13,16},{14,19},{15,18},{20,25},... | collective-permute-start | bytes 172040 | tf_op jit(solution)/shard_map/ppermute | solution.py:612
  24.0 6.4 %collective-permute-start.8 = (f32[112,128]{1,0:T(8,128)S(1)}, f32[112,128]{1,0:T(8,128)S(1)}, u32[]{:S(2)}, u32[]{:S(2)}) collective-permute-start(f32[112,128]{1,0:T(8,128)S(1)} %get-tuple-element.60), channel_id=1, source_target_pairs={{4,8},{12,16},{20,24},{8,4},{16,12},{24,20},{5,9},{13,17},{21,25},... | collective-permute-start | bytes 172040 | tf_op jit(solution)/shard_map/ppermute | solution.py:658
  31.8 6.0 %collective-permute-start.9 = (f32[2,5,8,128]{3,2,1,0:T(8,128)S(1)}, f32[2,5,8,128]{3,2,1,0:T(8,128)S(1)}, u32[]{:S(2)}, u32[]{:S(2)}) collective-permute-start(f32[2,5,8,128]{3,2,1,0:T(8,128)S(1)} %get-tuple-element.70), channel_id=1, source_target_pairs={{0,2},{3,1},{4,6},{7,5},{8,10},{11,9},{12,14},{15,13},{16,18},{19,... | collective-permute-start | bytes 122888 | tf_op jit(solution)/shard_map/ppermute | solution.py:682
  37.8 3.8 %collective-permute-start.10 = (f32[1,5,8,128]{3,2,1,0:T(8,128)S(1)}, f32[1,5,8,128]{3,2,1,0:T(8,128)S(1)}, u32[]{:S(2)}, u32[]{:S(2)}) collective-permute-start(f32[1,5,8,128]{3,2,1,0:T(8,128)S(1)} %get-tuple-element.76), channel_id=1, source_target_pairs={{0,1},{1,0},{2,3},{3,2},{4,5},{5,4},{6,7},{7,6},{8,9},{9,8},{10,11... | collective-permute-start | bytes 61448 | tf_op jit(solution)/shard_map/ppermute | solution.py:706

commit v5 on v4

--- a/solution.py
+++ b/solution.py
@@ -68,17 +68,18 @@
         out_ref[:, HF:] = source_ref[:, pl.ds(at, HP), own_rows]
 
 
-def pack_axial(cells, rows, state_ref, source_ref, edge_1, edge_2, corner_ref):
+def pack_axial(cells, rows, state_ref, source_ref, edge_1, edge_2, corner_1, corner_2):
     refs = (state_ref, source_ref)
     edges, _ = edge_layout(state_ref.shape[0], cells, 0)
     sides, _ = side_layout(state_ref.shape[0])
-    top = is_even("pitch")
+    even = is_even("pitch")
 
     def write(up):
-        for v, which, depth, count, place in sides:
-            width = (HF, HP)[which]
-            plane = jnp.where(top, width + cells - depth, width + depth - 1)
-            corner_ref[place : place + count] = refs[which][v, plane, edge_rows(rows, count, up)]
+        for corner_ref, top in ((corner_1, even), (corner_2, jnp.logical_not(even))):
+            for v, which, depth, count, place in sides:
+                width = (HF, HP)[which]
+                plane = jnp.where(top, width + cells - depth, width + depth - 1)
+                corner_ref[place : place + count] = refs[which][v, plane, edge_rows(rows, count, up)]
         for v, which, plane, count, place in edges:
             edge_1[place : place + count] = refs[which][v, plane, edge_rows(rows, count, not up)]
             edge_2[place : place + count] = refs[which][v, plane, edge_rows(rows, count, up)]
@@ -250,7 +251,7 @@
 
 def place_edges(cells, rows, slabs, blocks, *refs):
     edge_1, edge_2, band_ref = refs[2:5]
-    state_ref, source_ref, mid_1 = refs[5:8]
+    state_ref, source_ref, mid_1 = refs[6:9]
     into = (state_ref, source_ref)
     edges, _ = edge_layout(state_ref.shape[0], cells, 0)
 
@@ -261,19 +262,47 @@
 
     pl.when(is_even("blk"))(lambda: move(False))
     pl.when(jnp.logical_not(is_even("blk")))(lambda: move(True))
-    block = Block(cells, rows, slabs, blocks, state_ref, source_ref, band_ref, refs[8:])
+    block = Block(cells, rows, slabs, blocks, state_ref, source_ref, band_ref, refs[9:])
     block.clamp_ends(state_ref)
     block.advance(0, state_ref, mid_1, 2, cells - 2)
 
 
+def join_ghosts(rows, slabs, share_ref, after_ref, *refs):
+    del after_ref
+    got_refs, (ghost_ref, send_ref) = refs[:-2], refs[-2:]
+    part = rows // slabs
+    variables = ghost_ref.shape[0]
+    for end in range(2):
+
+        @pl.when(lax.axis_index("pitch") == end * (slabs - 1))
+        def _():
+            pieces = [share_ref[end]]
+            for got_ref in got_refs:
+                pieces += [got_ref[i] for i in range(got_ref.shape[0])]
+            for distance, piece in enumerate(pieces):
+                at = part * (distance if end == 0 else slabs - 1 - distance)
+                for layer in range(2):
+                    ghost_ref[:, layer, at : at + part] = piece[:, layer * part : (layer + 1) * part]
+
+    def write(at):
+        for v in range(variables):
+            for layer in range(2):
+                place = (2 * v + layer) * HP
+                send_ref[place : place + HP] = ghost_ref[v, layer, at : at + HP]
+
+    pl.when(is_even("blk"))(lambda: write(0))
+    pl.when(jnp.logical_not(is_even("blk")))(lambda: write(rows - HP))
+
+
+def ghost_planes(cells, end):
+    return HF + cells if end else HF - 2
+
+
 def place_halos(cells, rows, slabs, *refs):
-    first_ref, second_ref, share_ref = refs[2:5]
-    got_refs = refs[5:-4]
-    state_ref, source_ref, out_ref, corner_ref = refs[-4:]
+    first_ref, second_ref, ghost_ref = refs[2:5]
+    state_ref, source_ref, out_ref = refs[-3:]
     refs = (state_ref, source_ref)
-    pitch_at = lax.axis_index("pitch")
     even = is_even("pitch")
-    blk_even = is_even("blk")
     variables = state_ref.shape[0]
     own_rows = slice(PAD, PAD + rows)
     for halo_ref, upper in ((first_ref, even), (second_ref, jnp.logical_not(even))):
@@ -281,34 +310,21 @@
         state_ref[:, pl.ds(at, HF), own_rows] = halo_ref[:, :HF]
         at = jnp.where(upper, HP + cells, 0)
         source_ref[:, pl.ds(at, HP), own_rows] = halo_ref[:, HF:]
-
-    part = rows // slabs
-    for end, plane in ((0, HF - 2), (1, HF + cells)):
-
-        @pl.when(pitch_at == end * (slabs - 1))
+    for end in range(2):
+
+        @pl.when(lax.axis_index("pitch") == end * (slabs - 1))
         def _():
-            pieces = [share_ref[end]]
-            for got_ref in got_refs:
-                pieces += [got_ref[i] for i in range(got_ref.shape[0])]
-            for distance, piece in enumerate(pieces):
-                at = PAD + part * (distance if end == 0 else slabs - 1 - distance)
-                for layer in range(2):
-                    state_ref[:, plane + layer, at : at + part] = piece[
-                        :, layer * part : (layer + 1) * part
-                    ]
-
-    sides, _ = side_layout(variables)
+            plane = ghost_planes(cells, end)
+            state_ref[:, plane : plane + 2, own_rows] = ghost_ref[...]
+
     corners, _ = corner_layout(variables, cells)
 
     def move(up):
-        for v, which, depth, count, place in sides:
-            plane = halo_plane(cells, which, depth, jnp.logical_not(even))
-            corner_ref[place : place + count] = refs[which][v, plane, edge_rows(rows, count, up)]
         for v, which, plane, count, place in corners:
-            out_ref[place : place + count] = refs[which][v, plane, edge_rows(rows, count, not up)]
-
-    pl.when(blk_even)(lambda: move(False))
-    pl.when(jnp.logical_not(blk_even))(lambda: move(True))
+            out_ref[place : place + count] = refs[which][v, plane, edge_rows(rows, count, up)]
+
+    pl.when(is_even("blk"))(lambda: move(True))
+    pl.when(jnp.logical_not(is_even("blk")))(lambda: move(False))
 
 
 class Block:
@@ -423,9 +439,9 @@
 
 
 def start_sections(cells, rows, slabs, blocks, *refs):
-    got_ref, corner_1, corner_2, band_ref = refs[2:6]
-    state_ref, source_ref, mid_1, mid_2, new_ref, kept_ref, sent_ref = refs[7:14]
-    flux_refs = refs[14:]
+    got_ref, corner_1, corner_2, beyond_ref, band_ref = refs[2:7]
+    state_ref, source_ref, mid_1, mid_2, new_ref, kept_ref, sent_ref = refs[8:15]
+    flux_refs = refs[15:]
     block = Block(cells, rows, slabs, blocks, state_ref, source_ref, band_ref, flux_refs)
     variables = state_ref.shape[0]
     even = is_even("pitch")
@@ -440,6 +456,15 @@
             for v, which, depth, count, place in sides:
                 plane = halo_plane(cells, which, depth, upper)
                 into[which][v, plane, halo_rows(rows, count, up)] = corner_ref[place : place + count]
+        for end in range(2):
+
+            @pl.when(block.pitch_at == end * (slabs - 1))
+            def _():
+                for v in range(variables):
+                    for layer in range(2):
+                        place = (2 * v + layer) * HP
+                        plane = ghost_planes(cells, end) + layer
+                        state_ref[v, plane, halo_rows(rows, HP, up)] = beyond_ref[place : place + HP]
 
     pl.when(is_even("blk"))(lambda: unpack(False))
     pl.when(jnp.logical_not(is_even("blk")))(lambda: unpack(True))
@@ -562,12 +587,18 @@
 
 
 def diagonal_pairs(slabs, blocks, start):
-    along = dict((i, i) for i in range(slabs))
-    along.update(swap_pairs(slabs, start))
     return [
-        (b * slabs + p, other * slabs + along[p])
+        (b * slabs + p, other * slabs + q)
         for b, other in swap_pairs(blocks, 1)
-        for p in range(slabs)
+        for p, q in swap_pairs(slabs, start)
+    ]
+
+
+def end_pairs(slabs, blocks):
+    return [
+        (b * slabs + p, other * slabs + p)
+        for b, other in swap_pairs(blocks, 1)
+        for p in (0, slabs - 1)
     ]
 
 
@@ -601,15 +632,17 @@
     second = lax.ppermute(second, "pitch", swap_pairs(slabs, 1))
     edge_shape = (edge_layout(variables, cells, 0)[1], lanes)
     side_shape = (side_layout(variables)[1], lanes)
-    edge_1, edge_2, corner_1 = call(
+    edge_1, edge_2, corner_1, corner_2 = call(
         functools.partial(pack_axial, cells, rows),
-        [edge_shape, edge_shape, side_shape],
+        [edge_shape, edge_shape, side_shape, side_shape],
         state,
         source,
     )
     edge_2 = lax.ppermute(edge_2, "blk", swap_pairs(blocks, 1))
     edge_1 = lax.ppermute(edge_1, "blk", swap_pairs(blocks, 0))
-    corner_1 = lax.ppermute(corner_1, ("blk", "pitch"), diagonal_pairs(slabs, blocks, 0))
+    both = ("blk", "pitch")
+    corner_1 = lax.ppermute(corner_1, both, diagonal_pairs(slabs, blocks, 0))
+    corner_2 = lax.ppermute(corner_2, both, diagonal_pairs(slabs, blocks, 1))
     while 1 << step < slabs:
         [send] = call(
             functools.partial(join_shares, step), [(1 << step,) + face], share, *gathered
@@ -632,6 +665,14 @@
     ]
     flux_shape = (variables - 1, cells + 2 * HP + 2, long_rows, lanes)
     flux_scratch = [pltpu.VMEM(flux_shape, F32)] * 3
+    ghost, beyond = call(
+        functools.partial(join_ghosts, rows, slabs),
+        [(variables, 2, rows, lanes), (2 * variables * HP, lanes)],
+        share,
+        edge_2,
+        *gathered,
+    )
+    beyond = lax.ppermute(beyond, both, end_pairs(slabs, blocks))
     state, source, mid_1 = call(
         functools.partial(place_edges, *sizes),
         [state_shape, source_shape, mid_shapes[0]],
@@ -640,22 +681,21 @@
         edge_1,
         edge_2,
         band,
+        ghost,
         scratch=flux_scratch,
         aliases={0: 0, 1: 1},
         limit=12,
     )
-    state, source, out, corner_2 = call(
+    state, source, out = call(
         functools.partial(place_halos, *sizes[:3]),
-        [state_shape, source_shape, (corner_layout(variables, cells)[1], lanes), side_shape],
+        [state_shape, source_shape, (corner_layout(variables, cells)[1], lanes)],
         state,
         source,
         first,
         second,
-        share,
-        *gathered,
+        ghost,
         aliases={0: 0, 1: 1},
     )
-    corner_2 = lax.ppermute(corner_2, "blk", swap_pairs(blocks, 1))
     got = lax.ppermute(out, "blk", swap_pairs(blocks, 0))
     half_faces = (slabs // 2,) + face
     state, source, mid_1, mid_2, new, held, send = call(
@@ -668,10 +708,11 @@
         got,
         corner_1,
         corner_2,
+        beyond,
         band,
         mid_1,
         scratch=flux_scratch,
-        aliases={0: 0, 1: 1, 6: 2},
+        aliases={0: 0, 1: 1, 7: 2},
         limit=12,
     )
     step = slabs.bit_length() - 2

time: 42.9 us -> 44.6 us (1.040)
  starting transfers between devices: 23.7 us -> 24.7 us
  waiting for transfers between devices: 8.89 us -> 9.58 us
    ppermute x1, starting transfers between devices: 0.07 us -> 1.08 us  [shards(): edge_1 = lax.ppermute(edge_1, 'blk', swap_pairs(blocks, 0))]
    ppermute x1, starting transfers between devices: 3.43 us -> 2.5 us  [shards(): edge_2 = lax.ppermute(edge_2, 'blk', swap_pairs(blocks, 1))]
    ppermute x1, waiting for transfers between devices: 1.82 us -> 2.58 us  [shards(): gathered.append(lax.ppermute(send, 'pitch', flip_pairs(slabs, 1 << step)))]
    ppermute x2 -> x3, starting transfers between devices: 7.75 us -> 8.4 us  [the longest x1 4.71 us: shards(): corner_1 = lax.ppermute(corner_1, both, diagonal_pairs(slabs, blocks, 0))]
    ppermute x2 -> x3, waiting for transfers between devices: 2.65 us -> 2.95 us  [the longest x1 2.94 us: shards(): beyond = lax.ppermute(beyond, both, end_pairs(slabs, blocks))]
    pallas_call x12 -> x13, Pallas kernels: 9.28 us -> 9.25 us  [call(): pl.pallas_call(body, out_shape=outs, in_specs=in_specs or [VMEM] * len(ar...]
  transfers between devices with their start and end apart: 11 -> 12, of which waited for: 4 -> 4; matrix products, arithmetic and copies ran while one was open for 0% -> 0% of each run, Pallas kernels for 11% -> 11%
where the time goes in v5:
time: 44.6 us; the launch traced here: 44.3 us
  starting transfers between devices  24.7 us (55%)
  waiting for transfers between devices  9.58 us (21%)
  Pallas kernels  9.25 us (21%)
  between operations  0.82 us (2%)
    pallas_call x13, Pallas kernels, call(): pl.pallas_call(body, out_shape=outs, in_specs=in_specs or [VMEM] * len(ar...  9.25 us
    ppermute x1, starting transfers between devices, shards(): corner_1 = lax.ppermute(corner_1, both, diagonal_pairs(slabs, blocks, 0))  4.71 us
    ppermute x1, starting transfers between devices, shards(): gathered, step = ([lax.ppermute(send, 'pitch', flip_pairs(slabs, 1))], 1)  4.37 us
    ppermute x1, starting transfers between devices, shards(): spread.append(lax.ppermute(send, 'pitch', pairs))  3.33 us
    ppermute x1, starting transfers between devices, shards(): beyond = lax.ppermute(beyond, both, end_pairs(slabs, blocks))  3.03 us
    ppermute x1, waiting for transfers between devices, shards(): beyond = lax.ppermute(beyond, both, end_pairs(slabs, blocks))  2.94 us
    ppermute x1, waiting for transfers between devices, shards(): gathered.append(lax.ppermute(send, 'pitch', flip_pairs(slabs, 1 << step)))  2.58 us
    ppermute x1, starting transfers between devices, shards(): edge_2 = lax.ppermute(edge_2, 'blk', swap_pairs(blocks, 1))  2.5 us
  transfers between devices with their start and end apart: 12, of which 4 were waited for; matrix products, arithmetic and copies ran while one was open for 0% of the time, Pallas kernels for 11%

profile of v5, /device:TPU:4, one launch (start us, length us, event | category | flops | bytes accessed | tf_op | source)
XLA Modules:
  0.0 44.3 jit_solution(9766042869393840510)
XLA Ops:
  0.6 1.8 %shard_map.76 = (f32[2,49,5,8,128]{4,3,2,1,0:T(8,128)S(1)}, s32[2,4,128]{2,1,0:T(4,128)S(1)}, s32[4,128]{1,0:T(4,128)S(1)}, f32[5,20,32,128]{3,2,1,0:T(8,128)S(1...) custom-call(f32[2,49,5,8,128]{4,3,2,1,0:T(8,128)} %bitcast.3, ...), custom_call_target="tpu_custom_call" | custom-call | bytes 6709248 | tf_op jit(solution)/shard_map/pallas_call | solution.py:38
  2.4 0.1 shard_map.77
  2.5 1.6 %collective-permute-start.4 = (f32[5,10,16,128]{3,2,1,0:T(8,128)S(1)}, f32[5,10,16,128]{3,2,1,0:T(8,128)S(1)}, u32[]{:S(2)}, u32[]{:S(2)}) collective-permute-start(f32[5,10,16,128]{3,2,1,0:T(8,128)S(1)} %get-tuple-element.57), channel_id=1, source_target_pairs={{0,1},{2,3},{1,0},{3,2},{4,5},{6,7},{5,4},{7,6},{8,9},{10,11},{9,8... | collective-permute-start | bytes 1228808 | tf_op jit(solution)/shard_map/ppermute | solution.py:631
  4.2 0.7 %collective-permute-start.5 = (f32[5,10,16,128]{3,2,1,0:T(8,128)S(1)}, f32[5,10,16,128]{3,2,1,0:T(8,128)S(1)}, u32[]{:S(2)}, u32[]{:S(2)}) collective-permute-start(f32[5,10,16,128]{3,2,1,0:T(8,128)S(1)} %get-tuple-element.58), channel_id=1, source_target_pairs={{1,2},{2,1},{5,6},{6,5},{9,10},{10,9},{13,14},{14,13},{17,18},{18,... | collective-permute-start | bytes 1228808 | tf_op jit(solution)/shard_map/ppermute | solution.py:632
  4.8 0.1 shard_map.78
  5.0 2.5 %collective-permute-start.1 = (f32[400,128]{1,0:T(8,128)S(1)}, f32[400,128]{1,0:T(8,128)S(1)}, u32[]{:S(2)}, u32[]{:S(2)}) collective-permute-start(f32[400,128]{1,0:T(8,128)S(1)} %get-tuple-element.47), channel_id=1, source_target_pairs={{4,8},{12,16},{20,24},{8,4},{16,12},{24,20},{5,9},{13,17},{21,25},... | collective-permute-start | bytes 614408 | tf_op jit(solution)/shard_map/ppermute | solution.py:641
  7.5 1.1 %collective-permute-start = (f32[400,128]{1,0:T(8,128)S(1)}, f32[400,128]{1,0:T(8,128)S(1)}, u32[]{:S(2)}, u32[]{:S(2)}) collective-permute-start(f32[400,128]{1,0:T(8,128)S(1)} %get-tuple-element.46), channel_id=1, source_target_pairs={{0,4},{8,12},{16,20},{24,28},{4,0},{12,8},{20,16},{28,24},{1,5},{9... | collective-permute-start | bytes 614408 | tf_op jit(solution)/shard_map/ppermute | solution.py:642
  8.6 4.4 %collective-permute-start.2 = (f32[1,5,8,128]{3,2,1,0:T(8,128)S(1)}, f32[1,5,8,128]{3,2,1,0:T(8,128)S(1)}, u32[]{:S(2)}, u32[]{:S(2)}) collective-permute-start(f32[1,5,8,128]{3,2,1,0:T(8,128)S(1)} %get-tuple-element.53), channel_id=1, source_target_pairs={{0,1},{1,0},{2,3},{3,2},{4,5},{5,4},{6,7},{7,6},{8,9},{9,8},{10,11... | collective-permute-start | bytes 61448 | tf_op jit(solution)/shard_map/ppermute | solution.py:627
  12.9 1.8 %collective-permute-done.2.refs_0_ = f32[1,5,8,128]{3,2,1,0:T(8,128)S(1)} collective-permute-done((f32[1,5,8,128]{3,2,1,0:T(8,128)S(1)}, f32[1,5,8,128]{3,2,1,0:T(8,128)S(1)}, u32[]{:S(2)}, u32[]{:S(2)}) %collective-permute-start.2) | collective-permute-done | bytes 20512 | tf_op jit(solution)/shard_map/ppermute | solution.py:627
  14.7 2.1 %collective-permute-start.3 = (f32[2,5,8,128]{3,2,1,0:T(8,128)S(1)}, f32[2,5,8,128]{3,2,1,0:T(8,128)S(1)}, u32[]{:S(2)}, u32[]{:S(2)}) collective-permute-start(f32[2,5,8,128]{3,2,1,0:T(8,128)S(1)} %shard_map.80), channel_id=1, source_target_pairs={{0,2},{1,3},{2,0},{3,1},{4,6},{5,7},{6,4},{7,5},{8,10},{9,11},{10,... | collective-permute-start | bytes 122888 | tf_op jit(solution)/shard_map/ppermute | solution.py:650
  16.8 0.3 shard_map.79
  17.2 2.6 %collective-permute-done.3.refs_1_ = f32[2,5,8,128]{3,2,1,0:T(8,128)S(1)} collective-permute-done((f32[2,5,8,128]{3,2,1,0:T(8,128)S(1)}, f32[2,5,8,128]{3,2,1,0:T(8,128)S(1)}, u32[]{:S(2)}, u32[]{:S(2)}) %collective-permute-start.3) | collective-permute-done | bytes 40992 | tf_op jit(solution)/shard_map/ppermute | solution.py:650
  19.8 0.0 collective-permute-done.1.after_ref.refs_3_
  19.8 0.0 collective-permute-done.refs_2_
  19.8 0.7 %shard_map.82 = (f32[5,20,32,128]{3,2,1,0:T(8,128)S(1)}, f32[5,16,32,128]{3,2,1,0:T(8,128)S(1)}, f32[5,16,32,128]{3,2,1,0:T(8,128)S(1)}) custom-call(f32[5,20,32,128]{3,2,1,0:T(8,128)S(1)} %get-tuple-element.43.state_ref.refs_0_, f32[5,16,32,128]{3,2,1,0:T(8,128)S(1)} %get-tuple-element.45.source_ref.refs_1_, ...), custom_call_target="tpu_custom_call", output_to_operand_aliasing={{0}: (0, {}), {1}: (1, {})} | custom-call | bytes 7831552 | tf_op jit(solution)/shard_map/pallas_call | solution.py:38
  20.5 0.0 collective-permute-done.4.refs_2_
  20.5 0.0 collective-permute-done.5.refs_3_
  20.5 0.1 shard_map.83
  20.7 0.1 collective-permute-start.6
  20.7 4.7 %collective-permute-start.7 = (f32[112,128]{1,0:T(8,128)S(1)}, f32[112,128]{1,0:T(8,128)S(1)}, u32[]{:S(2)}, u32[]{:S(2)}) collective-permute-start(f32[112,128]{1,0:T(8,128)S(1)} %get-tuple-element.62), channel_id=1, source_target_pairs={{4,9},{6,11},{5,8},{7,10},{12,17},{14,19},{13,16},{15,18},{20,25},... | collective-permute-start | bytes 172040 | tf_op jit(solution)/shard_map/ppermute | solution.py:644
  25.5 0.7 %collective-permute-start.8 = (f32[112,128]{1,0:T(8,128)S(1)}, f32[112,128]{1,0:T(8,128)S(1)}, u32[]{:S(2)}, u32[]{:S(2)}) collective-permute-start(f32[112,128]{1,0:T(8,128)S(1)} %get-tuple-element.63), channel_id=1, source_target_pairs={{5,10},{6,9},{13,18},{14,17},{21,26},{22,25},{9,6},{10,5},{17,14},... | collective-permute-start | bytes 172040 | tf_op jit(solution)/shard_map/ppermute | solution.py:645
  26.1 3.0 %collective-permute-start.9 = (f32[40,128]{1,0:T(8,128)S(1)}, f32[40,128]{1,0:T(8,128)S(1)}, u32[]{:S(2)}, u32[]{:S(2)}) collective-permute-start(f32[40,128]{1,0:T(8,128)S(1)} %get-tuple-element.64), channel_id=1, source_target_pairs={{4,8},{7,11},{12,16},{15,19},{20,24},{23,27},{8,4},{11,7},{16,12},... | collective-permute-start | bytes 61448 | tf_op jit(solution)/shard_map/ppermute | solution.py:675
  29.2 0.0 collective-permute-done.7.refs_3_
  29.2 0.0 collective-permute-done.8.refs_4_
  29.2 2.9 %collective-permute-done.9.refs_5_ = f32[40,128]{1,0:T(8,128)S(1)} collective-permute-done((f32[40,128]{1,0:T(8,128)S(1)}, f32[40,128]{1,0:T(8,128)S(1)}, u32[]{:S(2)}, u32[]{:S(2)}) %collective-permute-start.9) | collective-permute-done | bytes 20512 | tf_op jit(solution)/shard_map/ppermute | solution.py:675
  32.1 0.0 collective-permute-done.6.refs_2_
  32.1 1.4 %shard_map.84 = (f32[5,20,32,128]{3,2,1,0:T(8,128)S(1)}, f32[5,16,32,128]{3,2,1,0:T(8,128)S(1)}, f32[5,16,32,128]{3,2,1,0:T(8,128)S(1)}, f32[5,12,32,128]{3,2,1,...) custom-call(f32[5,20,32,128]{3,2,1,0:T(8,128)S(1)} %get-tuple-elemen, ...), custom_call_target="tpu_custom_call", output_to_operand_aliasing={{0}: (0, {}), {1}: (1, {}), {2}: (7, {})} | custom-call | bytes 10289152 | tf_op jit(solution)/shard_map/pallas_call | solution.py:38
  33.5 3.3 %collective-permute-start.10 = (f32[2,5,8,128]{3,2,1,0:T(8,128)S(1)}, f32[2,5,8,128]{3,2,1,0:T(8,128)S(1)}, u32[]{:S(2)}, u32[]{:S(2)}) collective-permute-start(f32[2,5,8,128]{3,2,1,0:T(8,128)S(1)} %get-tuple-element.74), channel_id=1, source_target_pairs={{0,2},{3,1},{4,6},{7,5},{8,10},{11,9},{12,14},{15,13},{16,18},{19,... | collective-permute-start | bytes 122888 | tf_op jit(solution)/shard_map/ppermute | solution.py:723
  36.9 2.5 %shard_map.85 = (f32[5,16,32,128]{3,2,1,0:T(8,128)S(1)}, f32[5,12,32,128]{3,2,1,0:T(8,128)S(1)}, f32[5,8,16,128]{3,2,1,0:T(8,128)S(1)}) custom-call(f32[5,20,32,128]{3,2,1,0:T(8,128)S(1)} %get-tuple-element.66.refs_0_, f32[5,16,32,128]{3,2,1,0:T(8,128)S(1)} %get-tuple-element.67.refs_1_, ...), custom_call_target="tpu_custom_call", output_to_operand_aliasing={{0}: (3, {}), {1}: (4, {}), {2}: (5, {})} | custom-call | bytes 8323072 | tf_op jit(solution)/shard_map/pallas_call | solution.py:38
  39.4 0.0 collective-permute-done.10.got_ref
  39.4 0.5 %collective-permute-start.11 = (f32[1,5,8,128]{3,2,1,0:T(8,128)S(1)}, f32[1,5,8,128]{3,2,1,0:T(8,128)S(1)}, u32[]{:S(2)}, u32[]{:S(2)}) collective-permute-start(f32[1,5,8,128]{3,2,1,0:T(8,128)S(1)} %get-tuple-element.80), channel_id=1, source_target_pairs={{0,1},{1,0},{2,3},{3,2},{4,5},{5,4},{6,7},{7,6},{8,9},{9,8},{10,11... | collective-permute-start | bytes 61448 | tf_op jit(solution)/shard_map/ppermute | solution.py:747
  39.9 1.1 %shard_map.87 = (f32[5,8,16,128]{3,2,1,0:T(8,128)}, f32[2,49,5,8,128]{4,3,2,1,0:T(8,128)}) custom-call(f32[5,8,16,128]{3,2,1,0:T(8,128)S(1)} %get-tuple-element.71.after_ref.new_ref, f32[2,49,5,8,128]{4,3,2,1,0:T(8,128)S(1)} %get-tuple-element.48.store_ref.refs_1_, f32[2,48,8,128]{3,2,1,0:T(8,128)S(1)} %get-tuple-element.72.table_ref.refs_2_, ...), custom_call_target="tpu_custom_call" | custom-call | bytes 5083136 | tf_op jit(solution)/shard_map/pallas_call | solution.py:38
  41.0 2.3 %collective-permute-done.11.refs_6_ = f32[1,5,8,128]{3,2,1,0:T(8,128)S(1)} collective-permute-done((f32[1,5,8,128]{3,2,1,0:T(8,128)S(1)}, f32[1,5,8,128]{3,2,1,0:T(8,128)S(1)}, u32[]{:S(2)}, u32[]{:S(2)}) %collective-permute-start.11) | collective-permute-done | bytes 20512 | tf_op jit(solution)/shard_map/ppermute | solution.py:747
  43.3 1.0 %shard_map.88 = (f32[2,49,5,8,128]{4,3,2,1,0:T(8,128)}, f32[2,5,8,128]{3,2,1,0:T(8,128)}) custom-call(f32[2,49,5,8,128]{4,3,2,1,0:T(8,128)} %get-tuple-element.77.refs_0_, f32[2,49,5,8,128]{4,3,2,1,0:T(8,128)S(1)} %get-tuple-element.48.store_ref.refs_1_, f32[2,48,8,128]{3,2,1,0:T(8,128)S(1)} %get-tuple-element.72.table_ref.refs_2_, ...), custom_call_target="tpu_custom_call", output_to_operand_aliasing={{0}: (0, {})} | custom-call | bytes 6541312 | tf_op jit(solution)/shard_map/pallas_call | solution.py:38
  (3 shorter events, 0.1 us)
Async XLA Ops:
  2.5 18.0 %collective-permute-start.4 = (f32[5,10,16,128]{3,2,1,0:T(8,128)S(1)}, f32[5,10,16,128]{3,2,1,0:T(8,128)S(1)}, u32[]{:S(2)}, u32[]{:S(2)}) collective-permute-start(f32[5,10,16,128]{3,2,1,0:T(8,128)S(1)} %get-tuple-element.57), channel_id=1, source_target_pairs={{0,1},{2,3},{1,0},{3,2},{4,5},{6,7},{5,4},{7,6},{8,9},{10,11},{9,8... | collective-permute-start | bytes 1228808 | tf_op jit(solution)/shard_map/ppermute | solution.py:631
  4.2 16.3 %collective-permute-start.5 = (f32[5,10,16,128]{3,2,1,0:T(8,128)S(1)}, f32[5,10,16,128]{3,2,1,0:T(8,128)S(1)}, u32[]{:S(2)}, u32[]{:S(2)}) collective-permute-start(f32[5,10,16,128]{3,2,1,0:T(8,128)S(1)} %get-tuple-element.58), channel_id=1, source_target_pairs={{1,2},{2,1},{5,6},{6,5},{9,10},{10,9},{13,14},{14,13},{17,18},{18,... | collective-permute-start | bytes 1228808 | tf_op jit(solution)/shard_map/ppermute | solution.py:632
  5.0 14.8 %collective-permute-start.1 = (f32[400,128]{1,0:T(8,128)S(1)}, f32[400,128]{1,0:T(8,128)S(1)}, u32[]{:S(2)}, u32[]{:S(2)}) collective-permute-start(f32[400,128]{1,0:T(8,128)S(1)} %get-tuple-element.47), channel_id=1, source_target_pairs={{4,8},{12,16},{20,24},{8,4},{16,12},{24,20},{5,9},{13,17},{21,25},... | collective-permute-start | bytes 614408 | tf_op jit(solution)/shard_map/ppermute | solution.py:641
  7.5 12.3 %collective-permute-start = (f32[400,128]{1,0:T(8,128)S(1)}, f32[400,128]{1,0:T(8,128)S(1)}, u32[]{:S(2)}, u32[]{:S(2)}) collective-permute-start(f32[400,128]{1,0:T(8,128)S(1)} %get-tuple-element.46), channel_id=1, source_target_pairs={{0,4},{8,12},{16,20},{24,28},{4,0},{12,8},{20,16},{28,24},{1,5},{9... | collective-permute-start | bytes 614408 | tf_op jit(solution)/shard_map/ppermute | solution.py:642
  8.6 6.1 %collective-permute-start.2 = (f32[1,5,8,128]{3,2,1,0:T(8,128)S(1)}, f32[1,5,8,128]{3,2,1,0:T(8,128)S(1)}, u32[]{:S(2)}, u32[]{:S(2)}) collective-permute-start(f32[1,5,8,128]{3,2,1,0:T(8,128)S(1)} %get-tuple-element.53), channel_id=1, source_target_pairs={{0,1},{1,0},{2,3},{3,2},{4,5},{5,4},{6,7},{7,6},{8,9},{9,8},{10,11... | collective-permute-start | bytes 61448 | tf_op jit(solution)/shard_map/ppermute | solution.py:627
  14.7 5.1 %collective-permute-start.3 = (f32[2,5,8,128]{3,2,1,0:T(8,128)S(1)}, f32[2,5,8,128]{3,2,1,0:T(8,128)S(1)}, u32[]{:S(2)}, u32[]{:S(2)}) collective-permute-start(f32[2,5,8,128]{3,2,1,0:T(8,128)S(1)} %shard_map.80), channel_id=1, source_target_pairs={{0,2},{1,3},{2,0},{3,1},{4,6},{5,7},{6,4},{7,5},{8,10},{9,11},{10,... | collective-permute-start | bytes 122888 | tf_op jit(solution)/shard_map/ppermute | solution.py:650
  20.7 11.5 %collective-permute-start.6 = (f32[216,128]{1,0:T(8,128)S(1)}, f32[216,128]{1,0:T(8,128)S(1)}, u32[]{:S(2)}, u32[]{:S(2)}) collective-permute-start(f32[216,128]{1,0:T(8,128)S(1)} %get-tuple-element.61), channel_id=1, source_target_pairs={{0,4},{8,12},{16,20},{24,28},{4,0},{12,8},{20,16},{28,24},{1,5},{9... | collective-permute-start | bytes 331784 | tf_op jit(solution)/shard_map/ppermute | solution.py:699
  20.7 8.4 %collective-permute-start.7 = (f32[112,128]{1,0:T(8,128)S(1)}, f32[112,128]{1,0:T(8,128)S(1)}, u32[]{:S(2)}, u32[]{:S(2)}) collective-permute-start(f32[112,128]{1,0:T(8,128)S(1)} %get-tuple-element.62), channel_id=1, source_target_pairs={{4,9},{6,11},{5,8},{7,10},{12,17},{14,19},{13,16},{15,18},{20,25},... | collective-permute-start | bytes 172040 | tf_op jit(solution)/shard_map/ppermute | solution.py:644
  25.5 3.7 %collective-permute-start.8 = (f32[112,128]{1,0:T(8,128)S(1)}, f32[112,128]{1,0:T(8,128)S(1)}, u32[]{:S(2)}, u32[]{:S(2)}) collective-permute-start(f32[112,128]{1,0:T(8,128)S(1)} %get-tuple-element.63), channel_id=1, source_target_pairs={{5,10},{6,9},{13,18},{14,17},{21,26},{22,25},{9,6},{10,5},{17,14},... | collective-permute-start | bytes 172040 | tf_op jit(solution)/shard_map/ppermute | solution.py:645
  26.1 6.0 %collective-permute-start.9 = (f32[40,128]{1,0:T(8,128)S(1)}, f32[40,128]{1,0:T(8,128)S(1)}, u32[]{:S(2)}, u32[]{:S(2)}) collective-permute-start(f32[40,128]{1,0:T(8,128)S(1)} %get-tuple-element.64), channel_id=1, source_target_pairs={{4,8},{7,11},{12,16},{15,19},{20,24},{23,27},{8,4},{11,7},{16,12},... | collective-permute-start | bytes 61448 | tf_op jit(solution)/shard_map/ppermute | solution.py:675
  33.5 5.9 %collective-permute-start.10 = (f32[2,5,8,128]{3,2,1,0:T(8,128)S(1)}, f32[2,5,8,128]{3,2,1,0:T(8,128)S(1)}, u32[]{:S(2)}, u32[]{:S(2)}) collective-permute-start(f32[2,5,8,128]{3,2,1,0:T(8,128)S(1)} %get-tuple-element.74), channel_id=1, source_target_pairs={{0,2},{3,1},{4,6},{7,5},{8,10},{11,9},{12,14},{15,13},{16,18},{19,... | collective-permute-start | bytes 122888 | tf_op jit(solution)/shard_map/ppermute | solution.py:723
  39.4 3.8 %collective-permute-start.11 = (f32[1,5,8,128]{3,2,1,0:T(8,128)S(1)}, f32[1,5,8,128]{3,2,1,0:T(8,128)S(1)}, u32[]{:S(2)}, u32[]{:S(2)}) collective-permute-start(f32[1,5,8,128]{3,2,1,0:T(8,128)S(1)} %get-tuple-element.80), channel_id=1, source_target_pairs={{0,1},{1,0},{2,3},{3,2},{4,5},{5,4},{6,7},{7,6},{8,9},{9,8},{10,11... | collective-permute-start | bytes 61448 | tf_op jit(solution)/shard_map/ppermute | solution.py:747

commit v6 on v5

--- a/solution.py
+++ b/solution.py
@@ -106,7 +106,8 @@
 
 def rebuild_shares(*refs):
     store_hbm, times_hbm, active_hbm, flow_hbm, prior_hbm = refs[:5]
-    store_ref, times_ref, active_ref, state_ref, prior_ref, share_ref, send_ref, sems = refs[5:]
+    store_ref, times_ref, active_ref, state_ref, prior_ref, share_ref, send_ref = refs[5:12]
+    band_ref, sems = refs[12:]
     cells, rows = flow_hbm.shape[1:3]
     copies = [
         pltpu.make_async_copy(from_ref, to_ref, sems.at[i])
@@ -123,6 +124,7 @@
     ]
     for copy in copies:
         copy.start()
+    band_ref[...] = radial_band(band_ref.shape[1]).astype(band_ref.dtype)
     copies[0].wait()
     copies[1].wait()
     harm_count = (store_ref.shape[1] - 1) // 2
@@ -181,8 +183,8 @@
     return jnp.where(fluxes, entries([(1, 1.0), (-1, -1.0)]), state)
 
 
-def prepare_close(store_ref, times_ref, active_ref, table_ref, base_ref, gain_ref, band_ref):
-    band_ref[...] = radial_band(band_ref.shape[1]).astype(band_ref.dtype)
+def prepare_close(store_ref, times_ref, active_ref, after_ref, table_ref, base_ref, gain_ref):
+    del after_ref
     harm_count = (store_ref.shape[1] - 1) // 2
     signals = store_ref.shape[2]
     active = doubled(active_ref[...])
@@ -367,8 +369,13 @@
         variables, lanes = self.variables, self.lanes
         pitch_ref, axial_ref, radial_ref = self.flux_refs
 
+        flux_count = -(-(self.rows + 2 * out_width + 2) // 8) * 8
+        flux_rows = slice(row_at - 1, row_at - 1 + flux_count)
+        if flux_rows.stop > from_ref.shape[2]:
+            flux_rows = slice(0, from_ref.shape[2])
+
         def fluxes(plane):
-            u = [from_ref[v, plane + width] for v in range(variables)]
+            u = [from_ref[v, plane + width, flux_rows] for v in range(variables)]
             inverse = 1.0 / u[0]
             speed = [u[d] * inverse for d in (1, 2, 3)]
             pressure = gamma_less * (
@@ -380,8 +387,8 @@
                 w = 0.5 * speed[d]
                 for v in (1, 2, 3):
                     flux = u[v] * w
-                    flux_ref[v - 1, plane + HP + 1] = flux + half if v == d + 1 else flux
-                flux_ref[3, plane + HP + 1] = total * w
+                    flux_ref[v - 1, plane + HP + 1, flux_rows] = flux + half if v == d + 1 else flux
+                flux_ref[3, plane + HP + 1, flux_rows] = total * w
 
         def update(plane):
             at = slice(row_at, row_at + count)
@@ -616,11 +623,11 @@
 
     inputs = (store, sample_times, harmonics, flow_state, prior_state)
     shapes = [store.shape, sample_times.shape, harmonics.shape, state_shape, flow_state.shape]
-    store, times, active, state, prior, share, send = call(
+    store, times, active, state, prior, share, send, band = call(
         rebuild_shares,
-        shapes + [(2,) + face, (1,) + face],
+        shapes + [(2,) + face, (1,) + face, (2 * lanes, lanes)],
         *[pltpu.with_memory_space_constraint(a, pltpu.MemorySpace.HBM) for a in inputs],
-        types=(F32, jnp.int32, jnp.int32, F32, F32, F32, F32),
+        types=(F32, jnp.int32, jnp.int32, F32, F32, F32, F32, jnp.bfloat16),
         scratch=[pltpu.SemaphoreType.DMA((len(inputs) + 1,))],
         in_specs=[HBM] * len(inputs),
     )
@@ -649,15 +656,6 @@
         )
         gathered.append(lax.ppermute(send, "pitch", flip_pairs(slabs, 1 << step)))
         step += 1
-    table, base, gain, band = call(
-        prepare_close,
-        [(2, orders - 1, 2 * part, lanes), (2,) + face, (2 * part, lanes), (2 * lanes, lanes)],
-        store,
-        times,
-        active,
-        types=[F32, F32, F32, jnp.bfloat16],
-    )
-
     sizes = (cells, rows, slabs, blocks)
     mid_shapes = [
         (variables, cells + 2 * HP, long_rows, lanes),
@@ -734,6 +732,15 @@
         aliases={3: 0, 4: 1, 5: 2},
         limit=12,
     )
+    table, base, gain = call(
+        prepare_close,
+        [(2, orders - 1, 2 * part, lanes), (2,) + face, (2 * part, lanes)],
+        store,
+        times,
+        active,
+        new,
+    )
+
     while step > 0:
         half_faces = (held.shape[0] // 2,) + face
         held, send = call(
@@ -745,7 +752,7 @@
             pairs = low + [(slabs - 1 - i, slabs - 1 - j) for i, j in low]
             spread.append(lax.ppermute(send, "pitch", pairs))
     second_sample = lax.ppermute(send, "pitch", flip_pairs(slabs, 1))
-    parts = 4
+    parts = 2
     pieces = [orders * i // parts for i in range(parts + 1)]
     half_store = pltpu.VMEM(store.shape[1:], F32)
     new_state, new_store = call(

time: 44.6 us -> 44.5 us (level)
  no operation moved by 1% of the time
where the time goes in v6:
time: 44.5 us; the launch traced here: 44.2 us
  starting transfers between devices  24.8 us (56%)
  waiting for transfers between devices  9.55 us (21%)
  Pallas kernels  9.06 us (20%)
  between operations  0.82 us (2%)
    pallas_call x13, Pallas kernels, call(): pl.pallas_call(body, out_shape=outs, in_specs=in_specs or [VMEM] * len(ar...  9.06 us
    ppermute x1, starting transfers between devices, shards(): corner_1 = lax.ppermute(corner_1, both, diagonal_pairs(slabs, blocks, 0))  4.71 us
    ppermute x1, starting transfers between devices, shards(): gathered, step = ([lax.ppermute(send, 'pitch', flip_pairs(slabs, 1))], 1)  4.37 us
    ppermute x1, starting transfers between devices, shards(): spread.append(lax.ppermute(send, 'pitch', pairs))  3.38 us
    ppermute x1, starting transfers between devices, shards(): beyond = lax.ppermute(beyond, both, end_pairs(slabs, blocks))  3.03 us
    ppermute x1, waiting for transfers between devices, shards(): beyond = lax.ppermute(beyond, both, end_pairs(slabs, blocks))  2.94 us
    ppermute x1, waiting for transfers between devices, shards(): gathered.append(lax.ppermute(send, 'pitch', flip_pairs(slabs, 1 << step)))  2.92 us
    ppermute x1, starting transfers between devices, shards(): edge_2 = lax.ppermute(edge_2, 'blk', swap_pairs(blocks, 1))  2.5 us
  transfers between devices with their start and end apart: 12, of which 4 were waited for; matrix products, arithmetic and copies ran while one was open for 0% of the time, Pallas kernels for 11%

profile of v6, /device:TPU:4, one launch (start us, length us, event | category | flops | bytes accessed | tf_op | source)
XLA Modules:
  0.0 44.2 jit_solution(13201080814894967975)
XLA Ops:
  0.6 1.8 %shard_map.76 = (f32[2,49,5,8,128]{4,3,2,1,0:T(8,128)S(1)}, s32[2,4,128]{2,1,0:T(4,128)S(1)}, s32[4,128]{1,0:T(4,128)S(1)}, f32[5,20,32,128]{3,2,1,0:T(8,128)S(1...) custom-call(f32[2,49,5,8,128]{4,3,2,1,0:T(8,128)} %bitcast.3, ...), custom_call_target="tpu_custom_call" | custom-call | bytes 6840320 | tf_op jit(solution)/shard_map/pallas_call | solution.py:38
  2.4 0.1 shard_map.77
  2.5 1.6 %collective-permute-start.4 = (f32[5,10,16,128]{3,2,1,0:T(8,128)S(1)}, f32[5,10,16,128]{3,2,1,0:T(8,128)S(1)}, u32[]{:S(2)}, u32[]{:S(2)}) collective-permute-start(f32[5,10,16,128]{3,2,1,0:T(8,128)S(1)} %get-tuple-element.54), channel_id=1, source_target_pairs={{0,1},{2,3},{1,0},{3,2},{4,5},{6,7},{5,4},{7,6},{8,9},{10,11},{9,8... | collective-permute-start | bytes 1228808 | tf_op jit(solution)/shard_map/ppermute | solution.py:638
  4.2 0.7 %collective-permute-start.5 = (f32[5,10,16,128]{3,2,1,0:T(8,128)S(1)}, f32[5,10,16,128]{3,2,1,0:T(8,128)S(1)}, u32[]{:S(2)}, u32[]{:S(2)}) collective-permute-start(f32[5,10,16,128]{3,2,1,0:T(8,128)S(1)} %get-tuple-element.55), channel_id=1, source_target_pairs={{1,2},{2,1},{5,6},{6,5},{9,10},{10,9},{13,14},{14,13},{17,18},{18,... | collective-permute-start | bytes 1228808 | tf_op jit(solution)/shard_map/ppermute | solution.py:639
  4.8 0.1 shard_map.78
  5.0 2.5 %collective-permute-start.1 = (f32[400,128]{1,0:T(8,128)S(1)}, f32[400,128]{1,0:T(8,128)S(1)}, u32[]{:S(2)}, u32[]{:S(2)}) collective-permute-start(f32[400,128]{1,0:T(8,128)S(1)} %get-tuple-element.47), channel_id=1, source_target_pairs={{4,8},{12,16},{20,24},{8,4},{16,12},{24,20},{5,9},{13,17},{21,25},... | collective-permute-start | bytes 614408 | tf_op jit(solution)/shard_map/ppermute | solution.py:648
  7.5 1.1 %collective-permute-start = (f32[400,128]{1,0:T(8,128)S(1)}, f32[400,128]{1,0:T(8,128)S(1)}, u32[]{:S(2)}, u32[]{:S(2)}) collective-permute-start(f32[400,128]{1,0:T(8,128)S(1)} %get-tuple-element.46), channel_id=1, source_target_pairs={{0,4},{8,12},{16,20},{24,28},{4,0},{12,8},{20,16},{28,24},{1,5},{9... | collective-permute-start | bytes 614408 | tf_op jit(solution)/shard_map/ppermute | solution.py:649
  8.6 4.4 %collective-permute-start.2 = (f32[1,5,8,128]{3,2,1,0:T(8,128)S(1)}, f32[1,5,8,128]{3,2,1,0:T(8,128)S(1)}, u32[]{:S(2)}, u32[]{:S(2)}) collective-permute-start(f32[1,5,8,128]{3,2,1,0:T(8,128)S(1)} %get-tuple-element.50), channel_id=1, source_target_pairs={{0,1},{1,0},{2,3},{3,2},{4,5},{5,4},{6,7},{7,6},{8,9},{9,8},{10,11... | collective-permute-start | bytes 61448 | tf_op jit(solution)/shard_map/ppermute | solution.py:634
  12.9 1.8 %collective-permute-done.2.refs_0_ = f32[1,5,8,128]{3,2,1,0:T(8,128)S(1)} collective-permute-done((f32[1,5,8,128]{3,2,1,0:T(8,128)S(1)}, f32[1,5,8,128]{3,2,1,0:T(8,128)S(1)}, u32[]{:S(2)}, u32[]{:S(2)}) %collective-permute-start.2) | collective-permute-done | bytes 20512 | tf_op jit(solution)/shard_map/ppermute | solution.py:634
  14.7 2.1 %collective-permute-start.3 = (f32[2,5,8,128]{3,2,1,0:T(8,128)S(1)}, f32[2,5,8,128]{3,2,1,0:T(8,128)S(1)}, u32[]{:S(2)}, u32[]{:S(2)}) collective-permute-start(f32[2,5,8,128]{3,2,1,0:T(8,128)S(1)} %shard_map.79), channel_id=1, source_target_pairs={{0,2},{1,3},{2,0},{3,1},{4,6},{5,7},{6,4},{7,5},{8,10},{9,11},{10,... | collective-permute-start | bytes 122888 | tf_op jit(solution)/shard_map/ppermute | solution.py:657
  16.8 2.9 %collective-permute-done.3.refs_1_ = f32[2,5,8,128]{3,2,1,0:T(8,128)S(1)} collective-permute-done((f32[2,5,8,128]{3,2,1,0:T(8,128)S(1)}, f32[2,5,8,128]{3,2,1,0:T(8,128)S(1)}, u32[]{:S(2)}, u32[]{:S(2)}) %collective-permute-start.3) | collective-permute-done | bytes 40992 | tf_op jit(solution)/shard_map/ppermute | solution.py:657
  19.8 0.0 collective-permute-done.1.after_ref.refs_3_
  19.8 0.0 collective-permute-done.refs_2_
  19.8 0.7 %shard_map.81 = (f32[5,20,32,128]{3,2,1,0:T(8,128)S(1)}, f32[5,16,32,128]{3,2,1,0:T(8,128)S(1)}, f32[5,16,32,128]{3,2,1,0:T(8,128)S(1)}) custom-call(f32[5,20,32,128]{3,2,1,0:T(8,128)S(1)} %get-tuple-element.43.state_ref.refs_0_, f32[5,16,32,128]{3,2,1,0:T(8,128)S(1)} %get-tuple-element.45.source_ref.refs_1_, ...), custom_call_target="tpu_custom_call", output_to_operand_aliasing={{0}: (0, {}), {1}: (1, {})} | custom-call | bytes 7831552 | tf_op jit(solution)/shard_map/pallas_call | solution.py:38
  20.5 0.0 collective-permute-done.4.refs_2_
  20.5 0.0 collective-permute-done.5.refs_3_
  20.5 0.1 shard_map.82
  20.7 0.1 collective-permute-start.6
  20.7 4.7 %collective-permute-start.7 = (f32[112,128]{1,0:T(8,128)S(1)}, f32[112,128]{1,0:T(8,128)S(1)}, u32[]{:S(2)}, u32[]{:S(2)}) collective-permute-start(f32[112,128]{1,0:T(8,128)S(1)} %get-tuple-element.59), channel_id=1, source_target_pairs={{4,9},{6,11},{5,8},{7,10},{12,17},{14,19},{13,16},{15,18},{20,25},... | collective-permute-start | bytes 172040 | tf_op jit(solution)/shard_map/ppermute | solution.py:651
  25.5 0.7 %collective-permute-start.8 = (f32[112,128]{1,0:T(8,128)S(1)}, f32[112,128]{1,0:T(8,128)S(1)}, u32[]{:S(2)}, u32[]{:S(2)}) collective-permute-start(f32[112,128]{1,0:T(8,128)S(1)} %get-tuple-element.60), channel_id=1, source_target_pairs={{5,10},{6,9},{13,18},{14,17},{21,26},{22,25},{9,6},{10,5},{17,14},... | collective-permute-start | bytes 172040 | tf_op jit(solution)/shard_map/ppermute | solution.py:652
  26.1 3.0 %collective-permute-start.9 = (f32[40,128]{1,0:T(8,128)S(1)}, f32[40,128]{1,0:T(8,128)S(1)}, u32[]{:S(2)}, u32[]{:S(2)}) collective-permute-start(f32[40,128]{1,0:T(8,128)S(1)} %get-tuple-element.61), channel_id=1, source_target_pairs={{4,8},{7,11},{12,16},{15,19},{20,24},{23,27},{8,4},{11,7},{16,12},... | collective-permute-start | bytes 61448 | tf_op jit(solution)/shard_map/ppermute | solution.py:673
  29.2 0.0 collective-permute-done.7.refs_3_
  29.2 0.0 collective-permute-done.8.refs_4_
  29.2 2.9 %collective-permute-done.9.refs_5_ = f32[40,128]{1,0:T(8,128)S(1)} collective-permute-done((f32[40,128]{1,0:T(8,128)S(1)}, f32[40,128]{1,0:T(8,128)S(1)}, u32[]{:S(2)}, u32[]{:S(2)}) %collective-permute-start.9) | collective-permute-done | bytes 20512 | tf_op jit(solution)/shard_map/ppermute | solution.py:673
  32.1 0.0 collective-permute-done.6.refs_2_
  32.1 1.3 %shard_map.83 = (f32[5,20,32,128]{3,2,1,0:T(8,128)S(1)}, f32[5,16,32,128]{3,2,1,0:T(8,128)S(1)}, f32[5,16,32,128]{3,2,1,0:T(8,128)S(1)}, f32[5,12,32,128]{3,2,1,...) custom-call(f32[5,20,32,128]{3,2,1,0:T(8,128)S(1)} %get-tuple-elemen, ...), custom_call_target="tpu_custom_call", output_to_operand_aliasing={{0}: (0, {}), {1}: (1, {}), {2}: (7, {})} | custom-call | bytes 10289152 | tf_op jit(solution)/shard_map/pallas_call | solution.py:38
  33.5 3.4 %collective-permute-start.10 = (f32[2,5,8,128]{3,2,1,0:T(8,128)S(1)}, f32[2,5,8,128]{3,2,1,0:T(8,128)S(1)}, u32[]{:S(2)}, u32[]{:S(2)}) collective-permute-start(f32[2,5,8,128]{3,2,1,0:T(8,128)S(1)} %get-tuple-element.74), channel_id=1, source_target_pairs={{0,2},{3,1},{4,6},{7,5},{8,10},{11,9},{12,14},{15,13},{16,18},{19,... | collective-permute-start | bytes 122888 | tf_op jit(solution)/shard_map/ppermute | solution.py:721
  36.9 2.4 %shard_map.84 = (f32[5,16,32,128]{3,2,1,0:T(8,128)S(1)}, f32[5,12,32,128]{3,2,1,0:T(8,128)S(1)}, f32[5,8,16,128]{3,2,1,0:T(8,128)S(1)}) custom-call(f32[5,20,32,128]{3,2,1,0:T(8,128)S(1)} %get-tuple-element.63.refs_0_, f32[5,16,32,128]{3,2,1,0:T(8,128)S(1)} %get-tuple-element.64.refs_1_, ...), custom_call_target="tpu_custom_call", output_to_operand_aliasing={{0}: (3, {}), {1}: (4, {}), {2}: (5, {})} | custom-call | bytes 8323072 | tf_op jit(solution)/shard_map/pallas_call | solution.py:38
  39.3 0.0 collective-permute-done.10.got_ref
  39.4 0.5 %collective-permute-start.11 = (f32[1,5,8,128]{3,2,1,0:T(8,128)S(1)}, f32[1,5,8,128]{3,2,1,0:T(8,128)S(1)}, u32[]{:S(2)}, u32[]{:S(2)}) collective-permute-start(f32[1,5,8,128]{3,2,1,0:T(8,128)S(1)} %get-tuple-element.80), channel_id=1, source_target_pairs={{0,1},{1,0},{2,3},{3,2},{4,5},{5,4},{6,7},{7,6},{8,9},{9,8},{10,11... | collective-permute-start | bytes 61448 | tf_op jit(solution)/shard_map/ppermute | solution.py:754
  39.9 0.3 shard_map.85
  40.2 1.1 %shard_map.87 = (f32[5,8,16,128]{3,2,1,0:T(8,128)}, f32[2,49,5,8,128]{4,3,2,1,0:T(8,128)}) custom-call(f32[5,8,16,128]{3,2,1,0:T(8,128)S(1)} %get-tuple-element.68.after_ref.new_ref, f32[2,49,5,8,128]{4,3,2,1,0:T(8,128)S(1)} %get-tuple-element.69.store_ref.refs_1_, f32[2,48,8,128]{3,2,1,0:T(8,128)S(1)} %get-tuple-element.72.table_ref.refs_2_, ...), custom_call_target="tpu_custom_call" | custom-call | bytes 5083136 | tf_op jit(solution)/shard_map/pallas_call | solution.py:38
  41.3 1.9 %collective-permute-done.11.refs_6_ = f32[1,5,8,128]{3,2,1,0:T(8,128)S(1)} collective-permute-done((f32[1,5,8,128]{3,2,1,0:T(8,128)S(1)}, f32[1,5,8,128]{3,2,1,0:T(8,128)S(1)}, u32[]{:S(2)}, u32[]{:S(2)}) %collective-permute-start.11) | collective-permute-done | bytes 20512 | tf_op jit(solution)/shard_map/ppermute | solution.py:754
  43.2 1.0 %shard_map.88 = (f32[2,49,5,8,128]{4,3,2,1,0:T(8,128)}, f32[2,5,8,128]{3,2,1,0:T(8,128)}) custom-call(f32[2,49,5,8,128]{4,3,2,1,0:T(8,128)} %get-tuple-element.77.refs_0_, f32[2,49,5,8,128]{4,3,2,1,0:T(8,128)S(1)} %get-tuple-element.69.store_ref.refs_1_, f32[2,48,8,128]{3,2,1,0:T(8,128)S(1)} %get-tuple-element.72.table_ref.refs_2_, ...), custom_call_target="tpu_custom_call", output_to_operand_aliasing={{0}: (0, {})} | custom-call | bytes 6541312 | tf_op jit(solution)/shard_map/pallas_call | solution.py:38
  (3 shorter events, 0.1 us)
Async XLA Ops:
  2.5 18.0 %collective-permute-start.4 = (f32[5,10,16,128]{3,2,1,0:T(8,128)S(1)}, f32[5,10,16,128]{3,2,1,0:T(8,128)S(1)}, u32[]{:S(2)}, u32[]{:S(2)}) collective-permute-start(f32[5,10,16,128]{3,2,1,0:T(8,128)S(1)} %get-tuple-element.54), channel_id=1, source_target_pairs={{0,1},{2,3},{1,0},{3,2},{4,5},{6,7},{5,4},{7,6},{8,9},{10,11},{9,8... | collective-permute-start | bytes 1228808 | tf_op jit(solution)/shard_map/ppermute | solution.py:638
  4.2 16.3 %collective-permute-start.5 = (f32[5,10,16,128]{3,2,1,0:T(8,128)S(1)}, f32[5,10,16,128]{3,2,1,0:T(8,128)S(1)}, u32[]{:S(2)}, u32[]{:S(2)}) collective-permute-start(f32[5,10,16,128]{3,2,1,0:T(8,128)S(1)} %get-tuple-element.55), channel_id=1, source_target_pairs={{1,2},{2,1},{5,6},{6,5},{9,10},{10,9},{13,14},{14,13},{17,18},{18,... | collective-permute-start | bytes 1228808 | tf_op jit(solution)/shard_map/ppermute | solution.py:639
  5.0 14.8 %collective-permute-start.1 = (f32[400,128]{1,0:T(8,128)S(1)}, f32[400,128]{1,0:T(8,128)S(1)}, u32[]{:S(2)}, u32[]{:S(2)}) collective-permute-start(f32[400,128]{1,0:T(8,128)S(1)} %get-tuple-element.47), channel_id=1, source_target_pairs={{4,8},{12,16},{20,24},{8,4},{16,12},{24,20},{5,9},{13,17},{21,25},... | collective-permute-start | bytes 614408 | tf_op jit(solution)/shard_map/ppermute | solution.py:648
  7.5 12.3 %collective-permute-start = (f32[400,128]{1,0:T(8,128)S(1)}, f32[400,128]{1,0:T(8,128)S(1)}, u32[]{:S(2)}, u32[]{:S(2)}) collective-permute-start(f32[400,128]{1,0:T(8,128)S(1)} %get-tuple-element.46), channel_id=1, source_target_pairs={{0,4},{8,12},{16,20},{24,28},{4,0},{12,8},{20,16},{28,24},{1,5},{9... | collective-permute-start | bytes 614408 | tf_op jit(solution)/shard_map/ppermute | solution.py:649
  8.6 6.1 %collective-permute-start.2 = (f32[1,5,8,128]{3,2,1,0:T(8,128)S(1)}, f32[1,5,8,128]{3,2,1,0:T(8,128)S(1)}, u32[]{:S(2)}, u32[]{:S(2)}) collective-permute-start(f32[1,5,8,128]{3,2,1,0:T(8,128)S(1)} %get-tuple-element.50), channel_id=1, source_target_pairs={{0,1},{1,0},{2,3},{3,2},{4,5},{5,4},{6,7},{7,6},{8,9},{9,8},{10,11... | collective-permute-start | bytes 61448 | tf_op jit(solution)/shard_map/ppermute | solution.py:634
  14.7 5.1 %collective-permute-start.3 = (f32[2,5,8,128]{3,2,1,0:T(8,128)S(1)}, f32[2,5,8,128]{3,2,1,0:T(8,128)S(1)}, u32[]{:S(2)}, u32[]{:S(2)}) collective-permute-start(f32[2,5,8,128]{3,2,1,0:T(8,128)S(1)} %shard_map.79), channel_id=1, source_target_pairs={{0,2},{1,3},{2,0},{3,1},{4,6},{5,7},{6,4},{7,5},{8,10},{9,11},{10,... | collective-permute-start | bytes 122888 | tf_op jit(solution)/shard_map/ppermute | solution.py:657
  20.7 11.5 %collective-permute-start.6 = (f32[216,128]{1,0:T(8,128)S(1)}, f32[216,128]{1,0:T(8,128)S(1)}, u32[]{:S(2)}, u32[]{:S(2)}) collective-permute-start(f32[216,128]{1,0:T(8,128)S(1)} %get-tuple-element.58), channel_id=1, source_target_pairs={{0,4},{8,12},{16,20},{24,28},{4,0},{12,8},{20,16},{28,24},{1,5},{9... | collective-permute-start | bytes 331784 | tf_op jit(solution)/shard_map/ppermute | solution.py:697
  20.7 8.4 %collective-permute-start.7 = (f32[112,128]{1,0:T(8,128)S(1)}, f32[112,128]{1,0:T(8,128)S(1)}, u32[]{:S(2)}, u32[]{:S(2)}) collective-permute-start(f32[112,128]{1,0:T(8,128)S(1)} %get-tuple-element.59), channel_id=1, source_target_pairs={{4,9},{6,11},{5,8},{7,10},{12,17},{14,19},{13,16},{15,18},{20,25},... | collective-permute-start | bytes 172040 | tf_op jit(solution)/shard_map/ppermute | solution.py:651
  25.5 3.7 %collective-permute-start.8 = (f32[112,128]{1,0:T(8,128)S(1)}, f32[112,128]{1,0:T(8,128)S(1)}, u32[]{:S(2)}, u32[]{:S(2)}) collective-permute-start(f32[112,128]{1,0:T(8,128)S(1)} %get-tuple-element.60), channel_id=1, source_target_pairs={{5,10},{6,9},{13,18},{14,17},{21,26},{22,25},{9,6},{10,5},{17,14},... | collective-permute-start | bytes 172040 | tf_op jit(solution)/shard_map/ppermute | solution.py:652
  26.1 6.0 %collective-permute-start.9 = (f32[40,128]{1,0:T(8,128)S(1)}, f32[40,128]{1,0:T(8,128)S(1)}, u32[]{:S(2)}, u32[]{:S(2)}) collective-permute-start(f32[40,128]{1,0:T(8,128)S(1)} %get-tuple-element.61), channel_id=1, source_target_pairs={{4,8},{7,11},{12,16},{15,19},{20,24},{23,27},{8,4},{11,7},{16,12},... | collective-permute-start | bytes 61448 | tf_op jit(solution)/shard_map/ppermute | solution.py:673
  33.5 5.8 %collective-permute-start.10 = (f32[2,5,8,128]{3,2,1,0:T(8,128)S(1)}, f32[2,5,8,128]{3,2,1,0:T(8,128)S(1)}, u32[]{:S(2)}, u32[]{:S(2)}) collective-permute-start(f32[2,5,8,128]{3,2,1,0:T(8,128)S(1)} %get-tuple-element.74), channel_id=1, source_target_pairs={{0,2},{3,1},{4,6},{7,5},{8,10},{11,9},{12,14},{15,13},{16,18},{19,... | collective-permute-start | bytes 122888 | tf_op jit(solution)/shard_map/ppermute | solution.py:721
  39.4 3.8 %collective-permute-start.11 = (f32[1,5,8,128]{3,2,1,0:T(8,128)S(1)}, f32[1,5,8,128]{3,2,1,0:T(8,128)S(1)}, u32[]{:S(2)}, u32[]{:S(2)}) collective-permute-start(f32[1,5,8,128]{3,2,1,0:T(8,128)S(1)} %get-tuple-element.80), channel_id=1, source_target_pairs={{0,1},{1,0},{2,3},{3,2},{4,5},{5,4},{6,7},{7,6},{8,9},{9,8},{10,11... | collective-permute-start | bytes 61448 | tf_op jit(solution)/shard_map/ppermute | solution.py:754
